TPU v7x, 128 devices: a whole 4x4x4 slice. The times are simulated.
128 devices in a mesh: dp: 32 (over y, x, core), vocab: 4 (over z).
Axes of the slice: x: 4, y: 4, z: 4, core: 2. Of those that a mesh axis runs over, the one named last changes fastest.
Arguments:
- resid: bfloat16 [2, 4096, 4096], P(None, 'dp'), may hold values from -6 to 6
- norm_gain: float32 [4096], replicated, may hold values from 0.5 to 1.5
- in_x: bfloat16 [4096, 4096], P('dp', 'vocab'), may hold values from -0.09375 to 0.09375
- in_z: bfloat16 [4096, 4096], P('dp', 'vocab'), may hold values from -0.09375 to 0.09375
- conv_w: float32 [4, 4096], P(None, 'vocab'), may hold values from -3 to 3
- conv_b: float32 [4096], P('vocab'), may hold values from -3 to 3
- xdt_w: bfloat16 [4096, 256], P('vocab'), may hold values from -0.09375 to 0.09375
- xbc_w: bfloat16 [4096, 32], P('vocab'), may hold values from -0.09375 to 0.09375
- dt_gain: float32 [256], replicated, may hold values from 0.5 to 1.5
- dt_proj: bfloat16 [256, 4096], P(None, 'vocab'), may hold values from -0.375 to 0.375
- dt_bias: float32 [4096], P('vocab'), may hold values from -4 to 1
- a_rate: float32 [4096, 16], P('vocab'), may hold values from 0.0001 to 1
- out_w: bfloat16 [4096, 4096], P('vocab'), may hold values from -0.09375 to 0.09375
- final_gain: float32 [4096], replicated, may hold values from 0.5 to 1.5
- head_w: bfloat16 [8192, 4096], P('vocab', 'dp'), as said below
- targets: int32 [2, 4096], P(None, 'dp'), may hold values from 0 to 8191
- lengths: int32 [2], replicated, may hold values from 1024 to 4096
Outputs:
- hidden_out: bfloat16 [2, 4096, 4096], P(None, 'dp', 'vocab')
- token_logp: float32 [2, 4096], P(None, 'dp')
- mean_logp: float32 [], replicated
Inputs may be any that keep to these rules, and one draw needn't show every extreme that they name: `head_w`: entries lie within 720 / sqrt(4096) of zero.
All inputs are finite; a program needn't handle non-finite values.
Results may differ from a plain program's by a relative error of at most 0.019.
Values may be sent and summed in bfloat16 or wider, within the bound.
No kernel may reach another device: no remote copies, remote signals or barrier semaphores. Data moves between devices by JAX's collectives and lax.ppermute only.
A program may use at most 128 MiB of HBM per device.

v0:
```python
import math

import jax
import jax.numpy as jnp
from jax import lax
from jax.sharding import Mesh
from jax.sharding import PartitionSpec as P

DP = ("dp_0", "dp_1", "dp_2")


def in_one_piece(arrays, axis, dim, along):
    ends, at = ([], 0)
    for a in arrays[:-1]:
        at += a.shape[along]
        ends.append(at)
    both = jnp.concatenate(arrays, axis=along)
    return tuple(jnp.split(lax.all_gather(both, axis, axis=dim, tiled=True), ends, axis=along))


def shifted(array, axis, by):
    peers = lax.axis_size(axis)
    pairs = [(i, i + by) for i in range(peers) if 0 <= i + by < peers]
    return lax.ppermute(array, axis, pairs)


def sent_to_all(array, axis):
    peers = lax.axis_size(axis)
    return lax.all_to_all(
        jnp.broadcast_to(array[None], (peers, *array.shape)), axis, 0, 0, tiled=True
    )


def over_copies(array, axis):
    everything = sent_to_all(array, axis)
    return jnp.sum(everything.astype(jnp.float32), axis=0)


def neutral_like(array, identity):
    return jax.tree.map(
        lambda a, e: jnp.broadcast_to(jnp.asarray(e, a.dtype), a.shape), array, identity
    )


def entering(array, axes, combine, identity):
    before = start = neutral_like(array, identity)
    so_far = array
    for axis in reversed(axes):
        peers, index = (lax.axis_size(axis), lax.axis_index(axis))
        pieces = jax.tree.map(lambda part: lax.all_gather(part, axis), so_far)
        inside, so_far = (start, start)
        for k in range(peers):
            passed = k < index
            so_far = combine(so_far, jax.tree.map(lambda part: part[k], pieces))
            inside = jax.tree.map(lambda new, old: jnp.where(passed, new, old), so_far, inside)
        before = combine(inside, before)
    return before


def cut_along(array, dim, peers):
    before, after = (array.shape[:dim], array.shape[dim + 1 :])
    return jnp.moveaxis(array.reshape(*before, peers, -1, *after), dim, 0)


def sent_and_summed(array, axis, dim):
    peers = lax.axis_size(axis)
    tiles = lax.all_to_all(cut_along(array, dim, peers), axis, 0, 0, tiled=True)
    return jnp.sum(tiles.astype(jnp.float32), axis=0)


def taken_together(array, axis):
    everything = sent_to_all(array, axis)
    return jnp.sum(everything, axis=0)


def in_order(tiles, dim):
    tiles = jnp.moveaxis(tiles, 0, dim)
    lengths = tiles.shape
    return tiles.reshape(*lengths[:dim], lengths[dim] * lengths[dim + 1], *lengths[dim + 2 :])


def collect(array, axis, dim):
    return in_order(sent_to_all(array, axis), dim)


def collected_together(array, axis):
    leaves = jax.tree.leaves(array)
    turns = sorted(range(len(leaves)), key=lambda k: -leaves[k].size)
    width = (1, *leaves[turns[0]].shape)[-1]
    lines = [
        jnp.pad(leaves[k].reshape(-1), (0, -leaves[k].size % width)).reshape(-1, width)
        for k in turns
    ]
    both, at, found = (sent_to_all(jnp.concatenate(lines), axis), 0, {})
    for k, line in zip(turns, lines):
        section = both[:, at : at + len(line)].reshape(len(both), -1)
        found[k] = section[:, : leaves[k].size].reshape(-1, *leaves[k].shape)
        at += len(line)
    numbers = iter(range(len(leaves)))
    return jax.tree.map(lambda _: found[next(numbers)], array)


def joined_by_halves(pieces, combine):
    while len(jax.tree.leaves(pieces)[0]) > 1:
        pieces = jax.vmap(combine)(
            *(jax.tree.map(lambda part: part[side::2], pieces) for side in (0, 1))
        )
    return jax.tree.map(lambda part: part[0], pieces)


def joined_all(array, axis, combine):
    pieces = collected_together(array, axis)
    return joined_by_halves(pieces, combine)


def rms_norm(values, gain, epsilon):
    return values * lax.rsqrt(jnp.mean(values * values, axis=-1, keepdims=True) + epsilon) * gain


def head_logits(final, head_w):
    return lax.dot_general(
        final,
        lax.all_gather(head_w, DP, axis=1, tiled=True),
        (((1,), (1,)), ((), ())),
        preferred_element_type=jnp.float32,
    )


def body(
    resid,
    norm_gain,
    in_x,
    in_z,
    conv_w,
    conv_b,
    xdt_w,
    xbc_w,
    dt_gain,
    dt_proj,
    dt_bias,
    a_rate,
    out_w,
    final_gain,
    head_w,
    targets,
    lengths,
):
    batch_count, local_len, width = resid.shape
    channels = in_x.shape[1]
    nstate = a_rate.shape[1]
    kernel_len = conv_w.shape[0]
    row_count = batch_count * local_len
    stream = resid.astype(jnp.float32)
    normed = rms_norm(stream, norm_gain, 1e-05).astype(jnp.bfloat16).reshape(row_count, width)
    pieces = in_one_piece((in_x, in_z), DP, 0, 1)
    x_acc = jnp.dot(normed, pieces[0], preferred_element_type=jnp.float32)
    z_acc = jnp.dot(normed, pieces[1], preferred_element_type=jnp.float32)
    x_inner = x_acc.astype(jnp.bfloat16).reshape(batch_count, local_len, channels)
    z_gate = z_acc.astype(jnp.bfloat16).reshape(batch_count, local_len, channels)
    before = shifted(x_inner[:, local_len - (kernel_len - 1) :, :], DP, 1)
    padded = jnp.concatenate([before, x_inner], axis=1).astype(jnp.float32)
    conv_sum = jnp.zeros((batch_count, local_len, channels), jnp.float32) + conv_b
    for tap_index in range(kernel_len):
        conv_sum = conv_sum + conv_w[tap_index] * padded[:, tap_index : tap_index + local_len, :]
    conv_act = jax.nn.silu(conv_sum)
    conv_low = conv_act.astype(jnp.bfloat16).reshape(row_count, channels)
    dt_raw, bc_raw = (
        over_copies(
            jnp.dot(conv_low, xdt_w, preferred_element_type=jnp.float32).astype(jnp.bfloat16),
            "vocab",
        ).astype(jnp.float32),
        over_copies(
            jnp.dot(conv_low, xbc_w, preferred_element_type=jnp.float32).astype(jnp.bfloat16),
            "vocab",
        ).astype(jnp.float32),
    )
    dt_normed = rms_norm(dt_raw, dt_gain, 1e-06).astype(jnp.bfloat16)
    step_size = jax.nn.softplus(
        jnp.dot(dt_normed, dt_proj, preferred_element_type=jnp.float32) + dt_bias
    ).reshape(batch_count, local_len, channels)
    in_map = bc_raw[:, :nstate].reshape(batch_count, local_len, nstate)
    out_map = bc_raw[:, nstate:].reshape(batch_count, local_len, nstate)
    block_len = math.gcd(local_len, 16)
    block_count = local_len // block_len

    def by_block(values):
        return values.transpose(1, 0, 2).reshape(
            (block_count, block_len) + (values.shape[0], values.shape[2])
        )

    def run_block(carry_state, inputs):
        step_blk, conv_blk, in_blk, out_blk = inputs
        results = []
        for position in range(block_len):
            carry_state = (
                jnp.exp(-step_blk[position][..., None] * a_rate) * carry_state
                + (step_blk[position] * conv_blk[position])[..., None]
                * in_blk[position][:, None, :]
            )
            results.append(jnp.sum(carry_state * out_blk[position][:, None, :], axis=-1))
        return (carry_state, jnp.stack(results))

    start_state = jnp.zeros((batch_count, channels, nstate), jnp.float32)
    last_state, local_out = lax.scan(
        run_block,
        start_state,
        (by_block(step_size), by_block(conv_act), by_block(in_map), by_block(out_map)),
    )
    local_out = local_out.reshape(local_len, batch_count, channels).transpose(1, 0, 2)
    step_total = jnp.sum(step_size, axis=1)
    last_decay = jnp.exp(-step_total[..., None] * a_rate)

    def chain(earlier, later):
        return (earlier[0] * later[0], later[0] * earlier[1] + later[1])

    _, state_in = entering(
        (last_decay, last_state), DP, chain, (jnp.ones_like(last_decay), jnp.zeros_like(last_state))
    )
    step_cumul = jnp.cumsum(step_size, axis=1)
    carried = jnp.sum(
        out_map[:, :, None, :] * jnp.exp(-step_cumul[..., None] * a_rate) * state_in[:, None, :, :],
        axis=-1,
    )
    mixed = local_out + carried
    gated = (
        (mixed * jax.nn.silu(z_gate.astype(jnp.float32)))
        .astype(jnp.bfloat16)
        .reshape(row_count, channels)
    )
    partial_value = jnp.dot(gated, out_w, preferred_element_type=jnp.float32)
    vocab_count = lax.axis_size("vocab")
    vocab_index = lax.axis_index("vocab")
    share_width = width // vocab_count
    flat_stream = stream.reshape(row_count, width)
    mixer_part = sent_and_summed(partial_value.astype(jnp.bfloat16), "vocab", 1)
    stream_part = lax.dynamic_slice_in_dim(flat_stream, vocab_index * share_width, share_width, 1)
    hidden_share = (stream_part + mixer_part).astype(jnp.bfloat16)
    hidden_float = hidden_share.astype(jnp.float32)
    square_sum = taken_together(jnp.sum(hidden_float * hidden_float, axis=-1), "vocab")
    inv_scale = lax.rsqrt(square_sum / width + 1e-05)
    gain_part = lax.dynamic_slice_in_dim(final_gain, vocab_index * share_width, share_width, 0)
    final_share = (hidden_float * inv_scale[:, None] * gain_part).astype(jnp.bfloat16)
    final = collect(final_share, "vocab", 1)
    logits = head_logits(final, head_w)
    vocab_rows = head_w.shape[0]
    local_ids = targets.reshape(row_count) - vocab_index * vocab_rows
    entry_ids = lax.broadcasted_iota(jnp.int32, (row_count, vocab_rows), 1)
    picked = jnp.sum(jnp.where(entry_ids == local_ids[:, None], logits, 0.0), axis=-1)
    local_top = jnp.max(logits, axis=-1)
    exp_local = jnp.sum(jnp.exp(logits - local_top[:, None]), axis=-1)

    def combine_lse(first, second):
        larger = jnp.maximum(first[0], second[0])
        return (
            larger,
            first[1] * jnp.exp(first[0] - larger) + second[1] * jnp.exp(second[0] - larger),
            first[2] + second[2],
        )

    global_top, exp_total, picked_all = joined_all(
        (local_top, exp_local, picked), "vocab", combine_lse
    )
    log_total = global_top + jnp.log(exp_total)
    token_logp = (picked_all - log_total).reshape(batch_count, local_len)
    positions = lax.axis_index(DP) * local_len + jnp.arange(local_len, dtype=jnp.int32)
    valid_mask = positions[None, :] < lengths[:, None]
    masked_sum = jnp.sum(jnp.where(valid_mask, token_logp, 0.0))
    grand_sum = taken_together(masked_sum, DP)
    mean_logp = grand_sum / jnp.sum(lengths.astype(jnp.float32))
    return (hidden_share.reshape(batch_count, local_len, share_width), token_logp, mean_logp)


def solution(mesh):
    split = Mesh(
        mesh.devices.reshape(4, 4, 2, mesh.shape["vocab"]), ("dp_0", "dp_1", "dp_2", "vocab")
    )
    return jax.shard_map(
        body,
        mesh=split,
        in_specs=(
            P(None, DP, None),
            P(),
            P(DP, "vocab"),
            P(DP, "vocab"),
            P(None, "vocab"),
            P("vocab"),
            P("vocab", None),
            P("vocab", None),
            P(),
            P(None, "vocab"),
            P("vocab"),
            P("vocab", None),
            P("vocab", None),
            P(),
            P("vocab", DP),
            P(None, DP),
            P(),
        ),
        out_specs=(P(None, DP, "vocab"), P(None, DP), P()),
        check_vma=False,
    )
```

profile of v0, /device:TPU:1, one launch (start us, length us, event | category | flops | bytes accessed | tf_op | source)
XLA Modules:
  0.0 361.4 jit_solution(10704425099392257988)
XLA Ops:
  7.2 2.0 pad_maximum_fusion
  10.6 1.9 multiply_convert_fusion
  12.5 74.4 %all-gather.4.cloned.1.call-done = bf16[4096,2048]{1,0:T(8,128)(2,1)} async-done(((bf16[128,2048]{1,0:T(8,128)(2,1)}), bf16[4096,2048]{1,0:T(8,128)(2,1)}) %all-gather.4.cloned.1.call-update) | async-done | bytes 16777232 | tf_op jit(solution)/shard_map/all_gather | solution.py:18
  86.9 6.4 %fusion.53 = bf16[256,1024]{1,0:T(8,128)(2,1)S(1)} fusion(bf16[256,4096]{1,0:T(8,128)(2,1)} %bitcast.394, bf16[4096,2048]{1,0:T(8,128)(2,1)} %all-gather.4.cloned.1.call-done), kind=kOutput, calls=%fused_computation.213 | convolution fusion | flops 2147745792 | bytes 11010048 | tf_op jit(solution)/shard_map/dot_general | solution.py:156
  93.3 3.2 collective-permute-start
  97.6 1.7 fusion.94
  100.1 4.1 %all-to-all-start.1 = ((bf16[4,256,32]{1,2,0:T(8,128)(2,1)}), bf16[4,256,32]{1,2,0:T(8,128)(2,1)S(1)}, u32[]{:S(2)}, u32[]{:S(2)}) async-start(bf16[4,256,32]{1,2,0:T(8,128)(2,1)} %broadcast_in_dim.27), calls=%async_computation.1 | async-start | bytes 131072 | tf_op jit(solution)/shard_map/all_to_all | solution.py:29
  104.3 1.3 convolution_convert_fusion.1
  105.6 3.6 all-to-all-done.1
  110.0 3.5 all-to-all-start
  113.5 7.1 %fusion.56 = bf16[256,1024]{1,0:T(8,128)(2,1)} fusion(bf16[256,4096]{1,0:T(8,128)(2,1)} %bitcast.395, bf16[4096,2048]{1,0:T(8,128)(2,1)} %all-gather.4.cloned.1.call-done), kind=kOutput, calls=%fused_computation.214 | convolution fusion | flops 2147745792 | bytes 11010048 | tf_op jit(solution)/shard_map/dot_general | solution.py:157
  123.8 3.0 all_gather.33
  126.9 1.8 copy.62
  128.7 2.8 reduce_window_sum.11
  131.4 2.3 neg.205
  133.8 55.0 %while.13 = (s32[]{:T(128)}, f32[2,1024,16]{1,2,0:T(8,128)S(1)}, f32[8,16,2,1024]{3,1,0,2:T(8,128)}, f32[8,16,2,1024]{3,2,1,0:T(2,128)}, f32[1024,16]{0,1:T(8,12...) while((s32[]{:T(128)}, f32[2,1024,16]{1,2,0:T(8,128)S(1)}, ...), condition=%wide.region_21.22_spmd.clone, body=%wide.region_4.21_spmd.clone.sunk | while | flops 4816914 | bytes 3422316 | solution.py:204
  134.5 1.7 constant_dynamic-slice_fusion.65
  141.3 1.9 constant_dynamic-slice_fusion.65
  148.2 1.7 constant_dynamic-slice_fusion.65
  155.0 1.7 constant_dynamic-slice_fusion.65
  161.7 2.0 constant_dynamic-slice_fusion.65
  168.7 1.9 constant_dynamic-slice_fusion.65
  175.7 2.0 constant_dynamic-slice_fusion.65
  182.6 1.9 constant_dynamic-slice_fusion.65
  188.8 2.1 all-gather
  190.9 11.7 %all_gather.34 = f32[4,2,1024,16]{2,3,1,0:T(8,128)S(1)} all-gather(f32[1,2,1024,16]{2,3,1,0:T(8,128)S(1)} %get-tuple-element.251), channel_id=1, replica_groups=mesh['dp_0'=4,'dp_1'=4,'dp_2'=2,'vocab'=4] {'dp_1'}, dimensions={0}, use_global_device_ids=true | all-gather | bytes 655360 | tf_op jit(solution)/shard_map/all_gather | solution.py:50
  202.7 10.1 %all_gather.38 = f32[4,2,1024,16]{2,3,1,0:T(8,128)S(1)} all-gather(f32[1,2,1024,16]{2,3,1,0:T(8,128)S(1)} %get-tuple-element.252), channel_id=1, replica_groups=mesh['dp_0'=4,'dp_1'=4,'dp_2'=2,'vocab'=4] {'dp_1'}, dimensions={0}, use_global_device_ids=true | all-gather | bytes 655360 | tf_op jit(solution)/shard_map/all_gather | solution.py:50
  212.8 11.9 %all_gather.39 = f32[4,2,1024,16]{2,3,1,0:T(8,128)S(1)} all-gather(f32[1,2,1024,16]{2,3,1,0:T(8,128)S(1)} %get-tuple-element.250), channel_id=1, replica_groups=mesh['dp_0'=4,'dp_1'=4,'dp_2'=2,'vocab'=4] {'dp_0'}, dimensions={0}, use_global_device_ids=true | all-gather | bytes 655360 | tf_op jit(solution)/shard_map/all_gather | solution.py:50
  224.7 10.4 %all_gather.35 = f32[4,2,1024,16]{2,3,1,0:T(8,128)S(1)} all-gather(f32[1,2,1024,16]{2,3,1,0:T(8,128)S(1)} %get-tuple-element.249), channel_id=1, replica_groups=mesh['dp_0'=4,'dp_1'=4,'dp_2'=2,'vocab'=4] {'dp_0'}, dimensions={0}, use_global_device_ids=true | all-gather | bytes 655360 | tf_op jit(solution)/shard_map/all_gather | solution.py:50
  235.4 5.2 %multiply_reduce_fusion.16 = f32[2,128,1024]{2,1,0:T(8,128)S(1)} fusion(f32[2,1024,16]{1,2,0:T(8,128)S(1)} %fusion.74, f32[1024,16]{0,1:T(8,128)S(1)} %get-tuple-element.594, f32[2,128,1024]{2,1,0:T(8,128)S(1)} %copy-done.7, f32[2,128,16]{2,1,0:T(8,128)S(1)} %copy-done.9), kind=kLoop, calls=%fused_computation.194 | loop fusion | flops 16515072 | bytes 2310144 | tf_op jit(solution)/shard_map/reduce_sum | solution.py:220
  241.0 5.7 %convolution_convert_fusion = bf16[256,4096]{1,0:T(8,128)(2,1)S(1)} fusion(bf16[256,1024]{1,0:T(8,128)(2,1)S(1)} %bitcast.402, bf16[1024,4096]{1,0:T(8,128)(2,1)} %param.31), kind=kOutput, calls=%fused_computation.199 | convolution fusion | flops 2148532224 | bytes 11010048 | tf_op jit(solution)/shard_map/dot_general | solution.py:230
  246.7 1.6 copy.175
  248.3 6.0 %all-to-all-start.2 = ((bf16[4,256,1024]{2,1,0:T(8,128)(2,1)}), bf16[4,256,1024]{2,1,0:T(8,128)(2,1)}, u32[]{:S(2)}, u32[]{:S(2)}) async-start(bf16[4,256,1024]{2,1,0:T(8,128)(2,1)} %bitcast.386), calls=%async_computation.2 | async-start | bytes 4194304 | tf_op jit(solution)/shard_map/all_to_all | solution.py:67
  254.3 2.4 convert.16
  256.7 14.1 %all-to-all-done.2 = bf16[4,256,1024]{2,1,0:T(8,128)(2,1)} async-done(((bf16[4,256,1024]{2,1,0:T(8,128)(2,1)}), bf16[4,256,1024]{2,1,0:T(8,128)(2,1)}, u32[]{:S(2)}, u32[]{:S(2)}) %all-to-all-start.2) | async-done | bytes 2097184 | tf_op jit(solution)/shard_map/all_to_all | solution.py:67
  270.8 2.1 convert_reduce_fusion
  272.9 1.4 fusion.59
  275.0 3.2 all-to-all-start.3
  278.2 4.1 %all-to-all-done.3 = f32[4,1,256]{2,1,0:T(1,128)S(1)} async-done(((f32[4,1,256]{2,1,0:T(1,128)}), f32[4,1,256]{2,1,0:T(1,128)S(1)}, u32[]{:S(2)}, u32[]{:S(2)}) %all-to-all-start.3) | async-done | bytes 4128 | tf_op jit(solution)/shard_map/all_to_all | solution.py:29
  282.8 1.5 broadcast_in_dim.30
  284.3 3.7 %all-to-all-start.4 = ((bf16[4,256,1024]{1,2,0:T(8,128)(2,1)}), bf16[4,256,1024]{1,2,0:T(8,128)(2,1)S(1)}, u32[]{:S(2)}, u32[]{:S(2)}) async-start(bf16[4,256,1024]{1,2,0:T(8,128)(2,1)} %broadcast_in_dim.30), calls=%async_computation.4 | async-start | bytes 4194304 | tf_op jit(solution)/shard_map/all_to_all | solution.py:29
  288.1 15.3 %all-to-all-done.4 = bf16[4,256,1024]{1,2,0:T(8,128)(2,1)S(1)} async-done(((bf16[4,256,1024]{1,2,0:T(8,128)(2,1)}), bf16[4,256,1024]{1,2,0:T(8,128)(2,1)S(1)}, u32[]{:S(2)}, u32[]{:S(2)}) %all-to-all-start.4) | async-done | bytes 2097184 | tf_op jit(solution)/shard_map/all_to_all | solution.py:29
  303.3 9.8 %fusion.98 = (f32[256]{0:T(256)S(1)}, f32[256,2048]{1,0:T(8,128)}) fusion(bf16[256,4096]{0,1:T(8,128)(2,1)S(1)} %bitcast.396, bf16[2048,4096]{1,0:T(8,128)(2,1)} %all-gather.6.cloned.1.call-done), kind=kOutput, calls=%fused_computation.316 | convolution fusion | flops 4295491584 | bytes 20972544 | tf_op jit(solution)/shard_map/dot_general | solution.py:121
  313.1 2.2 exponential_reduce_fusion
  316.0 3.2 all-to-all-start.5
  319.3 4.1 %all-to-all-done.5 = f32[4,3,256]{2,1,0:T(4,128)S(1)} async-done(((f32[4,3,256]{2,1,0:T(4,128)}), f32[4,3,256]{2,1,0:T(4,128)S(1)}, u32[]{:S(2)}, u32[]{:S(2)}) %all-to-all-start.5) | async-done | bytes 12320 | tf_op jit(solution)/shard_map/all_to_all | solution.py:29
  326.0 18.6 %all-to-all-start.6 = ((f32[32,1,1]{2,1,0:T(1,128)}), f32[32,1,1]{2,1,0:T(1,128)S(1)}, u32[]{:S(2)}, u32[]{:S(2)}) async-start(f32[32,1,1]{2,1,0:T(1,128)} %broadcast_in_dim.34), calls=%async_computation.6 | async-start | bytes 32768 | tf_op jit(solution)/shard_map/all_to_all | solution.py:29
  345.2 6.3 %all-to-all-done.6 = f32[32,1,1]{2,1,0:T(1,128)S(1)} async-done(((f32[32,1,1]{2,1,0:T(1,128)}), f32[32,1,1]{2,1,0:T(1,128)S(1)}, u32[]{:S(2)}, u32[]{:S(2)}) %all-to-all-start.6) | async-done | bytes 160 | tf_op jit(solution)/shard_map/all_to_all | solution.py:29
  (297 shorter events, 53.1 us)
Async XLA Ops:
  7.2 115.7 %copy-start = (bf16[256,1024]{1,0:T(8,128)(2,1)S(1)}, bf16[256,1024]{1,0:T(8,128)(2,1)}, u32[]{:S(2)}) copy-start(bf16[256,1024]{1,0:T(8,128)(2,1)} %param.28) | copy-start | bytes 1572868
  7.2 2.9 copy-start.3
  7.2 3.4 copy-start.11
  7.2 79.7 %all-gather.4.cloned.1.call-start = ((), (), s32[]{:S(2)}) async-start(), calls=%async_computation.7 | async-start | bytes 17301504 | tf_op jit(solution)/shard_map/all_gather | solution.py:18
  9.3 278.8 %all-gather.6.cloned.1.call-start = ((), (), s32[]{:S(2)}) async-start(), calls=%async_computation.8 | async-start | bytes 17301504 | tf_op jit(solution)/shard_map/all_gather | solution.py:123
  86.9 9.6 %copy-start.12 = (f32[4,1024]{1,0:T(4,128)S(1)}, f32[4,1024]{1,0:T(4,128)}, u32[]{:S(2)}) copy-start(f32[4,1024]{1,0:T(4,128)} %param.23) | copy-start | bytes 49156
  86.9 10.6 %copy-start.13 = (f32[1024]{0:T(1024)S(1)}, f32[1024]{0:T(1024)}, u32[]{:S(2)}) copy-start(f32[1024]{0:T(1024)} %param.24) | copy-start | bytes 12292
  93.3 4.1 %collective-permute-start = (bf16[2,3,1024]{2,1,0:T(4,128)(2,1)S(1)}, bf16[2,3,1024]{2,1,0:T(4,128)(2,1)S(1)}, u32[]{:S(2)}, u32[]{:S(2)}) collective-permute-start(bf16[2,3,1024]{2,1,0:T(4,128)(2,1)S(1)} %slice.528), channel_id=1, source_target_pairs={{0,4},{4,8},{8,12},{12,16},{16,20},{20,24},{24,28},{28,32},{32,36}... | collective-permute-start | bytes 36872 | tf_op jit(solution)/shard_map/ppermute | solution.py:24
  97.5 1.7 copy-start.10
  100.1 9.0 %all-to-all-start.1 = ((bf16[4,256,32]{1,2,0:T(8,128)(2,1)}), bf16[4,256,32]{1,2,0:T(8,128)(2,1)S(1)}, u32[]{:S(2)}, u32[]{:S(2)}) async-start(bf16[4,256,32]{1,2,0:T(8,128)(2,1)} %broadcast_in_dim.27), calls=%async_computation.1 | async-start | bytes 131072 | tf_op jit(solution)/shard_map/all_to_all | solution.py:29
  110.0 12.6 %all-to-all-start = ((bf16[4,256,256]{2,1,0:T(8,128)(2,1)}), bf16[4,256,256]{2,1,0:T(8,128)(2,1)S(1)}, u32[]{:S(2)}, u32[]{:S(2)}) async-start(bf16[4,256,256]{2,1,0:T(8,128)(2,1)} %broadcast_in_dim.26), calls=%async_computation | async-start | bytes 1048576 | tf_op jit(solution)/shard_map/all_to_all | solution.py:29
  113.5 9.4 %copy-start.15 = (f32[1024]{0:T(1024)S(1)}, f32[1024]{0:T(1024)}, u32[]{:S(2)}) copy-start(f32[1024]{0:T(1024)} %param.29) | copy-start | bytes 12292
  113.5 9.4 %copy-start.16 = (f32[256]{0:T(256)S(1)}, f32[256]{0:T(256)}, u32[]{:S(2)}) copy-start(f32[256]{0:T(256)} %param.27) | copy-start | bytes 3076
  122.4 1.4 copy-start.2
  123.8 3.1 copy-start.4
  212.8 22.6 %copy-start.7 = (f32[2,128,1024]{2,1,0:T(8,128)S(1)}, f32[2,128,1024]{2,1,0:T(8,128)}, u32[]{:S(2)}) copy-start(f32[2,128,1024]{2,1,0:T(8,128)} %neg.205) | copy-start | bytes 3145732
  212.8 22.6 %copy-start.9 = (f32[2,128,16]{2,1,0:T(8,128)S(1)}, f32[2,128,16]{2,1,0:T(8,128)}, u32[]{:S(2)}) copy-start(f32[2,128,16]{2,1,0:T(8,128)} %copy.67) | copy-start | bytes 49156
  235.4 5.2 %copy-start.6 = (f32[8,16,2,1024]{3,1,0,2:T(8,128)S(1)}, f32[8,16,2,1024]{3,1,0,2:T(8,128)}, u32[]{:S(2)}) copy-start(f32[8,16,2,1024]{3,1,0,2:T(8,128)} %get-tuple-element.46) | copy-start | bytes 3145732
  235.4 5.2 %copy-start.8 = (bf16[256,1024]{1,0:T(8,128)(2,1)S(1)}, bf16[256,1024]{1,0:T(8,128)(2,1)}, u32[]{:S(2)}) copy-start(bf16[256,1024]{1,0:T(8,128)(2,1)} %fusion.56) | copy-start | bytes 1572868
  248.3 22.5 %all-to-all-start.2 = ((bf16[4,256,1024]{2,1,0:T(8,128)(2,1)}), bf16[4,256,1024]{2,1,0:T(8,128)(2,1)}, u32[]{:S(2)}, u32[]{:S(2)}) async-start(bf16[4,256,1024]{2,1,0:T(8,128)(2,1)} %bitcast.386), calls=%async_computation.2 | async-start | bytes 4194304 | tf_op jit(solution)/shard_map/all_to_all | solution.py:67
  272.9 9.5 %dynamic-slice-start = ((f32[4096]{0:T(1024)}, s32[]{:T(128)}), f32[1024]{0:T(1024)S(1)}, s32[]{:S(2)}) async-start(f32[4096]{0:T(1024)} %param.32, s32[]{:T(128)} %select_n.170), calls=%async_computation.9 | async-start | bytes 8704 | tf_op jit(solution)/shard_map/dynamic_slice | solution.py:241
  274.3 9.9 %copy-start.5 = (bf16[256,1024]{1,0:T(8,128)(2,1)}, bf16[256,1024]{1,0:T(8,128)(2,1)S(1)}, u32[]{:S(2)}) copy-start(bf16[256,1024]{1,0:T(8,128)(2,1)S(1)} %get-tuple-element.150) | copy-start | bytes 1572868
  275.0 7.3 %all-to-all-start.3 = ((f32[4,1,256]{2,1,0:T(1,128)}), f32[4,1,256]{2,1,0:T(1,128)S(1)}, u32[]{:S(2)}, u32[]{:S(2)}) async-start(f32[4,1,256]{2,1,0:T(1,128)} %broadcast_in_dim.29), calls=%async_computation.3 | async-start | bytes 8192 | tf_op jit(solution)/shard_map/all_to_all | solution.py:29
  284.3 3.8 %copy-start.14 = (s32[2,128]{1,0:T(2,128)S(1)}, s32[2,128]{1,0:T(2,128)}, u32[]{:S(2)}) copy-start(s32[2,128]{1,0:T(2,128)} %param.34) | copy-start | bytes 3076
  284.3 19.1 %all-to-all-start.4 = ((bf16[4,256,1024]{1,2,0:T(8,128)(2,1)}), bf16[4,256,1024]{1,2,0:T(8,128)(2,1)S(1)}, u32[]{:S(2)}, u32[]{:S(2)}) async-start(bf16[4,256,1024]{1,2,0:T(8,128)(2,1)} %broadcast_in_dim.30), calls=%async_computation.4 | async-start | bytes 4194304 | tf_op jit(solution)/shard_map/all_to_all | solution.py:29
  303.3 50.1 %copy-start.1 = (bf16[256,1024]{1,0:T(8,128)(2,1)S(1)}, bf16[256,1024]{1,0:T(8,128)(2,1)}, u32[]{:S(2)}) copy-start(bf16[256,1024]{1,0:T(8,128)(2,1)} %param.28) | copy-start | bytes 1572868
  313.1 6.1 %copy-start.17 = (s32[2]{0:T(128)S(1)}, s32[2]{0:T(128)}, u32[]{:S(2)}) copy-start(s32[2]{0:T(128)} %param.35) | copy-start | bytes 28
  316.0 7.4 %all-to-all-start.5 = ((f32[4,3,256]{2,1,0:T(4,128)}), f32[4,3,256]{2,1,0:T(4,128)S(1)}, u32[]{:S(2)}, u32[]{:S(2)}) async-start(f32[4,3,256]{2,1,0:T(4,128)} %broadcast_in_dim.32), calls=%async_computation.5 | async-start | bytes 32768 | tf_op jit(solution)/shard_map/all_to_all | solution.py:29
  326.0 25.5 %all-to-all-start.6 = ((f32[32,1,1]{2,1,0:T(1,128)}), f32[32,1,1]{2,1,0:T(1,128)S(1)}, u32[]{:S(2)}, u32[]{:S(2)}) async-start(f32[32,1,1]{2,1,0:T(1,128)} %broadcast_in_dim.34), calls=%async_computation.6 | async-start | bytes 32768 | tf_op jit(solution)/shard_map/all_to_all | solution.py:29
Sparse Core Ops, SparseCore 0:
  10.9 75.9 all-gather.3
  89.1 80.4 all-gather.5
where the time goes:
time: 364 us; the launch traced here: 361 us
  waiting for transfers between devices  124 us (34%)
  other arithmetic  55.3 us (15%)
  blocking collectives  49.2 us (14%)
  starting transfers between devices  45.7 us (13%)
  local copies, waits for them, and re-layouts  38.5 us (11%)
  matrix products  31.5 us (9%)
  between operations  16.9 us (5%)
    all_gather x1, waiting for transfers between devices, in_one_piece(): lax.all_gather(both, axis, axis=dim, tiled=True)  74.4 us
    all_gather x6, blocking collectives, entering(): pieces = jax.tree.map(lambda part: lax.all_gather(part, axis), so_far)  49.2 us
    all_to_all x6, starting transfers between devices, sent_to_all(): lax.all_to_all(jnp.broadcast_to(array[None], (peers, *array.shape)), axis...  36.4 us
    all_to_all x6, waiting for transfers between devices, sent_to_all(): lax.all_to_all(jnp.broadcast_to(array[None], (peers, *array.shape)), axis...  33.7 us
    neg x16, other arithmetic, run_block(): -step_blk[position][..., None] * a_rate  14.9 us
    slice x8, local copies, waits for them, and re-layouts, run_block(): conv_blk[position]  14.7 us
    all_to_all x1, waiting for transfers between devices, sent_and_summed(): tiles = lax.all_to_all(cut_along(array, dim, peers), axis, 0, 0, tiled=True)  14.1 us
    reduce_sum x40, other arithmetic, run_block(): jnp.sum(carry_state * out_blk[position][:, None, :], axis=-1)  11.9 us
  transfers between devices with their start and end apart: 10, of which 9 were waited for; matrix products, arithmetic and copies ran while one was open for 30% of the time, Pallas kernels for 0%

commit v1 on v0

v1 whole, which is shorter than its diff:
```python
import math

import jax
import jax.numpy as jnp
from jax import lax
from jax.experimental import pallas as pl
from jax.experimental.pallas import tpu as pltpu
from jax.sharding import Mesh
from jax.sharding import PartitionSpec as P

DP = ("dp_0", "dp_1", "dp_2")
CHIPS = ("dp_0", "dp_1")
YS, XS, CS = 4, 4, 2
BF = jnp.bfloat16
F32 = jnp.float32
LOG2E = math.log2(math.e)


def place(y, x, c):
    return ((y % YS) * XS + x % XS) * CS + c


def turns(by, phase):
    pairs = []
    for y in range(YS):
        for x in range(XS):
            for c in range(CS):
                along_x = (c == 0) == (phase == 0)
                to = place(y, x + by, c) if along_x else place(y + by, x, c)
                pairs.append((place(y, x, c), to))
    return pairs


def ring(peers, by):
    return [(i, (i + by) % peers) for i in range(peers)]


def swap_cores(array):
    return lax.ppermute(array, "dp_2", ring(CS, 1))


def line_of_chips(shard):
    near = {s: lax.ppermute(shard, DP, turns(s, 0)) for s in (1, 3, 2)}
    return jnp.concatenate([shard, near[1], near[2], near[3]], axis=0)


def blocks_in_order(y, x, core):
    found = []
    for s2 in range(4):
        for s1 in range(4):
            first = lax.rem(y - s2 + YS, YS) * XS + lax.rem(x - s1 + XS, XS)
            second = lax.rem(y - s1 + YS, YS) * XS + lax.rem(x - s2 + XS, XS)
            found.append(jnp.where(core == 0, first, second) * CS + core)
    return found


def rms_norm(values, gain, epsilon):
    return values * lax.rsqrt(jnp.mean(values * values, axis=-1, keepdims=True) + epsilon) * gain


def dot(a, b):
    return jnp.dot(a, b, preferred_element_type=F32)


def norm_kernel(wide, order, resid, tail, gain, normed, mine, theirs, tail_normed):
    rows, halo = resid.shape[0], tail.shape[0]
    for r in range(0, rows, 32):
        normed[r : r + 32] = rms_norm(resid[r : r + 32].astype(F32), gain[...], 1e-05).astype(BF)
    tail_normed[...] = rms_norm(tail[...].astype(F32), gain[...], 1e-05).astype(BF)
    count = mine.shape[1] // wide
    for k in range(2 * count):
        out = (mine, theirs)[k // count]
        at = pl.ds(pl.multiple_of(order[k] * wide, wide), wide)
        to = slice((k % count) * wide, (k % count + 1) * wide)
        out[:rows, to] = normed[:, at]
        out[rows : rows + halo, to] = tail_normed[:, at]


def steps_kernel(rows, length, nstate, bc, dt, gain, proj, bias, conv, rate, step3, du3, last, total):
    raw = dt[...]
    normed = rms_norm(raw, gain[...], 1e-06).astype(BF)
    v = dot(normed, proj[...]) + bias[...]
    step = jnp.maximum(v, 0.0) + jnp.log1p(jnp.exp(-jnp.abs(v)))
    du = step * conv[...]
    for j in range(step3.shape[1]):
        step3[:, j, :] = step[:, j * 128 : (j + 1) * 128]
        du3[:, j, :] = du[:, j * 128 : (j + 1) * 128]
    batches = rows // length

    def advance(t, carry):
        state, sums = carry
        state, sums = list(state), list(sums)
        for b in range(batches):
            at = b * length + t
            s, u = step3[at], du3[at]
            sums[b] = sums[b] + s
            for n in range(nstate):
                k = b * nstate + n
                state[k] = jnp.exp2(s * rate[n]) * state[k] + u * bc[at * 2 * nstate + n]
        return tuple(state), tuple(sums)

    zero = jnp.zeros(step3.shape[1:], F32)
    state, sums = lax.fori_loop(
        0, length, advance, ((zero,) * (batches * nstate), (zero,) * batches), unroll=2
    )
    for b in range(batches):
        total[b] = sums[b]
        for n in range(nstate):
            last[b, n] = state[b * nstate + n]


def outputs_kernel(rows, length, nstate, bc, step3, du3, rate, start, z, gated, y3):
    batches = rows // length

    def advance(t, state):
        state = list(state)
        for b in range(batches):
            at = b * length + t
            s, u = step3[at], du3[at]
            y = None
            for n in range(nstate):
                k = b * nstate + n
                state[k] = jnp.exp2(s * rate[n]) * state[k] + u * bc[at * 2 * nstate + n]
                part = state[k] * bc[at * 2 * nstate + nstate + n]
                y = part if y is None else y + part
            y3[at] = y
        return tuple(state)

    state = tuple(start[b, n] for b in range(batches) for n in range(nstate))
    lax.fori_loop(0, length, advance, state, unroll=2)
    for j in range(y3.shape[1]):
        gate = z[:, j * 128 : (j + 1) * 128].astype(F32)
        gate = gate / (1.0 + jnp.exp(-gate))
        gated[:, j * 128 : (j + 1) * 128] = (y3[:, j, :] * gate).astype(BF)


def vmem():
    return pl.BlockSpec(memory_space=pltpu.VMEM)


def smem():
    return pl.BlockSpec(memory_space=pltpu.SMEM)


def body(
    resid,
    norm_gain,
    in_x,
    in_z,
    conv_w,
    conv_b,
    xdt_w,
    xbc_w,
    dt_gain,
    dt_proj,
    dt_bias,
    a_rate,
    out_w,
    final_gain,
    head_w,
    targets,
    lengths,
):
    batch_count, local_len, width = resid.shape
    k_rows, channels = in_x.shape
    nstate = a_rate.shape[1]
    taps = conv_w.shape[0]
    rank = xdt_w.shape[1]
    rows = batch_count * local_len
    y, x, core = (lax.axis_index(a) for a in DP)
    zi = lax.axis_index("vocab")
    zs = lax.axis_size("vocab")

    all_z = lax.all_gather(in_z, DP, axis=0, tiled=True)

    order = [(i, i + 1) for i in range(YS * XS * CS - 1)]
    tail = lax.ppermute(resid[:, local_len - (taps - 1) :, :], DP, order)
    line = line_of_chips(in_x)
    far = {s: lax.ppermute(line, DP, turns(s, 1)) for s in (1, 3, 2)}
    pieces = [line] + [far[s] for s in (1, 2, 3)]
    halo = 16
    tail = jnp.pad(
        tail.reshape(batch_count * (taps - 1), width),
        ((0, halo - batch_count * (taps - 1)), (0, 0)),
    )
    tail, _ = lax.optimization_barrier((tail, line))
    flat = resid.reshape(rows, width)
    half_rows = jax.ShapeDtypeStruct((rows + halo, width // CS), BF)
    normed, mine, theirs = pl.pallas_call(
        lambda *refs: norm_kernel(k_rows, *refs),
        out_shape=(jax.ShapeDtypeStruct((rows, width), BF), half_rows, half_rows),
        in_specs=[smem()] + [vmem()] * 3,
        out_specs=(vmem(),) * 3,
        scratch_shapes=[pltpu.VMEM((halo, width), BF)],
        compiler_params=pltpu.CompilerParams(vmem_limit_bytes=48 << 20),
        name="norm",
    )(
        jnp.stack(blocks_in_order(y, x, core) + blocks_in_order(y, x, 1 - core)),
        flat,
        tail,
        norm_gain.reshape(1, width),
    )
    theirs = swap_cores(theirs)
    depth = width // CS // 4
    cut = [slice(s * depth, (s + 1) * depth) for s in range(4)]
    turn = (0, 1, 3, 2)
    for_them = sum(dot(theirs[:, cut[s]], pieces[s]) for s in turn)
    from_them = swap_cores(for_them.astype(BF))
    x_acc = sum(dot(mine[:, cut[s]], pieces[s]) for s in turn) + from_them.astype(F32)
    x_all = x_acc.astype(BF)
    x_inner = x_all[:rows].reshape(batch_count, local_len, channels)
    before = x_all[rows : rows + batch_count * (taps - 1)].reshape(batch_count, taps - 1, channels)
    padded = jnp.concatenate([before, x_inner], axis=1).astype(F32)
    conv_sum = jnp.zeros((batch_count, local_len, channels), F32) + conv_b
    for k in range(taps):
        conv_sum = conv_sum + conv_w[k] * padded[:, k : k + local_len, :]
    conv_act = jax.nn.silu(conv_sum).reshape(rows, channels)
    low = dot(conv_act.astype(BF), jnp.concatenate([xdt_w, xbc_w], axis=1))
    low_sent = low.astype(BF)
    low_sum = low_sent.astype(F32)
    for s in (1, 3, 2):
        low_sum = low_sum + lax.ppermute(low_sent, "vocab", ring(zs, s)).astype(F32)
    head_t, _, _ = lax.optimization_barrier((head_w.T, all_z, low_sum))
    all_head = lax.all_gather(head_t, DP, axis=0, tiled=True)
    dt_raw = low_sum[:, :rank]
    bc_raw = low_sum[:, rank:].reshape(-1)

    fold = channels // 128
    rate = (a_rate.T * (-LOG2E)).reshape(nstate, fold, 128)
    seq = jax.ShapeDtypeStruct((rows, fold, 128), F32)
    step3, du3, last, total = pl.pallas_call(
        lambda *refs: steps_kernel(rows, local_len, nstate, *refs),
        out_shape=(
            seq,
            seq,
            jax.ShapeDtypeStruct((batch_count, nstate, fold, 128), F32),
            jax.ShapeDtypeStruct((batch_count, fold, 128), F32),
        ),
        in_specs=[smem()] + [vmem()] * 6,
        out_specs=(vmem(),) * 4,
        compiler_params=pltpu.CompilerParams(vmem_limit_bytes=48 << 20),
        name="steps",
    )(
        bc_raw,
        dt_raw,
        dt_gain.reshape(1, rank),
        dt_proj,
        dt_bias.reshape(1, channels),
        conv_act,
        rate,
    )

    half = nstate // CS
    own = lax.dynamic_slice_in_dim(last, core * half, half, 1)
    other = lax.dynamic_slice_in_dim(last, (1 - core) * half, half, 1)
    rate_half = lax.dynamic_slice_in_dim(rate, core * half, half, 0)
    sent = jnp.concatenate([other, total[:, None]], axis=1)
    got = swap_cores(sent)
    state_0 = jnp.where(core == 0, own, got[:, :half])
    state_1 = jnp.where(core == 0, got[:, :half], own)
    total_0 = jnp.where(core == 0, total, got[:, half])
    total_1 = jnp.where(core == 0, got[:, half], total)

    def decay(steps):
        return jnp.exp2(steps[:, None] * rate_half)

    chip_state = decay(total_1) * state_0 + state_1
    chip_total = total_0 + total_1
    coarse = chip_total.astype(BF)
    fine = (chip_total - coarse.astype(F32)).astype(BF)
    packed = jnp.concatenate(
        [chip_state.astype(BF), coarse[:, None], fine[:, None]], axis=1
    )
    chips = YS * XS
    everyone = lax.all_to_all(
        jnp.broadcast_to(packed[None], (chips, *packed.shape)), CHIPS, 0, 0, tiled=True
    )
    z_gate = dot(normed, all_z).astype(BF)
    everyone, z_gate = lax.optimization_barrier((everyone, z_gate))
    chip = y * XS + x
    enter = jnp.zeros_like(chip_state)
    for k in range(chips - 1):
        part = everyone[k].astype(F32)
        later = decay(part[:, half] + part[:, half + 1]) * enter + part[:, :half]
        enter = jnp.where(k < chip, later, enter)
    enter_1 = decay(total_0) * enter + state_0
    kept = jnp.where(core == 0, enter, enter_1)
    given = swap_cores(jnp.where(core == 0, enter_1, enter))
    start = jnp.concatenate(
        [jnp.where(core == 0, kept, given), jnp.where(core == 0, given, kept)], axis=1
    )

    gated = pl.pallas_call(
        lambda *refs: outputs_kernel(rows, local_len, nstate, *refs),
        out_shape=jax.ShapeDtypeStruct((rows, channels), BF),
        in_specs=[smem()] + [vmem()] * 5,
        out_specs=vmem(),
        scratch_shapes=[pltpu.VMEM((rows, fold, 128), F32)],
        compiler_params=pltpu.CompilerParams(vmem_limit_bytes=48 << 20),
        name="outputs",
    )(bc_raw, step3, du3, rate, start, z_gate)

    share = width // zs

    def out_share(by):
        to = lax.rem(zi + by, zs) * share
        return dot(gated, lax.dynamic_slice_in_dim(out_w, to, share, 1))

    arrived = [lax.ppermute(out_share(s).astype(BF), "vocab", ring(zs, s)) for s in (1, 3, 2)]
    mixer = out_share(0)
    for piece in arrived:
        mixer = mixer + piece.astype(F32)
    part = lax.dynamic_slice_in_dim(flat, zi * share, share, 1).astype(F32)
    hidden_share = (part + mixer).astype(BF)
    hidden = jnp.zeros((rows, width), BF)
    for s in (0, 1, 3, 2):
        piece = hidden_share if s == 0 else lax.ppermute(hidden_share, "vocab", ring(zs, s))
        hidden = lax.dynamic_update_slice_in_dim(
            hidden, piece, lax.rem(zi - s + zs, zs) * share, 1
        )
    final = rms_norm(hidden.astype(F32), final_gain, 1e-05).astype(BF)
    logits = dot(final, all_head)
    vocab_rows = head_w.shape[0]
    local_ids = targets.reshape(rows) - zi * vocab_rows
    entry_ids = lax.broadcasted_iota(jnp.int32, (rows, vocab_rows), 1)
    picked = jnp.sum(jnp.where(entry_ids == local_ids[:, None], logits, 0.0), axis=-1)
    top = jnp.max(logits, axis=-1)
    exps = jnp.sum(jnp.exp(logits - top[:, None]), axis=-1)
    stats = jnp.stack([top, exps, picked])
    stats = lax.all_to_all(
        jnp.broadcast_to(stats[None], (zs, *stats.shape)), "vocab", 0, 0, tiled=True
    )
    all_top = jnp.max(stats[:, 0], axis=0)
    all_exps = jnp.sum(stats[:, 1] * jnp.exp(stats[:, 0] - all_top), axis=0)
    token_logp = (jnp.sum(stats[:, 2], axis=0) - (all_top + jnp.log(all_exps))).reshape(
        batch_count, local_len
    )
    positions = lax.axis_index(DP) * local_len + jnp.arange(local_len, dtype=jnp.int32)
    valid = positions[None, :] < lengths[:, None]
    masked = jnp.sum(jnp.where(valid, token_logp, 0.0))
    peers = YS * XS * CS
    sums = lax.all_to_all(jnp.broadcast_to(masked, (peers, 1)), DP, 0, 0, tiled=True)
    mean_logp = jnp.sum(sums) / jnp.sum(lengths.astype(F32))
    return (hidden_share.reshape(batch_count, local_len, share), token_logp, mean_logp)


def solution(mesh):
    split = Mesh(mesh.devices.reshape(YS, XS, CS, mesh.shape["vocab"]), (*DP, "vocab"))
    return jax.shard_map(
        body,
        mesh=split,
        in_specs=(
            P(None, DP, None),
            P(),
            P(DP, "vocab"),
            P(DP, "vocab"),
            P(None, "vocab"),
            P("vocab"),
            P("vocab", None),
            P("vocab", None),
            P(),
            P(None, "vocab"),
            P("vocab"),
            P("vocab", None),
            P("vocab", None),
            P(),
            P("vocab", DP),
            P(None, DP),
            P(),
        ),
        out_specs=(P(None, DP, "vocab"), P(None, DP), P()),
        check_vma=False,
    )
```

time: 364 us -> 263 us (0.72)
  blocking collectives: 49.2 us -> 0 us
  other arithmetic: 55.3 us -> 6.7 us
  local copies, waits for them, and re-layouts: 38.5 us -> 15.4 us
  Pallas kernels: 0 us -> 17.7 us
  waiting for transfers between devices: 124 us -> 117 us
  matrix products: 31.5 us -> 37.3 us
  starting transfers between devices: 45.7 us -> 50.9 us
    ppermute x1 -> x20, waiting for transfers between devices: 0.77 us -> 96.5 us  [the longest x3 31.5 us: body(): far = {s: lax.ppermute(line, DP, turns(s, 1)) for s in (1, 3, 2)}]
    all_gather x2, waiting for transfers between devices: 74.4 us -> 0.04 us  [the longest x1 0.02 us: body(): all_head = lax.all_gather(head_t, DP, axis=0, tiled=True)]
    all_gather x6 -> x0, blocking collectives: 49.2 us -> none  [entering(): pieces = jax.tree.map(lambda part: lax.all_gather(part, axis), so_far)]
    ppermute x1 -> x20, starting transfers between devices: 3.23 us -> 33.2 us  [the longest x3 6.54 us: body(): lax.ppermute(hidden_share, 'vocab', ring(zs, s))]
    all_to_all x7 -> x3, waiting for transfers between devices: 47.8 us -> 19.6 us  [the longest x1 9.05 us: body(): lax.all_to_all(jnp.broadcast_to(packed[None], (chips, *packed.shape)), CH...]
    all_to_all x7 -> x3, starting transfers between devices: 42.4 us -> 17.6 us  [the longest x1 8.11 us: body(): lax.all_to_all(jnp.broadcast_to(masked, (peers, 1)), DP, 0, 0, tiled=True)]
    reduce_sum x50 -> x5, other arithmetic: 25.4 us -> 4.66 us  [the longest x1 2.22 us: body(): exps = jnp.sum(jnp.exp(logits - top[:, None]), axis=-1)]
    pallas_call x0 -> x3, Pallas kernels: none -> 17.7 us  [the longest x1 7.47 us: body(): pl.pallas_call(lambda *refs: outputs_kernel(rows, local_len, nstate, *ref...]
  transfers between devices with their start and end apart: 10 -> 25, of which waited for: 9 -> 17; matrix products, arithmetic and copies ran while one was open for 30% -> 15% of each run, Pallas kernels for 0% -> 7%
where the time goes in v1:
time: 263 us; the launch traced here: 262 us
  waiting for transfers between devices  117 us (44%)
  starting transfers between devices  50.9 us (19%)
  matrix products  37.3 us (14%)
  Pallas kernels  17.7 us (7%)
  between operations  17.3 us (7%)
  local copies, waits for them, and re-layouts  15.4 us (6%)
  other arithmetic  6.7 us (3%)
    dot_general x15, matrix products, dot(): return jnp.dot(a, b, preferred_element_type=F32)  37.3 us
    ppermute x3, waiting for transfers between devices, body(): far = {s: lax.ppermute(line, DP, turns(s, 1)) for s in (1, 3, 2)}  31.5 us
    ppermute x3, waiting for transfers between devices, body(): lax.ppermute(hidden_share, 'vocab', ring(zs, s))  19.6 us
    ppermute x3, waiting for transfers between devices, body(): lax.ppermute(out_share(s).astype(BF), 'vocab', ring(zs, s))  17 us
    ppermute x3, waiting for transfers between devices, body(): low_sum = low_sum + lax.ppermute(low_sent, 'vocab', ring(zs, s)).astype(F32)  11.5 us
    ppermute x1, waiting for transfers between devices, body(): tail = lax.ppermute(resid[:, local_len - (taps - 1):, :], DP, order)  10.1 us
    all_to_all x1, waiting for transfers between devices, body(): lax.all_to_all(jnp.broadcast_to(packed[None], (chips, *packed.shape)), CH...  9.05 us
    all_to_all x1, starting transfers between devices, body(): lax.all_to_all(jnp.broadcast_to(masked, (peers, 1)), DP, 0, 0, tiled=True)  8.11 us
  transfers between devices with their start and end apart: 25, of which 17 were waited for; matrix products, arithmetic and copies ran while one was open for 15% of the time, Pallas kernels for 7%

profile of v1, /device:TPU:1, one launch (start us, length us, event | category | flops | bytes accessed | tf_op | source)
XLA Modules:
  0.0 262.1 jit_solution(18071798827227852979)
XLA Ops:
  8.0 2.2 collective-permute-start.1
  10.1 2.6 collective-permute-start.2
  15.9 4.0 %collective-permute-done.2 = bf16[128,1024]{1,0:T(8,128)(2,1)S(1)} collective-permute-done((bf16[128,1024]{1,0:T(8,128)(2,1)}, bf16[128,1024]{1,0:T(8,128)(2,1)S(1)}, u32[]{:S(2)}, u32[]{:S(2)}) %collective-permute-start.2) | collective-permute-done | bytes 262176 | tf_op jit(solution)/shard_map/ppermute | solution.py:43
  21.8 5.3 %collective-permute-start = (bf16[2,3,4096]{2,1,0:T(4,128)(2,1)S(1)}, bf16[2,3,4096]{2,1,0:T(4,128)(2,1)S(1)}, u32[]{:S(2)}, u32[]{:S(2)}) collective-permute-start(bf16[2,3,4096]{2,1,0:T(4,128)(2,1)S(1)} %slice.262), channel_id=1, source_target_pairs={{0,4},{4,8},{8,12},{12,16},{16,20},{20,24},{24,28},{28,32},{32,36}... | collective-permute-start | bytes 147464 | tf_op jit(solution)/shard_map/ppermute | solution.py:177
  27.4 10.1 %collective-permute-done = bf16[2,3,4096]{2,1,0:T(4,128)(2,1)S(1)} collective-permute-done((bf16[2,3,4096]{2,1,0:T(4,128)(2,1)S(1)}, bf16[2,3,4096]{2,1,0:T(4,128)(2,1)S(1)}, u32[]{:S(2)}, u32[]{:S(2)}) %collective-permute-start) | collective-permute-done | bytes 49184 | tf_op jit(solution)/shard_map/ppermute | solution.py:177
  37.6 3.3 %norm.1 = (bf16[256,4096]{1,0:T(8,128)(2,1)S(1)}, bf16[272,2048]{1,0:T(8,128)(2,1)S(1)}, bf16[272,2048]{1,0:T(8,128)(2,1)S(1)}) custom-call(s32[32]{0:T(128)S(1)} %stack.143.refs_0_, bf16[256,4096]{1,0:T(8,128)(2,1)} %bitcast.182, bf16[16,4096]{1,0:T(8,128)(2,1)S(1)} %pad.4.refs_2_, f32[1,4096]{1,0:T(1,128)S(1)} %bitcast.179), custom_call_target="tpu_custom_call" | custom-call | tf_op jit(solution)/shard_map/norm/pallas_call | solution.py:189
  41.0 1.3 copy-done.4
  42.3 4.2 %collective-permute-start.6 = (bf16[512,1024]{1,0:T(8,128)(2,1)S(1)}, bf16[512,1024]{1,0:T(8,128)(2,1)}, u32[]{:S(2)}, u32[]{:S(2)}) collective-permute-start(bf16[512,1024]{1,0:T(8,128)(2,1)S(1)} %constant_dynamic-update-slice_fusion), channel_id=1, source_target_pairs={{0,64},{4,20},{8,72},{12,28},{16,80},{20,4},{24,88},{28,12},{32,96... | collective-permute-start | bytes 3145736 | tf_op jit(solution)/shard_map/ppermute | solution.py:179
  48.4 1.5 fusion.119
  49.9 1.7 fusion.65
  51.6 1.8 fusion.58
  53.4 22.5 %collective-permute-done.6 = bf16[512,1024]{1,0:T(8,128)(2,1)} collective-permute-done((bf16[512,1024]{1,0:T(8,128)(2,1)S(1)}, bf16[512,1024]{1,0:T(8,128)(2,1)}, u32[]{:S(2)}, u32[]{:S(2)}) %collective-permute-start.6) | collective-permute-done | bytes 1048608 | tf_op jit(solution)/shard_map/ppermute | solution.py:179
  75.9 1.8 fusion.54
  77.7 9.0 %collective-permute-done.5 = bf16[512,1024]{1,0:T(8,128)(2,1)S(1)} collective-permute-done((bf16[512,1024]{1,0:T(8,128)(2,1)S(1)}, bf16[512,1024]{1,0:T(8,128)(2,1)S(1)}, u32[]{:S(2)}, u32[]{:S(2)}) %collective-permute-start.5) | collective-permute-done | bytes 1048608 | tf_op jit(solution)/shard_map/ppermute | solution.py:179
  86.7 1.4 fusion.56
  88.1 1.4 fusion.32
  90.5 1.7 fusion.61
  94.9 2.7 %collective-permute-start.10 = (bf16[256,288]{1,0:T(8,128)(2,1)S(1)}, bf16[256,288]{1,0:T(8,128)(2,1)S(1)}, u32[]{:S(2)}, u32[]{:S(2)}) collective-permute-start(bf16[256,288]{1,0:T(8,128)(2,1)S(1)} %convolution_convert_fusion.1), channel_id=1, source_target_pairs={{0,3},{1,0},{2,1},{3,2},{4,7},{5,4},{6,5},{7,6},{8,11},{9,8},{10,9... | collective-permute-start | bytes 442376 | tf_op jit(solution)/shard_map/ppermute | solution.py:222
  98.7 7.2 %collective-permute-done.10 = bf16[256,288]{1,0:T(8,128)(2,1)S(1)} collective-permute-done((bf16[256,288]{1,0:T(8,128)(2,1)S(1)}, bf16[256,288]{1,0:T(8,128)(2,1)S(1)}, u32[]{:S(2)}, u32[]{:S(2)}) %collective-permute-start.10) | collective-permute-done | bytes 147488 | tf_op jit(solution)/shard_map/ppermute | solution.py:222
  105.9 4.3 %collective-permute-done.9 = bf16[256,288]{1,0:T(8,128)(2,1)S(1)} collective-permute-done((bf16[256,288]{1,0:T(8,128)(2,1)S(1)}, bf16[256,288]{1,0:T(8,128)(2,1)S(1)}, u32[]{:S(2)}, u32[]{:S(2)}) %collective-permute-start.9) | collective-permute-done | bytes 147488 | tf_op jit(solution)/shard_map/ppermute | solution.py:222
  111.6 6.9 %steps.1 = (f32[256,8,128]{2,1,0:T(8,128)S(1)}, f32[256,8,128]{2,1,0:T(8,128)S(1)}, f32[2,16,8,128]{3,2,1,0:T(8,128)S(1)}, f32[2,8,128]{2,1,0:T(8,128)S(1)}) custom-call(f32[8192]{0:T(1024)S(1)} %reshape.129.refs_0_, f32[256,256]{1,0:T(8,128)S(1)} %slice.358.refs_1_, f32[1,256]{1,0:T(1,128)S(1)} %bitcast.181, bf16[256,1024]{1,0:T(8,128)(2,1)S(1)} %copy-done, ...), custom_call_target="tpu_custom_call" | custom-call | tf_op jit(solution)/shard_map/steps/pallas_call | solution.py:231
  121.1 6.2 %all-to-all-start = ((bf16[16,2,10,8,128]{4,3,2,1,0:T(8,128)(2,1)}), bf16[16,2,10,8,128]{4,3,2,1,0:T(8,128)(2,1)S(1)}, u32[]{:S(2)}, u32[]{:S(2)}) async-start(bf16[16,2,10,8,128]{4,3,2,1,0:T(8,128)(2,1)} %broadcast_in_dim.25), calls=%async_computation | async-start | bytes 1310720 | tf_op jit(solution)/shard_map/all_to_all | solution.py:275
  127.4 6.4 %convolution_convert_fusion.refs_5_ = bf16[256,1024]{1,0:T(8,128)(2,1)S(1)} fusion(bf16[256,4096]{1,0:T(8,128)(2,1)} %copy-done.4, bf16[4096,1024]{1,0:T(8,128)(2,1)} %all-gather.3.cloned.1.call-done), kind=kOutput, calls=%fused_computation.33 | convolution fusion | flops 2147745792 | bytes 11010048 | tf_op jit(solution)/shard_map/dot_general | solution.py:62
  133.7 9.1 %all-to-all-done = bf16[16,2,10,8,128]{4,3,2,1,0:T(8,128)(2,1)S(1)} async-done(((bf16[16,2,10,8,128]{4,3,2,1,0:T(8,128)(2,1)}), bf16[16,2,10,8,128]{4,3,2,1,0:T(8,128)(2,1)S(1)}, u32[]{:S(2)}, u32[]{:S(2)}) %all-to-all-start) | async-done | bytes 655392 | tf_op jit(solution)/shard_map/all_to_all | solution.py:275
  143.3 1.3 collective-permute-start.13
  145.6 7.5 %outputs.1 = bf16[256,1024]{1,0:T(8,128)(2,1)S(1)} custom-call(f32[8192]{0:T(1024)S(1)} %reshape.129.refs_0_, f32[256,8,128]{2,1,0:T(8,128)S(1)} %get-tuple-element.17.refs_1_, f32[256,8,128]{2,1,0:T(8,128)S(1)} %get-tuple-element.18.refs_2_, f32[16,8,128]{2,1,0:T(8,128)S(1)} %bitcast.177, f32[2,16,8,128]{3,2,1,0:T(8,128)S(1)} %pad_maximum_fusion.refs_4_, ...), custom_call_target="tpu_custom_call" | custom-call | tf_op jit(solution)/shard_map/outputs/pallas_call | solution.py:293
  153.1 2.4 fusion.37
  155.7 2.4 fusion.40
  158.1 2.6 collective-permute-start.15
  160.7 2.3 fusion.43
  163.4 6.6 %collective-permute-done.14 = bf16[256,1024]{1,0:T(8,128)(2,1)S(1)} collective-permute-done((bf16[256,1024]{1,0:T(8,128)(2,1)S(1)}, bf16[256,1024]{1,0:T(8,128)(2,1)S(1)}, u32[]{:S(2)}, u32[]{:S(2)}) %collective-permute-start.14) | collective-permute-done | bytes 524320 | tf_op jit(solution)/shard_map/ppermute | solution.py:309
  170.0 2.2 collective-permute-done.15
  173.0 8.3 %collective-permute-done.16 = bf16[256,1024]{1,0:T(8,128)(2,1)} collective-permute-done((bf16[256,1024]{1,0:T(8,128)(2,1)S(1)}, bf16[256,1024]{1,0:T(8,128)(2,1)}, u32[]{:S(2)}, u32[]{:S(2)}) %collective-permute-start.16) | collective-permute-done | bytes 524320 | tf_op jit(solution)/shard_map/ppermute | solution.py:309
  182.8 2.9 %constant_dynamic-update-slice_fusion.6 = (bf16[256,4096]{1,0:T(8,128)(2,1)S(1)}, bf16[256,1024]{1,0:T(8,128)(2,1)S(1)}) fusion(bf16[256,4096]{1,0:T(8,128)(2,1)S(1)} %broadcast_in_dim.27, s32[]{:T(128)S(6)} %select_n.322, bf16[256,1024]{1,0:T(8,128)(2,1)} %collective-permute-done.16, bf16[256,1024]{1,0:T(8,128)(2,1)S(1)} %copy-done.9, ...), kind=kOutput, calls=%fused_computation.175 | convolution fusion | flops 539230208 | bytes 5767180 | tf_op jit(solution)/shard_map/dot_general | solution.py:62
  185.7 2.8 %collective-permute-start.17 = (bf16[256,1024]{1,0:T(8,128)(2,1)S(1)}, bf16[256,1024]{1,0:T(8,128)(2,1)}, u32[]{:S(2)}, u32[]{:S(2)}) collective-permute-start(bf16[256,1024]{1,0:T(8,128)(2,1)S(1)} %get-tuple-element.67), channel_id=1, source_target_pairs={{0,1},{1,2},{2,3},{3,0},{4,5},{5,6},{6,7},{7,4},{8,9},{9,10},{10,1... | collective-permute-start | bytes 1572872 | tf_op jit(solution)/shard_map/ppermute | solution.py:317
  188.5 2.7 %collective-permute-start.18 = (bf16[256,1024]{1,0:T(8,128)(2,1)S(1)}, bf16[256,1024]{1,0:T(8,128)(2,1)}, u32[]{:S(2)}, u32[]{:S(2)}) collective-permute-start(bf16[256,1024]{1,0:T(8,128)(2,1)S(1)} %get-tuple-element.67), channel_id=1, source_target_pairs={{0,3},{1,0},{2,1},{3,2},{4,7},{5,4},{6,5},{7,6},{8,11},{9,8},{10,9... | collective-permute-start | bytes 1572872 | tf_op jit(solution)/shard_map/ppermute | solution.py:317
  191.1 1.1 collective-permute-start.19
  192.2 9.8 %collective-permute-done.17 = bf16[256,1024]{1,0:T(8,128)(2,1)} collective-permute-done((bf16[256,1024]{1,0:T(8,128)(2,1)S(1)}, bf16[256,1024]{1,0:T(8,128)(2,1)}, u32[]{:S(2)}, u32[]{:S(2)}) %collective-permute-start.17) | collective-permute-done | bytes 524320 | tf_op jit(solution)/shard_map/ppermute | solution.py:317
  203.1 1.1 constant_dynamic-update-slice_fusion.4
  204.2 9.8 %collective-permute-done.19 = bf16[256,1024]{1,0:T(8,128)(2,1)S(1)} collective-permute-done((bf16[256,1024]{1,0:T(8,128)(2,1)S(1)}, bf16[256,1024]{1,0:T(8,128)(2,1)S(1)}, u32[]{:S(2)}, u32[]{:S(2)}) %collective-permute-start.19) | collective-permute-done | bytes 524320 | tf_op jit(solution)/shard_map/ppermute | solution.py:317
  214.6 9.7 %fusion.120 = (f32[256]{0:T(256)S(1)}, f32[256,2048]{1,0:T(8,128)}) fusion(bf16[4096,2048]{0,1:T(8,128)(2,1)} %all-gather.5.cloned.1.call-done, bf16[256,4096]{1,0:T(8,128)(2,1)S(1)} %constant_dynamic-update-slice_fusion.7, f32[4096]{0:T(1024)S(1)} %copy-done.19, f32[256]{0:T(256)S(1)} %add_rsqrt_fusion), kind=kOutput, calls=%fused_computation.195 | convolution fusion | flops 4299685888 | bytes 20989952 | tf_op jit(solution)/shard_map/dot_general | solution.py:62
  224.3 2.2 exponential_reduce_fusion
  227.2 3.2 %all-to-all-start.1 = ((f32[4,3,256]{2,1,0:T(4,128)}), f32[4,3,256]{2,1,0:T(4,128)S(1)}, u32[]{:S(2)}, u32[]{:S(2)}) async-start(f32[4,3,256]{2,1,0:T(4,128)} %broadcast_in_dim.29), calls=%async_computation.1 | async-start | bytes 32768 | tf_op jit(solution)/shard_map/all_to_all | solution.py:330
  230.5 4.2 %all-to-all-done.1 = f32[4,3,256]{2,1,0:T(4,128)S(1)} async-done(((f32[4,3,256]{2,1,0:T(4,128)}), f32[4,3,256]{2,1,0:T(4,128)S(1)}, u32[]{:S(2)}, u32[]{:S(2)}) %all-to-all-start.1) | async-done | bytes 12320 | tf_op jit(solution)/shard_map/all_to_all | solution.py:330
  234.7 1.2 fusion.113
  235.9 1.2 broadcast_in_dim.31
  237.1 8.1 %all-to-all-start.2 = ((f32[32,1,1]{2,1,0:T(1,128)}), f32[32,1,1]{2,1,0:T(1,128)S(1)}, u32[]{:S(2)}, u32[]{:S(2)}) async-start(f32[32,1,1]{2,1,0:T(1,128)} %broadcast_in_dim.31), calls=%async_computation.2 | async-start | bytes 32768 | tf_op jit(solution)/shard_map/all_to_all | solution.py:342
  245.8 6.4 %all-to-all-done.2 = f32[32,1,1]{2,1,0:T(1,128)S(1)} async-done(((f32[32,1,1]{2,1,0:T(1,128)}), f32[32,1,1]{2,1,0:T(1,128)S(1)}, u32[]{:S(2)}, u32[]{:S(2)}) %all-to-all-start.2) | async-done | bytes 160 | tf_op jit(solution)/shard_map/all_to_all | solution.py:342
  (121 shorter events, 24.4 us)
Async XLA Ops:
  7.2 30.5 %copy-start.1 = (f32[4096]{0:T(1024)S(1)}, f32[4096]{0:T(1024)}, u32[]{:S(2)}) copy-start(f32[4096]{0:T(1024)} %param.18) | copy-start | bytes 49156
  7.2 103.1 %all-gather.3.cloned.1.call-start = ((), (), s32[]{:S(2)}) async-start(), calls=%async_computation.3 | async-start | bytes 8650752 | tf_op jit(solution)/shard_map/all_gather | solution.py:174
  7.9 206.7 %all-gather.5.cloned.1.call-start = ((), (), s32[]{:S(2)}) async-start(), calls=%async_computation.4 | async-start | bytes 17301504 | tf_op jit(solution)/shard_map/all_gather | solution.py:224
  8.0 7.9 %collective-permute-start.1 = (bf16[128,1024]{1,0:T(8,128)(2,1)}, bf16[128,1024]{1,0:T(8,128)(2,1)S(1)}, u32[]{:S(2)}, u32[]{:S(2)}) collective-permute-start(bf16[128,1024]{1,0:T(8,128)(2,1)} %param.19), channel_id=1, source_target_pairs={{0,8},{4,36},{8,16},{12,44},{16,24},{20,52},{24,0},{28,60},{32,40}... | collective-permute-start | bytes 786440 | tf_op jit(solution)/shard_map/ppermute | solution.py:43
  10.1 9.7 %collective-permute-start.2 = (bf16[128,1024]{1,0:T(8,128)(2,1)}, bf16[128,1024]{1,0:T(8,128)(2,1)S(1)}, u32[]{:S(2)}, u32[]{:S(2)}) collective-permute-start(bf16[128,1024]{1,0:T(8,128)(2,1)} %param.19), channel_id=1, source_target_pairs={{0,16},{4,68},{8,24},{12,76},{16,0},{20,84},{24,8},{28,92},{32,48}... | collective-permute-start | bytes 786440 | tf_op jit(solution)/shard_map/ppermute | solution.py:43
  12.8 7.1 %collective-permute-start.3 = (bf16[128,1024]{1,0:T(8,128)(2,1)}, bf16[128,1024]{1,0:T(8,128)(2,1)S(1)}, u32[]{:S(2)}, u32[]{:S(2)}) collective-permute-start(bf16[128,1024]{1,0:T(8,128)(2,1)} %param.19), channel_id=1, source_target_pairs={{0,24},{4,100},{8,0},{12,108},{16,8},{20,116},{24,16},{28,124},{32... | collective-permute-start | bytes 786440 | tf_op jit(solution)/shard_map/ppermute | solution.py:43
  19.9 30.0 %collective-permute-start.4 = (bf16[512,1024]{1,0:T(8,128)(2,1)S(1)}, bf16[512,1024]{1,0:T(8,128)(2,1)}, u32[]{:S(2)}, u32[]{:S(2)}) collective-permute-start(bf16[512,1024]{1,0:T(8,128)(2,1)S(1)} %constant_dynamic-update-slice_fusion), channel_id=1, source_target_pairs={{0,32},{4,12},{8,40},{12,20},{16,48},{20,28},{24,56},{28,4},{32,64... | collective-permute-start | bytes 3145736 | tf_op jit(solution)/shard_map/ppermute | solution.py:179
  21.8 15.7 %collective-permute-start = (bf16[2,3,4096]{2,1,0:T(4,128)(2,1)S(1)}, bf16[2,3,4096]{2,1,0:T(4,128)(2,1)S(1)}, u32[]{:S(2)}, u32[]{:S(2)}) collective-permute-start(bf16[2,3,4096]{2,1,0:T(4,128)(2,1)S(1)} %slice.262), channel_id=1, source_target_pairs={{0,4},{4,8},{8,12},{12,16},{16,20},{20,24},{24,28},{28,32},{32,36}... | collective-permute-start | bytes 147464 | tf_op jit(solution)/shard_map/ppermute | solution.py:177
  41.0 1.4 copy-start.4
  42.3 9.3 %collective-permute-start.7 = (bf16[272,2048]{1,0:T(8,128)(2,1)S(1)}, bf16[272,2048]{1,0:T(8,128)(2,1)}, u32[]{:S(2)}, u32[]{:S(2)}) collective-permute-start(bf16[272,2048]{1,0:T(8,128)(2,1)S(1)} %get-tuple-element.16), channel_id=1, source_target_pairs={{0,4},{4,0},{1,5},{5,1},{2,6},{6,2},{3,7},{7,3},{8,12},{12,8},{9,1... | collective-permute-start | bytes 3342344 | tf_op jit(solution)/shard_map/ppermute | solution.py:39
  42.3 33.6 %collective-permute-start.6 = (bf16[512,1024]{1,0:T(8,128)(2,1)S(1)}, bf16[512,1024]{1,0:T(8,128)(2,1)}, u32[]{:S(2)}, u32[]{:S(2)}) collective-permute-start(bf16[512,1024]{1,0:T(8,128)(2,1)S(1)} %constant_dynamic-update-slice_fusion), channel_id=1, source_target_pairs={{0,64},{4,20},{8,72},{12,28},{16,80},{20,4},{24,88},{28,12},{32,96... | collective-permute-start | bytes 3145736 | tf_op jit(solution)/shard_map/ppermute | solution.py:179
  47.5 39.2 %collective-permute-start.5 = (bf16[512,1024]{1,0:T(8,128)(2,1)S(1)}, bf16[512,1024]{1,0:T(8,128)(2,1)S(1)}, u32[]{:S(2)}, u32[]{:S(2)}) collective-permute-start(bf16[512,1024]{1,0:T(8,128)(2,1)S(1)} %constant_dynamic-update-slice_fusion), channel_id=1, source_target_pairs={{0,96},{4,28},{8,104},{12,4},{16,112},{20,12},{24,120},{28,20},{32... | collective-permute-start | bytes 3145736 | tf_op jit(solution)/shard_map/ppermute | solution.py:179
  89.5 2.6 collective-permute-start.8
  92.7 0.7 copy-start.12
  92.7 0.7 copy-start.13
  92.7 0.7 copy-start.14
  92.7 0.7 copy-start.15
  92.7 0.7 copy-start.16
  93.4 1.0 copy-start.10
  94.1 16.3 %copy-start.11 = (f32[1024,16]{0,1:T(8,128)S(1)}, f32[1024,16]{0,1:T(8,128)}, u32[]{:S(2)}) copy-start(f32[1024,16]{0,1:T(8,128)} %param.28) | copy-start | bytes 196612
  94.5 16.1 %copy-start.2 = (f32[1024]{0:T(1024)S(1)}, f32[1024]{0:T(1024)}, u32[]{:S(2)}) copy-start(f32[1024]{0:T(1024)} %param.27) | copy-start | bytes 12292
  94.5 16.1 %copy-start.3 = (f32[256]{0:T(256)S(1)}, f32[256]{0:T(256)}, u32[]{:S(2)}) copy-start(f32[256]{0:T(256)} %param.25) | copy-start | bytes 3076
  94.9 11.0 %collective-permute-start.10 = (bf16[256,288]{1,0:T(8,128)(2,1)S(1)}, bf16[256,288]{1,0:T(8,128)(2,1)S(1)}, u32[]{:S(2)}, u32[]{:S(2)}) collective-permute-start(bf16[256,288]{1,0:T(8,128)(2,1)S(1)} %convolution_convert_fusion.1), channel_id=1, source_target_pairs={{0,3},{1,0},{2,1},{3,2},{4,7},{5,4},{6,5},{7,6},{8,11},{9,8},{10,9... | collective-permute-start | bytes 442376 | tf_op jit(solution)/shard_map/ppermute | solution.py:222
  97.6 8.2 %collective-permute-start.11 = (bf16[256,288]{1,0:T(8,128)(2,1)S(1)}, bf16[256,288]{1,0:T(8,128)(2,1)S(1)}, u32[]{:S(2)}, u32[]{:S(2)}) collective-permute-start(bf16[256,288]{1,0:T(8,128)(2,1)S(1)} %convolution_convert_fusion.1), channel_id=1, source_target_pairs={{0,2},{1,3},{2,0},{3,1},{4,6},{5,7},{6,4},{7,5},{8,10},{9,11},{10,... | collective-permute-start | bytes 442376 | tf_op jit(solution)/shard_map/ppermute | solution.py:222
  98.0 12.1 %collective-permute-start.9 = (bf16[256,288]{1,0:T(8,128)(2,1)S(1)}, bf16[256,288]{1,0:T(8,128)(2,1)S(1)}, u32[]{:S(2)}, u32[]{:S(2)}) collective-permute-start(bf16[256,288]{1,0:T(8,128)(2,1)S(1)} %convolution_convert_fusion.1), channel_id=1, source_target_pairs={{0,1},{1,2},{2,3},{3,0},{4,5},{5,6},{6,7},{7,4},{8,9},{9,10},{10,1... | collective-permute-start | bytes 442376 | tf_op jit(solution)/shard_map/ppermute | solution.py:222
  110.6 1.0 copy-start
  118.6 1.5 collective-permute-start.12
  121.1 21.7 %all-to-all-start = ((bf16[16,2,10,8,128]{4,3,2,1,0:T(8,128)(2,1)}), bf16[16,2,10,8,128]{4,3,2,1,0:T(8,128)(2,1)S(1)}, u32[]{:S(2)}, u32[]{:S(2)}) async-start(bf16[16,2,10,8,128]{4,3,2,1,0:T(8,128)(2,1)} %broadcast_in_dim.25), calls=%async_computation | async-start | bytes 1310720 | tf_op jit(solution)/shard_map/all_to_all | solution.py:275
  143.3 2.2 collective-permute-start.13
  155.5 14.5 %collective-permute-start.14 = (bf16[256,1024]{1,0:T(8,128)(2,1)S(1)}, bf16[256,1024]{1,0:T(8,128)(2,1)S(1)}, u32[]{:S(2)}, u32[]{:S(2)}) collective-permute-start(bf16[256,1024]{1,0:T(8,128)(2,1)S(1)} %fusion.37), channel_id=1, source_target_pairs={{0,1},{1,2},{2,3},{3,0},{4,5},{5,6},{6,7},{7,4},{8,9},{9,10},{10,1... | collective-permute-start | bytes 1572872 | tf_op jit(solution)/shard_map/ppermute | solution.py:309
  158.1 14.1 %collective-permute-start.15 = (bf16[256,1024]{1,0:T(8,128)(2,1)S(1)}, bf16[256,1024]{1,0:T(8,128)(2,1)S(1)}, u32[]{:S(2)}, u32[]{:S(2)}) collective-permute-start(bf16[256,1024]{1,0:T(8,128)(2,1)S(1)} %fusion.40), channel_id=1, source_target_pairs={{0,3},{1,0},{2,1},{3,2},{4,7},{5,4},{6,5},{7,6},{8,11},{9,8},{10,9... | collective-permute-start | bytes 1572872 | tf_op jit(solution)/shard_map/ppermute | solution.py:309
  163.0 18.3 %collective-permute-start.16 = (bf16[256,1024]{1,0:T(8,128)(2,1)S(1)}, bf16[256,1024]{1,0:T(8,128)(2,1)}, u32[]{:S(2)}, u32[]{:S(2)}) collective-permute-start(bf16[256,1024]{1,0:T(8,128)(2,1)S(1)} %fusion.43), channel_id=1, source_target_pairs={{0,2},{1,3},{2,0},{3,1},{4,6},{5,7},{6,4},{7,5},{8,10},{9,11},{10,... | collective-permute-start | bytes 1572872 | tf_op jit(solution)/shard_map/ppermute | solution.py:309
  170.0 2.2 copy-start.6
  172.2 0.8 copy-start.8
  181.2 1.2 copy-start.7
  181.2 1.5 copy-start.9
  182.8 9.5 %copy-start.17 = (s32[2,128]{1,0:T(2,128)S(1)}, s32[2,128]{1,0:T(2,128)}, u32[]{:S(2)}) copy-start(s32[2,128]{1,0:T(2,128)} %param.32) | copy-start | bytes 3076
  185.7 28.9 %copy-start.5 = (bf16[256,1024]{1,0:T(8,128)(2,1)}, bf16[256,1024]{1,0:T(8,128)(2,1)S(1)}, u32[]{:S(2)}) copy-start(bf16[256,1024]{1,0:T(8,128)(2,1)S(1)} %get-tuple-element.67) | copy-start | bytes 1572868
  185.7 16.3 %collective-permute-start.17 = (bf16[256,1024]{1,0:T(8,128)(2,1)S(1)}, bf16[256,1024]{1,0:T(8,128)(2,1)}, u32[]{:S(2)}, u32[]{:S(2)}) collective-permute-start(bf16[256,1024]{1,0:T(8,128)(2,1)S(1)} %get-tuple-element.67), channel_id=1, source_target_pairs={{0,1},{1,2},{2,3},{3,0},{4,5},{5,6},{6,7},{7,4},{8,9},{9,10},{10,1... | collective-permute-start | bytes 1572872 | tf_op jit(solution)/shard_map/ppermute | solution.py:317
  188.5 14.6 %collective-permute-start.18 = (bf16[256,1024]{1,0:T(8,128)(2,1)S(1)}, bf16[256,1024]{1,0:T(8,128)(2,1)}, u32[]{:S(2)}, u32[]{:S(2)}) collective-permute-start(bf16[256,1024]{1,0:T(8,128)(2,1)S(1)} %get-tuple-element.67), channel_id=1, source_target_pairs={{0,3},{1,0},{2,1},{3,2},{4,7},{5,4},{6,5},{7,6},{8,11},{9,8},{10,9... | collective-permute-start | bytes 1572872 | tf_op jit(solution)/shard_map/ppermute | solution.py:317
  191.1 22.9 %collective-permute-start.19 = (bf16[256,1024]{1,0:T(8,128)(2,1)S(1)}, bf16[256,1024]{1,0:T(8,128)(2,1)S(1)}, u32[]{:S(2)}, u32[]{:S(2)}) collective-permute-start(bf16[256,1024]{1,0:T(8,128)(2,1)S(1)} %get-tuple-element.67), channel_id=1, source_target_pairs={{0,2},{1,3},{2,0},{3,1},{4,6},{5,7},{6,4},{7,5},{8,10},{9,11},{10,... | collective-permute-start | bytes 1572872 | tf_op jit(solution)/shard_map/ppermute | solution.py:317
  203.1 11.5 %copy-start.19 = (f32[4096]{0:T(1024)S(1)}, f32[4096]{0:T(1024)}, u32[]{:S(2)}) copy-start(f32[4096]{0:T(1024)} %param.30) | copy-start | bytes 49156
  224.3 10.3 %copy-start.18 = (s32[2]{0:T(128)S(1)}, s32[2]{0:T(128)}, u32[]{:S(2)}) copy-start(s32[2]{0:T(128)} %param.33) | copy-start | bytes 28
  227.2 7.4 %all-to-all-start.1 = ((f32[4,3,256]{2,1,0:T(4,128)}), f32[4,3,256]{2,1,0:T(4,128)S(1)}, u32[]{:S(2)}, u32[]{:S(2)}) async-start(f32[4,3,256]{2,1,0:T(4,128)} %broadcast_in_dim.29), calls=%async_computation.1 | async-start | bytes 32768 | tf_op jit(solution)/shard_map/all_to_all | solution.py:330
  237.1 15.1 %all-to-all-start.2 = ((f32[32,1,1]{2,1,0:T(1,128)}), f32[32,1,1]{2,1,0:T(1,128)S(1)}, u32[]{:S(2)}, u32[]{:S(2)}) async-start(f32[32,1,1]{2,1,0:T(1,128)} %broadcast_in_dim.31), calls=%async_computation.2 | async-start | bytes 32768 | tf_op jit(solution)/shard_map/all_to_all | solution.py:342
Sparse Core Ops, SparseCore 0:
  10.3 69.7 all-gather.2
  110.5 86.7 all-gather.4

commit v2 on v1

--- a/solution.py
+++ b/solution.py
@@ -39,9 +39,13 @@
     return lax.ppermute(array, "dp_2", ring(CS, 1))
 
 
-def line_of_chips(shard):
-    near = {s: lax.ppermute(shard, DP, turns(s, 0)) for s in (1, 3, 2)}
-    return jnp.concatenate([shard, near[1], near[2], near[3]], axis=0)
+def around(array, axis, hops):
+    middle = array.shape[0] // 2
+    behind = lax.ppermute(array, axis, hops(1))
+    ahead = lax.ppermute(array, axis, hops(3))
+    first = lax.ppermute(behind[:middle], axis, hops(1))
+    second = lax.ppermute(ahead[middle:], axis, hops(3))
+    return behind, (first, second), ahead
 
 
 def blocks_in_order(y, x, core):
@@ -132,6 +136,63 @@
         gate = z[:, j * 128 : (j + 1) * 128].astype(F32)
         gate = gate / (1.0 + jnp.exp(-gate))
         gated[:, j * 128 : (j + 1) * 128] = (y3[:, j, :] * gate).astype(BF)
+
+
+def scaled_dot(j, order, deep, lhs, gain, head):
+    values = lhs.astype(F32)
+    at = pl.ds(pl.multiple_of(order[j] * deep, deep), deep)
+    squares = jnp.sum(values * values, axis=-1, keepdims=True)
+    return dot((values * gain[:, at]).astype(BF), head[...]), squares
+
+
+def add_blocks(pieces, order, gain, head, before, acc, squares):
+    deep = head.shape[0]
+    per = pieces[0].shape[1] // deep
+    for j in range(len(pieces) // 2 * per):
+
+        @pl.when(pl.program_id(0) == j)
+        def _():
+            cut = slice(j % per * deep, (j % per + 1) * deep)
+            upper, lower = pieces[j // per * 2 : j // per * 2 + 2]
+            lhs = jnp.concatenate([upper[:, cut], lower[:, cut]], axis=0)
+            product, part = scaled_dot(j, order, deep, lhs, gain, head)
+            part = jnp.broadcast_to(part, squares.shape)
+            if j > 0:
+                acc[...] += product
+                squares[...] += part
+            elif before:
+                acc[...] = product + before[0][...]
+                squares[...] = part + before[1][...]
+            else:
+                acc[...] = product
+                squares[...] = part
+
+
+def own_kernel(order, upper, lower, gain, head, acc, squares):
+    add_blocks((upper, lower), order, gain, head, None, acc, squares)
+
+
+def near_kernel(order, a, b, c, d, gain, head, acc_in, squares_in, acc, squares):
+    add_blocks((a, b, c, d), order, gain, head, (acc_in, squares_in), acc, squares)
+
+
+def last_kernel(order, upper, lower, gain, head, acc_in, squares_in, ids, stats, acc, squares):
+    add_blocks((upper, lower), order, gain, head, (acc_in, squares_in), acc, squares)
+    per = upper.shape[1] // head.shape[0]
+    width = gain.shape[1]
+
+    @pl.when(pl.program_id(0) == per - 1)
+    def _():
+        rows, some = acc.shape[0], 16
+        lane = lax.broadcasted_iota(jnp.int32, (some, 128), 1)
+        entry = lax.broadcasted_iota(jnp.int32, (some, acc.shape[1]), 1)
+        for r in range(0, rows, some):
+            cut = slice(r, r + some)
+            logits = acc[cut] * lax.rsqrt(squares[cut, :1] / width + 1e-05)
+            top = jnp.max(logits, axis=-1, keepdims=True)
+            exps = jnp.sum(jnp.exp(logits - top), axis=-1, keepdims=True)
+            picked = jnp.sum(jnp.where(entry == ids[cut], logits, 0.0), axis=-1, keepdims=True)
+            stats[cut] = jnp.where(lane == 0, top, jnp.where(lane == 1, exps, picked))
 
 
 def vmem():
@@ -171,19 +232,15 @@
     zi = lax.axis_index("vocab")
     zs = lax.axis_size("vocab")
 
-    all_z = lax.all_gather(in_z, DP, axis=0, tiled=True)
-
     order = [(i, i + 1) for i in range(YS * XS * CS - 1)]
     tail = lax.ppermute(resid[:, local_len - (taps - 1) :, :], DP, order)
-    line = line_of_chips(in_x)
-    far = {s: lax.ppermute(line, DP, turns(s, 1)) for s in (1, 3, 2)}
-    pieces = [line] + [far[s] for s in (1, 2, 3)]
+    near = {s: lax.ppermute(in_x, DP, turns(s, 0)) for s in (1, 3, 2)}
+    line = jnp.concatenate([in_x, near[1], near[2], near[3]], axis=0)
     halo = 16
     tail = jnp.pad(
         tail.reshape(batch_count * (taps - 1), width),
         ((0, halo - batch_count * (taps - 1)), (0, 0)),
     )
-    tail, _ = lax.optimization_barrier((tail, line))
     flat = resid.reshape(rows, width)
     half_rows = jax.ShapeDtypeStruct((rows + halo, width // CS), BF)
     normed, mine, theirs = pl.pallas_call(
@@ -200,6 +257,16 @@
         tail,
         norm_gain.reshape(1, width),
     )
+    line, mine, theirs, in_z = lax.optimization_barrier((line, mine, theirs, in_z))
+    all_z = lax.all_gather(in_z, DP, axis=0, tiled=True)
+    behind, opposite, ahead = around(line, DP, lambda by: turns(by, 1))
+    share = width // zs
+    out_cut = [
+        lax.dynamic_slice_in_dim(out_w, lax.rem(zi + by, zs) * share, share, 1)
+        for by in range(zs)
+    ]
+    opposite, out_cut = lax.optimization_barrier((opposite, out_cut))
+    pieces = [line, behind, jnp.concatenate(opposite, axis=0), ahead]
     theirs = swap_cores(theirs)
     depth = width // CS // 4
     cut = [slice(s * depth, (s + 1) * depth) for s in range(4)]
@@ -300,33 +367,91 @@
         name="outputs",
     )(bc_raw, step3, du3, rate, start, z_gate)
 
-    share = width // zs
-
-    def out_share(by):
-        to = lax.rem(zi + by, zs) * share
-        return dot(gated, lax.dynamic_slice_in_dim(out_w, to, share, 1))
-
-    arrived = [lax.ppermute(out_share(s).astype(BF), "vocab", ring(zs, s)) for s in (1, 3, 2)]
-    mixer = out_share(0)
-    for piece in arrived:
-        mixer = mixer + piece.astype(F32)
+    def hops(by):
+        return ring(zs, by)
+
+    middle = rows // 2
+    far = dot(gated, out_cut[2]).astype(BF)
+    up = lax.ppermute(far[:middle], "vocab", hops(1))
+    down = lax.ppermute(far[middle:], "vocab", hops(3))
+    after = dot(gated, out_cut[1])
+    prior = dot(gated, out_cut[3])
     part = lax.dynamic_slice_in_dim(flat, zi * share, share, 1).astype(F32)
-    hidden_share = (part + mixer).astype(BF)
-    hidden = jnp.zeros((rows, width), BF)
-    for s in (0, 1, 3, 2):
-        piece = hidden_share if s == 0 else lax.ppermute(hidden_share, "vocab", ring(zs, s))
-        hidden = lax.dynamic_update_slice_in_dim(
-            hidden, piece, lax.rem(zi - s + zs, zs) * share, 1
-        )
-    final = rms_norm(hidden.astype(F32), final_gain, 1e-05).astype(BF)
-    logits = dot(final, all_head)
+    mixer = dot(gated, out_cut[0]) + part
+    up, mixer = lax.optimization_barrier((up, mixer))
+    up_low = lax.ppermute(after[middle:].astype(BF), "vocab", hops(1))
+    down_high = lax.ppermute(prior[:middle].astype(BF), "vocab", hops(3))
+    up_high = lax.ppermute(
+        (after[:middle] + up.astype(F32)).astype(BF), "vocab", hops(1)
+    )
+    down_low = lax.ppermute(
+        (prior[middle:] + down.astype(F32)).astype(BF), "vocab", hops(3)
+    )
+    upper = (mixer[:middle] + (up_high.astype(F32) + down_high.astype(F32))).astype(BF)
+    lower = (mixer[middle:] + (up_low.astype(F32) + down_low.astype(F32))).astype(BF)
+    hidden_share = jnp.concatenate([upper, lower], axis=0)
+
+    behind_upper = lax.ppermute(upper, "vocab", hops(1))
+    ahead_lower = lax.ppermute(lower, "vocab", hops(3))
+    behind_lower = lax.ppermute(lower, "vocab", hops(1))
+    ahead_upper = lax.ppermute(upper, "vocab", hops(3))
+    opposite_upper = lax.ppermute(behind_upper, "vocab", hops(1))
+    opposite_lower = lax.ppermute(ahead_lower, "vocab", hops(3))
     vocab_rows = head_w.shape[0]
-    local_ids = targets.reshape(rows) - zi * vocab_rows
-    entry_ids = lax.broadcasted_iota(jnp.int32, (rows, vocab_rows), 1)
-    picked = jnp.sum(jnp.where(entry_ids == local_ids[:, None], logits, 0.0), axis=-1)
-    top = jnp.max(logits, axis=-1)
-    exps = jnp.sum(jnp.exp(logits - top[:, None]), axis=-1)
-    stats = jnp.stack([top, exps, picked])
+    deep = 512
+    per = share // deep
+    gain = final_gain.reshape(1, width)
+
+    def blocks(*hops_back):
+        firsts = [lax.rem(zi - s + zs, zs) * per for s in hops_back]
+        return jnp.stack([first + i for first in firsts for i in range(per)])
+
+    def whole(*shape):
+        return pl.BlockSpec(shape, lambda j, order: (0,) * len(shape))
+
+    head_block = pl.BlockSpec((deep, vocab_rows), lambda j, order: (order[j], 0))
+    sums = [whole(rows, vocab_rows), whole(rows, 128)]
+    sums_shape = (
+        jax.ShapeDtypeStruct((rows, vocab_rows), F32),
+        jax.ShapeDtypeStruct((rows, 128), F32),
+    )
+
+    def logits_call(kernel, name, from_where, pieces, extra, last=False):
+        halves = [whole(middle, share)] * len(pieces)
+        weights = [whole(1, width), head_block]
+        extra_specs = [whole(*e.shape) for e in extra]
+        return pl.pallas_call(
+            kernel,
+            grid_spec=pltpu.PrefetchScalarGridSpec(
+                num_scalar_prefetch=1,
+                grid=(len(pieces) // 2 * per,),
+                in_specs=halves + weights + extra_specs,
+                out_specs=whole(rows, 128) if last else tuple(sums),
+                scratch_shapes=[pltpu.VMEM(s.shape, F32) for s in sums_shape] if last else [],
+            ),
+            out_shape=jax.ShapeDtypeStruct((rows, 128), F32) if last else sums_shape,
+            compiler_params=pltpu.CompilerParams(vmem_limit_bytes=48 << 20),
+            name=name,
+        )(blocks(*from_where), *pieces, gain, all_head, *extra)
+
+    acc = logits_call(own_kernel, "own_logits", (0,), (upper, lower), ())
+    acc = logits_call(
+        near_kernel,
+        "near_logits",
+        (1, 3),
+        (behind_upper, behind_lower, ahead_upper, ahead_lower),
+        acc,
+    )
+    local_ids = targets.reshape(rows, 1) - zi * vocab_rows
+    stats = logits_call(
+        last_kernel,
+        "last_logits",
+        (2,),
+        (opposite_upper, opposite_lower),
+        (*acc, local_ids),
+        True,
+    )
+    stats = stats[:, :3].T
     stats = lax.all_to_all(
         jnp.broadcast_to(stats[None], (zs, *stats.shape)), "vocab", 0, 0, tiled=True
     )

time: 263 us -> 216 us (0.82)
  waiting for transfers between devices: 117 us -> 53.1 us
  matrix products: 37.3 us -> 21.5 us
  Pallas kernels: 17.7 us -> 32.1 us
  starting transfers between devices: 50.9 us -> 62 us
  local copies, waits for them, and re-layouts: 15.4 us -> 22.1 us
    ppermute x12 -> x19, waiting for transfers between devices: 73.1 us -> 20.6 us  [the longest x1 4.98 us: body(): up_low = lax.ppermute(after[middle:].astype(BF), 'vocab', hops(1))]
    dot_general x15 -> x14, matrix products: 37.3 us -> 21.5 us  [dot(): return jnp.dot(a, b, preferred_element_type=F32)]
    pallas_call x0 -> x3, Pallas kernels: none -> 14.3 us  [logits_call(): pl.pallas_call(kernel, grid_spec=pltpu.PrefetchScalarGridSpec(num_scalar_...]
    ppermute x1, waiting for transfers between devices: 10.1 us -> 1.04 us  [body(): tail = lax.ppermute(resid[:, local_len - (taps - 1):, :], DP, order)]
    dynamic_slice x0 -> x1, local copies, waits for them, and re-layouts: none -> 7 us  [body(): lax.dynamic_slice_in_dim(out_w, lax.rem(zi + by, zs) * share, share, 1)]
    ppermute x12 -> x19, starting transfers between devices: 21.7 us -> 28.4 us  [the longest x3 5.88 us: body(): near = {s: lax.ppermute(in_x, DP, turns(s, 0)) for s in (1, 3, 2)}]
    ppermute x4, starting transfers between devices: 2.35 us -> 6.99 us  [swap_cores(): return lax.ppermute(array, 'dp_2', ring(CS, 1))]
    ppermute x3, waiting for transfers between devices: 11.5 us -> 8.18 us  [body(): low_sum = low_sum + lax.ppermute(low_sent, 'vocab', ring(zs, s)).astype(F32)]
  transfers between devices with their start and end apart: 25 -> 32, of which waited for: 17 -> 16; matrix products, arithmetic and copies ran while one was open for 15% -> 18% of each run, Pallas kernels for 7% -> 13%
where the time goes in v2:
time: 216 us; the launch traced here: 215 us
  starting transfers between devices  62 us (29%)
  waiting for transfers between devices  53.1 us (25%)
  Pallas kernels  32.1 us (15%)
  local copies, waits for them, and re-layouts  22.1 us (10%)
  matrix products  21.5 us (10%)
  between operations  17.5 us (8%)
  other arithmetic  6.53 us (3%)
    dot_general x14, matrix products, dot(): return jnp.dot(a, b, preferred_element_type=F32)  21.5 us
    pallas_call x3, Pallas kernels, logits_call(): pl.pallas_call(kernel, grid_spec=pltpu.PrefetchScalarGridSpec(num_scalar_...  14.3 us
    all_to_all x1, waiting for transfers between devices, body(): lax.all_to_all(jnp.broadcast_to(packed[None], (chips, *packed.shape)), CH...  9.08 us
    ppermute x3, waiting for transfers between devices, body(): low_sum = low_sum + lax.ppermute(low_sent, 'vocab', ring(zs, s)).astype(F32)  8.18 us
    unnamed x50, local copies, waits for them, and re-layouts  7.86 us
    pallas_call x1, Pallas kernels, body(): pl.pallas_call(lambda *refs: outputs_kernel(rows, local_len, nstate, *ref...  7.47 us
    all_to_all x1, starting transfers between devices, body(): lax.all_to_all(jnp.broadcast_to(masked, (peers, 1)), DP, 0, 0, tiled=True)  7.12 us
    dynamic_slice x1, local copies, waits for them, and re-layouts, body(): lax.dynamic_slice_in_dim(out_w, lax.rem(zi + by, zs) * share, share, 1)  7 us
  transfers between devices with their start and end apart: 32, of which 16 were waited for; matrix products, arithmetic and copies ran while one was open for 18% of the time, Pallas kernels for 13%

profile of v2, /device:TPU:1, one launch (start us, length us, event | category | flops | bytes accessed | tf_op | source)
XLA Modules:
  0.0 214.9 jit_solution(12816366877802221391)
XLA Ops:
  7.2 2.2 %collective-permute-start = (bf16[128,1024]{1,0:T(8,128)(2,1)}, bf16[128,1024]{1,0:T(8,128)(2,1)S(1)}, u32[]{:S(2)}, u32[]{:S(2)}) collective-permute-start(bf16[128,1024]{1,0:T(8,128)(2,1)} %param.19), channel_id=1, source_target_pairs={{0,8},{4,36},{8,16},{12,44},{16,24},{20,52},{24,0},{28,60},{32,40}... | collective-permute-start | bytes 786440 | tf_op jit(solution)/shard_map/ppermute | solution.py:237
  9.4 2.6 %collective-permute-start.1 = (bf16[128,1024]{1,0:T(8,128)(2,1)}, bf16[128,1024]{1,0:T(8,128)(2,1)S(1)}, u32[]{:S(2)}, u32[]{:S(2)}) collective-permute-start(bf16[128,1024]{1,0:T(8,128)(2,1)} %param.19), channel_id=1, source_target_pairs={{0,16},{4,68},{8,24},{12,76},{16,0},{20,84},{24,8},{28,92},{32,48}... | collective-permute-start | bytes 786440 | tf_op jit(solution)/shard_map/ppermute | solution.py:237
  14.0 3.5 %collective-permute-start.3 = (bf16[2,3,4096]{2,1,0:T(4,128)(2,1)S(1)}, bf16[2,3,4096]{2,1,0:T(4,128)(2,1)S(1)}, u32[]{:S(2)}, u32[]{:S(2)}) collective-permute-start(bf16[2,3,4096]{2,1,0:T(4,128)(2,1)S(1)} %slice.297), channel_id=1, source_target_pairs={{0,4},{4,8},{8,12},{12,16},{16,20},{20,24},{24,28},{28,32},{32,36}... | collective-permute-start | bytes 147464 | tf_op jit(solution)/shard_map/ppermute | solution.py:236
  19.6 3.4 %norm.1 = (bf16[256,4096]{1,0:T(8,128)(2,1)S(1)}, bf16[272,2048]{1,0:T(8,128)(2,1)S(1)}, bf16[272,2048]{1,0:T(8,128)(2,1)S(1)}) custom-call(s32[32]{0:T(128)S(1)} %stack.164.refs_0_, bf16[256,4096]{1,0:T(8,128)(2,1)} %bitcast.195, bf16[16,4096]{1,0:T(8,128)(2,1)S(1)} %pad.4.refs_2_, f32[1,4096]{1,0:T(1,128)S(1)} %bitcast.192), custom_call_target="tpu_custom_call" | custom-call | tf_op jit(solution)/shard_map/norm/pallas_call | solution.py:246
  23.0 1.3 copy-done.5
  26.3 2.5 %collective-permute-start.4 = (bf16[512,1024]{1,0:T(8,128)(2,1)S(1)}, bf16[512,1024]{1,0:T(8,128)(2,1)}, u32[]{:S(2)}, u32[]{:S(2)}) collective-permute-start(bf16[512,1024]{1,0:T(8,128)(2,1)S(1)} %pad_maximum_fusion), channel_id=1, source_target_pairs={{0,32},{4,12},{8,40},{12,20},{16,48},{20,28},{24,56},{28,4},{32,64... | collective-permute-start | bytes 3145736 | tf_op jit(solution)/shard_map/ppermute | solution.py:44
  31.5 7.0 %constant_dynamic-slice_fusion.3 = (bf16[1024,1024]{1,0:T(8,128)(2,1)}, bf16[1024,1024]{1,0:T(8,128)(2,1)}, bf16[1024,1024]{1,0:T(8,128)(2,1)}, bf16[1024,1024]{1,0:T(8,128)(2,1)}) fusion(bf16[1024,4096]{1,0:T(8,128)(2,1)} %param.29, s32[]{:T(128)S(6)} %select_n.268, s32[]{:T(128)S(6)} %select_n.266, s32[]{:T(128)S(6)} %select_n.265, s32[]{:T(128)S(6)} %select_n.267), kind=kLoop, calls=%fused_computation.158 | loop fusion | bytes 16777232 | tf_op jit(solution)/shard_map/dynamic_slice | solution.py:265
  39.0 3.4 %collective-permute-done.4 = bf16[512,1024]{1,0:T(8,128)(2,1)} collective-permute-done((bf16[512,1024]{1,0:T(8,128)(2,1)S(1)}, bf16[512,1024]{1,0:T(8,128)(2,1)}, u32[]{:S(2)}, u32[]{:S(2)}) %collective-permute-start.4) | collective-permute-done | bytes 1048608 | tf_op jit(solution)/shard_map/ppermute | solution.py:44
  45.1 2.6 %collective-permute-start.7 = (bf16[256,1024]{1,0:T(8,128)(2,1)S(1)}, bf16[256,1024]{1,0:T(8,128)(2,1)S(1)}, u32[]{:S(2)}, u32[]{:S(2)}) collective-permute-start(bf16[256,1024]{1,0:T(8,128)(2,1)S(1)} %slice.394), channel_id=1, source_target_pairs={{0,96},{4,28},{8,104},{12,4},{16,112},{20,12},{24,120},{28,20},{32... | collective-permute-start | bytes 1572872 | tf_op jit(solution)/shard_map/ppermute | solution.py:47
  47.6 1.8 fusion.18
  49.4 1.8 fusion.20
  51.2 4.3 %collective-permute-done.6 = bf16[256,1024]{1,0:T(8,128)(2,1)S(1)} collective-permute-done((bf16[256,1024]{1,0:T(8,128)(2,1)S(1)}, bf16[256,1024]{1,0:T(8,128)(2,1)S(1)}, u32[]{:S(2)}, u32[]{:S(2)}) %collective-permute-start.6) | collective-permute-done | bytes 524320 | tf_op jit(solution)/shard_map/ppermute | solution.py:46
  55.6 1.4 fusion.16
  57.1 1.4 fusion.4
  58.5 5.2 %collective-permute-start.9 = (bf16[272,1024]{1,0:T(8,128)(2,1)S(1)}, bf16[272,1024]{1,0:T(8,128)(2,1)S(1)}, u32[]{:S(2)}, u32[]{:S(2)}) collective-permute-start(bf16[272,1024]{1,0:T(8,128)(2,1)S(1)} %fusion.4), channel_id=1, source_target_pairs={{0,4},{4,0},{1,5},{5,1},{2,6},{6,2},{3,7},{7,3},{8,12},{12,8},{9,1... | collective-permute-start | bytes 1671176 | tf_op jit(solution)/shard_map/ppermute | solution.py:39
  63.7 1.7 convolution_add_fusion.2
  65.8 1.7 fusion.5
  69.8 1.7 collective-permute-start.10
  71.5 3.0 %collective-permute-start.11 = (bf16[256,288]{1,0:T(8,128)(2,1)S(1)}, bf16[256,288]{1,0:T(8,128)(2,1)S(1)}, u32[]{:S(2)}, u32[]{:S(2)}) collective-permute-start(bf16[256,288]{1,0:T(8,128)(2,1)S(1)} %convolution_convert_fusion.2), channel_id=1, source_target_pairs={{0,3},{1,0},{2,1},{3,2},{4,7},{5,4},{6,5},{7,6},{8,11},{9,8},{10,9... | collective-permute-start | bytes 442376 | tf_op jit(solution)/shard_map/ppermute | solution.py:289
  76.6 3.1 %collective-permute-done.10 = bf16[256,288]{1,0:T(8,128)(2,1)S(1)} collective-permute-done((bf16[256,288]{1,0:T(8,128)(2,1)S(1)}, bf16[256,288]{1,0:T(8,128)(2,1)S(1)}, u32[]{:S(2)}, u32[]{:S(2)}) %collective-permute-start.10) | collective-permute-done | bytes 147488 | tf_op jit(solution)/shard_map/ppermute | solution.py:289
  79.7 3.1 %collective-permute-done.11 = bf16[256,288]{1,0:T(8,128)(2,1)S(1)} collective-permute-done((bf16[256,288]{1,0:T(8,128)(2,1)S(1)}, bf16[256,288]{1,0:T(8,128)(2,1)S(1)}, u32[]{:S(2)}, u32[]{:S(2)}) %collective-permute-start.11) | collective-permute-done | bytes 147488 | tf_op jit(solution)/shard_map/ppermute | solution.py:289
  82.8 2.0 collective-permute-done.12
  86.6 6.9 %steps.1 = (f32[256,8,128]{2,1,0:T(8,128)S(1)}, f32[256,8,128]{2,1,0:T(8,128)S(1)}, f32[2,16,8,128]{3,2,1,0:T(8,128)S(1)}, f32[2,8,128]{2,1,0:T(8,128)S(1)}) custom-call(f32[8192]{0:T(1024)S(1)} %reshape.129.refs_0_, f32[256,256]{1,0:T(8,128)S(1)} %slice.406.refs_1_, f32[1,256]{1,0:T(1,128)S(1)} %bitcast.194, bf16[256,1024]{1,0:T(8,128)(2,1)S(1)} %copy-done, ...), custom_call_target="tpu_custom_call" | custom-call | tf_op jit(solution)/shard_map/steps/pallas_call | solution.py:298
  96.5 6.0 %all-to-all-start = ((bf16[16,2,10,8,128]{4,3,2,1,0:T(8,128)(2,1)}), bf16[16,2,10,8,128]{4,3,2,1,0:T(8,128)(2,1)S(1)}, u32[]{:S(2)}, u32[]{:S(2)}) async-start(bf16[16,2,10,8,128]{4,3,2,1,0:T(8,128)(2,1)} %broadcast_in_dim.20), calls=%async_computation | async-start | bytes 1310720 | tf_op jit(solution)/shard_map/all_to_all | solution.py:342
  102.6 6.5 %convolution_convert_fusion.refs_5_ = bf16[256,1024]{1,0:T(8,128)(2,1)S(1)} fusion(bf16[256,4096]{1,0:T(8,128)(2,1)} %copy-done.5, bf16[4096,1024]{1,0:T(8,128)(2,1)} %all-gather.3.cloned.1.call-done), kind=kOutput, calls=%fused_computation.10 | convolution fusion | flops 2147745792 | bytes 11010048 | tf_op jit(solution)/shard_map/dot_general | solution.py:66
  109.1 9.1 %all-to-all-done = bf16[16,2,10,8,128]{4,3,2,1,0:T(8,128)(2,1)S(1)} async-done(((bf16[16,2,10,8,128]{4,3,2,1,0:T(8,128)(2,1)}), bf16[16,2,10,8,128]{4,3,2,1,0:T(8,128)(2,1)S(1)}, u32[]{:S(2)}, u32[]{:S(2)}) %all-to-all-start) | async-done | bytes 655392 | tf_op jit(solution)/shard_map/all_to_all | solution.py:342
  120.5 7.5 %outputs.1 = bf16[256,1024]{1,0:T(8,128)(2,1)S(1)} custom-call(f32[8192]{0:T(1024)S(1)} %reshape.129.refs_0_, f32[256,8,128]{2,1,0:T(8,128)S(1)} %get-tuple-element.36.refs_1_, f32[256,8,128]{2,1,0:T(8,128)S(1)} %get-tuple-element.37.refs_2_, f32[16,8,128]{2,1,0:T(8,128)S(1)} %bitcast.187, f32[2,16,8,128]{3,2,1,0:T(8,128)S(1)} %pad_maximum_fusion.2.refs_4_, ...), custom_call_target="tpu_custom_call" | custom-call | tf_op jit(solution)/shard_map/outputs/pallas_call | solution.py:360
  128.7 2.6 %collective-permute-start.19 = (bf16[128,1024]{1,0:T(8,128)(2,1)S(1)}, bf16[128,1024]{1,0:T(8,128)(2,1)S(1)}, u32[]{:S(2)}, u32[]{:S(2)}) collective-permute-start(bf16[128,1024]{1,0:T(8,128)(2,1)S(1)} %get-tuple-element.90), channel_id=1, source_target_pairs={{0,3},{1,0},{2,1},{3,2},{4,7},{5,4},{6,5},{7,6},{8,11},{9,8},{10,9... | collective-permute-start | bytes 786440 | tf_op jit(solution)/shard_map/ppermute | solution.py:376
  133.8 1.9 collective-permute-start.17
  135.6 1.8 convolution_add_fusion.3
  137.5 2.8 %collective-permute-start.20 = (bf16[128,1024]{1,0:T(8,128)(2,1)S(1)}, bf16[128,1024]{1,0:T(8,128)(2,1)S(1)}, u32[]{:S(2)}, u32[]{:S(2)}) collective-permute-start(bf16[128,1024]{1,0:T(8,128)(2,1)S(1)} %fusion.13), channel_id=1, source_target_pairs={{0,3},{1,0},{2,1},{3,2},{4,7},{5,4},{6,5},{7,6},{8,11},{9,8},{10,9... | collective-permute-start | bytes 786440 | tf_op jit(solution)/shard_map/ppermute | solution.py:387
  140.5 5.0 %collective-permute-done.18 = bf16[128,1024]{1,0:T(8,128)(2,1)S(1)} collective-permute-done((bf16[128,1024]{1,0:T(8,128)(2,1)S(1)}, bf16[128,1024]{1,0:T(8,128)(2,1)S(1)}, u32[]{:S(2)}, u32[]{:S(2)}) %collective-permute-start.18) | collective-permute-done | bytes 262176 | tf_op jit(solution)/shard_map/ppermute | solution.py:382
  145.4 2.5 %collective-permute-done.20 = bf16[128,1024]{1,0:T(8,128)(2,1)S(1)} collective-permute-done((bf16[128,1024]{1,0:T(8,128)(2,1)S(1)}, bf16[128,1024]{1,0:T(8,128)(2,1)S(1)}, u32[]{:S(2)}, u32[]{:S(2)}) %collective-permute-start.20) | collective-permute-done | bytes 262176 | tf_op jit(solution)/shard_map/ppermute | solution.py:387
  147.9 3.1 %collective-permute-done.16 = bf16[128,1024]{1,0:T(8,128)(2,1)S(1)} collective-permute-done((bf16[128,1024]{1,0:T(8,128)(2,1)S(1)}, bf16[128,1024]{1,0:T(8,128)(2,1)S(1)}, u32[]{:S(2)}, u32[]{:S(2)}) %collective-permute-start.16) | collective-permute-done | bytes 262176 | tf_op jit(solution)/shard_map/ppermute | solution.py:384
  151.6 2.7 %collective-permute-start.23 = (bf16[128,1024]{1,0:T(8,128)(2,1)S(1)}, bf16[128,1024]{1,0:T(8,128)(2,1)S(1)}, u32[]{:S(2)}, u32[]{:S(2)}) collective-permute-start(bf16[128,1024]{1,0:T(8,128)(2,1)S(1)} %get-tuple-element.73.lower), channel_id=1, source_target_pairs={{0,3},{1,0},{2,1},{3,2},{4,7},{5,4},{6,5},{7,6},{8,11},{9,8},{10,9... | collective-permute-start | bytes 786440 | tf_op jit(solution)/shard_map/ppermute | solution.py:395
  154.4 2.7 %collective-permute-start.26 = (bf16[128,1024]{1,0:T(8,128)(2,1)S(1)}, bf16[128,1024]{1,0:T(8,128)(2,1)S(1)}, u32[]{:S(2)}, u32[]{:S(2)}) collective-permute-start(bf16[128,1024]{1,0:T(8,128)(2,1)S(1)} %get-tuple-element.72.upper), channel_id=1, source_target_pairs={{0,3},{1,0},{2,1},{3,2},{4,7},{5,4},{6,5},{7,6},{8,11},{9,8},{10,9... | collective-permute-start | bytes 786440 | tf_op jit(solution)/shard_map/ppermute | solution.py:397
  157.0 2.3 %collective-permute-done.21.a = bf16[128,1024]{1,0:T(8,128)(2,1)S(1)} collective-permute-done((bf16[128,1024]{1,0:T(8,128)(2,1)S(1)}, bf16[128,1024]{1,0:T(8,128)(2,1)S(1)}, u32[]{:S(2)}, u32[]{:S(2)}) %collective-permute-start.21) | collective-permute-done | bytes 262176 | tf_op jit(solution)/shard_map/ppermute | solution.py:394
  159.3 2.7 %collective-permute-start.24 = (bf16[128,1024]{1,0:T(8,128)(2,1)S(1)}, bf16[128,1024]{1,0:T(8,128)(2,1)S(1)}, u32[]{:S(2)}, u32[]{:S(2)}) collective-permute-start(bf16[128,1024]{1,0:T(8,128)(2,1)S(1)} %collective-permute-done.23.d), channel_id=1, source_target_pairs={{0,3},{1,0},{2,1},{3,2},{4,7},{5,4},{6,5},{7,6},{8,11},{9,8},{10,9... | collective-permute-start | bytes 786440 | tf_op jit(solution)/shard_map/ppermute | solution.py:399
  163.0 2.0 all-gather.5.cloned.1.call-done.head
  164.9 3.6 %own_logits.1 = (f32[256,2048]{1,0:T(8,128)S(1)}, f32[256,128]{1,0:T(8,128)S(1)}) custom-call(s32[2]{0:T(128)S(1)} %pad_add_fusion.2.order, bf16[128,1024]{1,0:T(8,128)(2,1)S(1)} %get-tuple-element.72.upper, bf16[128,1024]{1,0:T(8,128)(2,1)S(1)} %get-tuple-element.73.lower, f32[1,4096]{1,0:T(1,128)S(1)} %bitcast.188, ...), custom_call_target="tpu_custom_call" | custom-call | tf_op jit(solution)/shard_map/own_logits/pallas_call | solution.py:423
  168.6 6.1 %near_logits.1 = (f32[256,2048]{1,0:T(8,128)S(1)}, f32[256,128]{1,0:T(8,128)S(1)}) custom-call(s32[4]{0:T(128)S(1)} %pad_add_fusion.1.order, bf16[128,1024]{1,0:T(8,128)(2,1)S(1)} %collective-permute-done.21.a, bf16[128,1024]{1,0:T(8,128)(2,1)S(1)} %collective-permute-done.25.b, bf16[128,1024]{1,0:T(8,128)(2,1)S(1)} %collective-permute-done.26.c, ...), custom_call_target="tpu_custom_call" | custom-call | tf_op jit(solution)/shard_map/near_logits/pallas_call | solution.py:423
  174.7 4.6 %last_logits.1 = f32[256,128]{1,0:T(8,128)S(1)} custom-call(s32[2]{0:T(128)S(1)} %pad_add_fusion.order, bf16[128,1024]{1,0:T(8,128)(2,1)S(1)} %collective-permute-done.22.upper, bf16[128,1024]{1,0:T(8,128)(2,1)S(1)} %collective-permute-done.24.lower, f32[1,4096]{1,0:T(1,128)S(1)} %bitcast.190, bf16[4096,2048]{1,0:T(8,128)(2,1)} %all-gather.5.cloned.1.call-done.head, ...), custom_call_target="tpu_custom_call" | custom-call | tf_op jit(solution)/shard_map/last_logits/pallas_call | solution.py:423
  180.0 4.1 %all-to-all-start.1 = ((f32[4,3,256]{2,1,0:T(4,128)}), f32[4,3,256]{2,1,0:T(4,128)S(1)}, u32[]{:S(2)}, u32[]{:S(2)}) async-start(f32[4,3,256]{2,1,0:T(4,128)} %broadcast_in_dim.22), calls=%async_computation.1 | async-start | bytes 32768 | tf_op jit(solution)/shard_map/all_to_all | solution.py:455
  184.2 4.2 %all-to-all-done.1 = f32[4,3,256]{2,1,0:T(4,128)S(1)} async-done(((f32[4,3,256]{2,1,0:T(4,128)}), f32[4,3,256]{2,1,0:T(4,128)S(1)}, u32[]{:S(2)}, u32[]{:S(2)}) %all-to-all-start.1) | async-done | bytes 12320 | tf_op jit(solution)/shard_map/all_to_all | solution.py:455
  188.4 1.2 fusion.70
  189.6 1.3 broadcast_in_dim.24
  190.9 7.1 %all-to-all-start.2 = ((f32[32,1,1]{2,1,0:T(1,128)}), f32[32,1,1]{2,1,0:T(1,128)S(1)}, u32[]{:S(2)}, u32[]{:S(2)}) async-start(f32[32,1,1]{2,1,0:T(1,128)} %broadcast_in_dim.24), calls=%async_computation.2 | async-start | bytes 32768 | tf_op jit(solution)/shard_map/all_to_all | solution.py:467
  198.8 6.1 %all-to-all-done.2 = f32[32,1,1]{2,1,0:T(1,128)S(1)} async-done(((f32[32,1,1]{2,1,0:T(1,128)}), f32[32,1,1]{2,1,0:T(1,128)S(1)}, u32[]{:S(2)}, u32[]{:S(2)}) %all-to-all-start.2) | async-done | bytes 160 | tf_op jit(solution)/shard_map/all_to_all | solution.py:467
  (151 shorter events, 30.7 us)
Async XLA Ops:
  7.2 77.8 %all-gather.3.cloned.1.call-start = ((), (), s32[]{:S(2)}) async-start(), calls=%async_computation.3 | async-start | bytes 8650752 | tf_op jit(solution)/shard_map/all_gather | solution.py:261
  7.2 17.1 %collective-permute-start = (bf16[128,1024]{1,0:T(8,128)(2,1)}, bf16[128,1024]{1,0:T(8,128)(2,1)S(1)}, u32[]{:S(2)}, u32[]{:S(2)}) collective-permute-start(bf16[128,1024]{1,0:T(8,128)(2,1)} %param.19), channel_id=1, source_target_pairs={{0,8},{4,36},{8,16},{12,44},{16,24},{20,52},{24,0},{28,60},{32,40}... | collective-permute-start | bytes 786440 | tf_op jit(solution)/shard_map/ppermute | solution.py:237
  9.4 14.9 %collective-permute-start.1 = (bf16[128,1024]{1,0:T(8,128)(2,1)}, bf16[128,1024]{1,0:T(8,128)(2,1)S(1)}, u32[]{:S(2)}, u32[]{:S(2)}) collective-permute-start(bf16[128,1024]{1,0:T(8,128)(2,1)} %param.19), channel_id=1, source_target_pairs={{0,16},{4,68},{8,24},{12,76},{16,0},{20,84},{24,8},{28,92},{32,48}... | collective-permute-start | bytes 786440 | tf_op jit(solution)/shard_map/ppermute | solution.py:237
  12.0 13.0 %collective-permute-start.2 = (bf16[128,1024]{1,0:T(8,128)(2,1)}, bf16[128,1024]{1,0:T(8,128)(2,1)}, u32[]{:S(2)}, u32[]{:S(2)}) collective-permute-start(bf16[128,1024]{1,0:T(8,128)(2,1)} %param.19), channel_id=1, source_target_pairs={{0,24},{4,100},{8,0},{12,108},{16,8},{20,116},{24,16},{28,124},{32... | collective-permute-start | bytes 786440 | tf_op jit(solution)/shard_map/ppermute | solution.py:237
  14.0 4.8 %collective-permute-start.3 = (bf16[2,3,4096]{2,1,0:T(4,128)(2,1)S(1)}, bf16[2,3,4096]{2,1,0:T(4,128)(2,1)S(1)}, u32[]{:S(2)}, u32[]{:S(2)}) collective-permute-start(bf16[2,3,4096]{2,1,0:T(4,128)(2,1)S(1)} %slice.297), channel_id=1, source_target_pairs={{0,4},{4,8},{8,12},{12,16},{16,20},{20,24},{24,28},{28,32},{32,36}... | collective-permute-start | bytes 147464 | tf_op jit(solution)/shard_map/ppermute | solution.py:236
  18.9 0.7 copy-start.2
  19.6 5.5 %copy-start.12 = (bf16[128,1024]{1,0:T(8,128)(2,1)S(1)}, bf16[128,1024]{1,0:T(8,128)(2,1)}, u32[]{:S(2)}) copy-start(bf16[128,1024]{1,0:T(8,128)(2,1)} %param.19) | copy-start | bytes 786436
  23.0 1.3 copy-start.5
  24.3 6.6 %copy-start.15 = (f32[4,1024]{1,0:T(4,128)S(1)}, f32[4,1024]{1,0:T(4,128)}, u32[]{:S(2)}) copy-start(f32[4,1024]{1,0:T(4,128)} %param.21) | copy-start | bytes 49156
  24.3 0.7 copy-start.13
  26.2 138.7 %all-gather.5.cloned.1.call-start = ((), (), s32[]{:S(2)}) async-start(), calls=%async_computation.4 | async-start | bytes 17301504 | tf_op jit(solution)/shard_map/all_gather | solution.py:291
  26.2 21.4 %collective-permute-start.8 = (bf16[272,2048]{1,0:T(8,128)(2,1)S(1)}, bf16[272,2048]{1,0:T(8,128)(2,1)}, u32[]{:S(2)}, u32[]{:S(2)}) collective-permute-start(bf16[272,2048]{1,0:T(8,128)(2,1)S(1)} %get-tuple-element.35), channel_id=1, source_target_pairs={{0,4},{4,0},{1,5},{5,1},{2,6},{6,2},{3,7},{7,3},{8,12},{12,8},{9,1... | collective-permute-start | bytes 3342344 | tf_op jit(solution)/shard_map/ppermute | solution.py:39
  26.3 16.0 %collective-permute-start.4 = (bf16[512,1024]{1,0:T(8,128)(2,1)S(1)}, bf16[512,1024]{1,0:T(8,128)(2,1)}, u32[]{:S(2)}, u32[]{:S(2)}) collective-permute-start(bf16[512,1024]{1,0:T(8,128)(2,1)S(1)} %pad_maximum_fusion), channel_id=1, source_target_pairs={{0,32},{4,12},{8,40},{12,20},{16,48},{20,28},{24,56},{28,4},{32,64... | collective-permute-start | bytes 3145736 | tf_op jit(solution)/shard_map/ppermute | solution.py:44
  28.8 15.2 %collective-permute-start.5 = (bf16[512,1024]{1,0:T(8,128)(2,1)S(1)}, bf16[512,1024]{1,0:T(8,128)(2,1)}, u32[]{:S(2)}, u32[]{:S(2)}) collective-permute-start(bf16[512,1024]{1,0:T(8,128)(2,1)S(1)} %pad_maximum_fusion), channel_id=1, source_target_pairs={{0,96},{4,28},{8,104},{12,4},{16,112},{20,12},{24,120},{28,20},{32... | collective-permute-start | bytes 3145736 | tf_op jit(solution)/shard_map/ppermute | solution.py:45
  43.4 12.1 %collective-permute-start.6 = (bf16[256,1024]{1,0:T(8,128)(2,1)S(1)}, bf16[256,1024]{1,0:T(8,128)(2,1)S(1)}, u32[]{:S(2)}, u32[]{:S(2)}) collective-permute-start(bf16[256,1024]{1,0:T(8,128)(2,1)S(1)} %slice.393), channel_id=1, source_target_pairs={{0,32},{4,12},{8,40},{12,20},{16,48},{20,28},{24,56},{28,4},{32,64... | collective-permute-start | bytes 1572872 | tf_op jit(solution)/shard_map/ppermute | solution.py:46
  45.1 10.5 %collective-permute-start.7 = (bf16[256,1024]{1,0:T(8,128)(2,1)S(1)}, bf16[256,1024]{1,0:T(8,128)(2,1)S(1)}, u32[]{:S(2)}, u32[]{:S(2)}) collective-permute-start(bf16[256,1024]{1,0:T(8,128)(2,1)S(1)} %slice.394), channel_id=1, source_target_pairs={{0,96},{4,28},{8,104},{12,4},{16,112},{20,12},{24,120},{28,20},{32... | collective-permute-start | bytes 1572872 | tf_op jit(solution)/shard_map/ppermute | solution.py:47
  58.5 7.3 %collective-permute-start.9 = (bf16[272,1024]{1,0:T(8,128)(2,1)S(1)}, bf16[272,1024]{1,0:T(8,128)(2,1)S(1)}, u32[]{:S(2)}, u32[]{:S(2)}) collective-permute-start(bf16[272,1024]{1,0:T(8,128)(2,1)S(1)} %fusion.4), channel_id=1, source_target_pairs={{0,4},{4,0},{1,5},{5,1},{2,6},{6,2},{3,7},{7,3},{8,12},{12,8},{9,1... | collective-permute-start | bytes 1671176 | tf_op jit(solution)/shard_map/ppermute | solution.py:39
  68.3 1.1 copy-start.11
  69.0 6.6 %copy-start.10 = (bf16[2048,128]{1,0:T(8,128)(2,1)S(1)}, bf16[2048,128]{1,0:T(8,128)(2,1)}, u32[]{:S(2)}) copy-start(bf16[2048,128]{1,0:T(8,128)(2,1)} %param.31) | copy-start | bytes 1572868
  69.8 9.9 %collective-permute-start.10 = (bf16[256,288]{1,0:T(8,128)(2,1)S(1)}, bf16[256,288]{1,0:T(8,128)(2,1)S(1)}, u32[]{:S(2)}, u32[]{:S(2)}) collective-permute-start(bf16[256,288]{1,0:T(8,128)(2,1)S(1)} %convolution_convert_fusion.2), channel_id=1, source_target_pairs={{0,1},{1,2},{2,3},{3,0},{4,5},{5,6},{6,7},{7,4},{8,9},{9,10},{10,1... | collective-permute-start | bytes 442376 | tf_op jit(solution)/shard_map/ppermute | solution.py:289
  71.5 11.3 %collective-permute-start.11 = (bf16[256,288]{1,0:T(8,128)(2,1)S(1)}, bf16[256,288]{1,0:T(8,128)(2,1)S(1)}, u32[]{:S(2)}, u32[]{:S(2)}) collective-permute-start(bf16[256,288]{1,0:T(8,128)(2,1)S(1)} %convolution_convert_fusion.2), channel_id=1, source_target_pairs={{0,3},{1,0},{2,1},{3,2},{4,7},{5,4},{6,5},{7,6},{8,11},{9,8},{10,9... | collective-permute-start | bytes 442376 | tf_op jit(solution)/shard_map/ppermute | solution.py:289
  74.5 10.3 %collective-permute-start.12 = (bf16[256,288]{1,0:T(8,128)(2,1)S(1)}, bf16[256,288]{1,0:T(8,128)(2,1)S(1)}, u32[]{:S(2)}, u32[]{:S(2)}) collective-permute-start(bf16[256,288]{1,0:T(8,128)(2,1)S(1)} %convolution_convert_fusion.2), channel_id=1, source_target_pairs={{0,2},{1,3},{2,0},{3,1},{4,6},{5,7},{6,4},{7,5},{8,10},{9,11},{10,... | collective-permute-start | bytes 442376 | tf_op jit(solution)/shard_map/ppermute | solution.py:289
  76.6 8.4 %copy-start.14 = (f32[1024,16]{0,1:T(8,128)S(1)}, f32[1024,16]{0,1:T(8,128)}, u32[]{:S(2)}) copy-start(f32[1024,16]{0,1:T(8,128)} %param.28) | copy-start | bytes 196612
  85.6 1.0 copy-start
  93.6 1.9 collective-permute-start.13
  96.5 21.6 %all-to-all-start = ((bf16[16,2,10,8,128]{4,3,2,1,0:T(8,128)(2,1)}), bf16[16,2,10,8,128]{4,3,2,1,0:T(8,128)(2,1)S(1)}, u32[]{:S(2)}, u32[]{:S(2)}) async-start(bf16[16,2,10,8,128]{4,3,2,1,0:T(8,128)(2,1)} %broadcast_in_dim.20), calls=%async_computation | async-start | bytes 1310720 | tf_op jit(solution)/shard_map/all_to_all | solution.py:342
  118.7 1.7 collective-permute-start.14
  120.4 7.5 %copy-start.9 = (bf16[1024,1024]{1,0:T(8,128)(2,1)S(1)}, bf16[1024,1024]{1,0:T(8,128)(2,1)}, u32[]{:S(2)}) copy-start(bf16[1024,1024]{1,0:T(8,128)(2,1)} %get-tuple-element.44) | copy-start | bytes 6291460
  127.9 3.4 %copy-start.7 = (bf16[1024,1024]{1,0:T(8,128)(2,1)S(1)}, bf16[1024,1024]{1,0:T(8,128)(2,1)}, u32[]{:S(2)}) copy-start(bf16[1024,1024]{1,0:T(8,128)(2,1)} %get-tuple-element.47) | copy-start | bytes 6291460
  128.7 8.7 %collective-permute-start.19 = (bf16[128,1024]{1,0:T(8,128)(2,1)S(1)}, bf16[128,1024]{1,0:T(8,128)(2,1)S(1)}, u32[]{:S(2)}, u32[]{:S(2)}) collective-permute-start(bf16[128,1024]{1,0:T(8,128)(2,1)S(1)} %get-tuple-element.90), channel_id=1, source_target_pairs={{0,3},{1,0},{2,1},{3,2},{4,7},{5,4},{6,5},{7,6},{8,11},{9,8},{10,9... | collective-permute-start | bytes 786440 | tf_op jit(solution)/shard_map/ppermute | solution.py:376
  131.3 1.7 copy-start.6
  131.3 9.0 %collective-permute-start.15 = (bf16[128,1024]{1,0:T(8,128)(2,1)S(1)}, bf16[128,1024]{1,0:T(8,128)(2,1)S(1)}, u32[]{:S(2)}, u32[]{:S(2)}) collective-permute-start(bf16[128,1024]{1,0:T(8,128)(2,1)S(1)} %get-tuple-element.89), channel_id=1, source_target_pairs={{0,1},{1,2},{2,3},{3,0},{4,5},{5,6},{6,7},{7,4},{8,9},{9,10},{10,1... | collective-permute-start | bytes 786440 | tf_op jit(solution)/shard_map/ppermute | solution.py:375
  132.0 3.6 %copy-start.8 = (bf16[1024,1024]{1,0:T(8,128)(2,1)S(1)}, bf16[1024,1024]{1,0:T(8,128)(2,1)}, u32[]{:S(2)}) copy-start(bf16[1024,1024]{1,0:T(8,128)(2,1)} %get-tuple-element.45) | copy-start | bytes 6291460
  132.0 13.4 %collective-permute-start.18 = (bf16[128,1024]{1,0:T(8,128)(2,1)S(1)}, bf16[128,1024]{1,0:T(8,128)(2,1)S(1)}, u32[]{:S(2)}, u32[]{:S(2)}) collective-permute-start(bf16[128,1024]{1,0:T(8,128)(2,1)S(1)} %slice.673), channel_id=1, source_target_pairs={{0,1},{1,2},{2,3},{3,0},{4,5},{5,6},{6,7},{7,4},{8,9},{9,10},{10,1... | collective-permute-start | bytes 786440 | tf_op jit(solution)/shard_map/ppermute | solution.py:382
  133.8 11.7 %collective-permute-start.17 = (bf16[128,1024]{1,0:T(8,128)(2,1)S(1)}, bf16[128,1024]{1,0:T(8,128)(2,1)S(1)}, u32[]{:S(2)}, u32[]{:S(2)}) collective-permute-start(bf16[128,1024]{1,0:T(8,128)(2,1)S(1)} %slice.674), channel_id=1, source_target_pairs={{0,3},{1,0},{2,1},{3,2},{4,7},{5,4},{6,5},{7,6},{8,11},{9,8},{10,9... | collective-permute-start | bytes 786440 | tf_op jit(solution)/shard_map/ppermute | solution.py:383
  137.5 10.4 %collective-permute-start.20 = (bf16[128,1024]{1,0:T(8,128)(2,1)S(1)}, bf16[128,1024]{1,0:T(8,128)(2,1)S(1)}, u32[]{:S(2)}, u32[]{:S(2)}) collective-permute-start(bf16[128,1024]{1,0:T(8,128)(2,1)S(1)} %fusion.13), channel_id=1, source_target_pairs={{0,3},{1,0},{2,1},{3,2},{4,7},{5,4},{6,5},{7,6},{8,11},{9,8},{10,9... | collective-permute-start | bytes 786440 | tf_op jit(solution)/shard_map/ppermute | solution.py:387
  140.3 10.7 %collective-permute-start.16 = (bf16[128,1024]{1,0:T(8,128)(2,1)S(1)}, bf16[128,1024]{1,0:T(8,128)(2,1)S(1)}, u32[]{:S(2)}, u32[]{:S(2)}) collective-permute-start(bf16[128,1024]{1,0:T(8,128)(2,1)S(1)} %fusion.14), channel_id=1, source_target_pairs={{0,1},{1,2},{2,3},{3,0},{4,5},{5,6},{6,7},{7,4},{8,9},{9,10},{10,1... | collective-permute-start | bytes 786440 | tf_op jit(solution)/shard_map/ppermute | solution.py:384
  140.4 13.9 %copy-start.21 = (s32[2,128]{1,0:T(2,128)S(1)}, s32[2,128]{1,0:T(2,128)}, u32[]{:S(2)}) copy-start(s32[2,128]{1,0:T(2,128)} %param.32) | copy-start | bytes 3076
  140.4 21.9 %copy-start.22 = (s32[2]{0:T(128)S(1)}, s32[2]{0:T(128)}, u32[]{:S(2)}) copy-start(s32[2]{0:T(128)} %param.33) | copy-start | bytes 28
  140.4 24.5 %copy-start.1 = (f32[4096]{0:T(1024)S(1)}, f32[4096]{0:T(1024)}, u32[]{:S(2)}) copy-start(f32[4096]{0:T(1024)} %param.30) | copy-start | bytes 49156
  151.3 8.0 %collective-permute-start.21 = (bf16[128,1024]{1,0:T(8,128)(2,1)S(1)}, bf16[128,1024]{1,0:T(8,128)(2,1)S(1)}, u32[]{:S(2)}, u32[]{:S(2)}) collective-permute-start(bf16[128,1024]{1,0:T(8,128)(2,1)S(1)} %get-tuple-element.72.upper), channel_id=1, source_target_pairs={{0,1},{1,2},{2,3},{3,0},{4,5},{5,6},{6,7},{7,4},{8,9},{9,10},{10,1... | collective-permute-start | bytes 786440 | tf_op jit(solution)/shard_map/ppermute | solution.py:394
  151.6 7.7 %collective-permute-start.23 = (bf16[128,1024]{1,0:T(8,128)(2,1)S(1)}, bf16[128,1024]{1,0:T(8,128)(2,1)S(1)}, u32[]{:S(2)}, u32[]{:S(2)}) collective-permute-start(bf16[128,1024]{1,0:T(8,128)(2,1)S(1)} %get-tuple-element.73.lower), channel_id=1, source_target_pairs={{0,3},{1,0},{2,1},{3,2},{4,7},{5,4},{6,5},{7,6},{8,11},{9,8},{10,9... | collective-permute-start | bytes 786440 | tf_op jit(solution)/shard_map/ppermute | solution.py:395
  154.3 14.2 %collective-permute-start.25 = (bf16[128,1024]{1,0:T(8,128)(2,1)S(1)}, bf16[128,1024]{1,0:T(8,128)(2,1)S(1)}, u32[]{:S(2)}, u32[]{:S(2)}) collective-permute-start(bf16[128,1024]{1,0:T(8,128)(2,1)S(1)} %get-tuple-element.73.lower), channel_id=1, source_target_pairs={{0,1},{1,2},{2,3},{3,0},{4,5},{5,6},{6,7},{7,4},{8,9},{9,10},{10,1... | collective-permute-start | bytes 786440 | tf_op jit(solution)/shard_map/ppermute | solution.py:396
  154.4 14.2 %collective-permute-start.26 = (bf16[128,1024]{1,0:T(8,128)(2,1)S(1)}, bf16[128,1024]{1,0:T(8,128)(2,1)S(1)}, u32[]{:S(2)}, u32[]{:S(2)}) collective-permute-start(bf16[128,1024]{1,0:T(8,128)(2,1)S(1)} %get-tuple-element.72.upper), channel_id=1, source_target_pairs={{0,3},{1,0},{2,1},{3,2},{4,7},{5,4},{6,5},{7,6},{8,11},{9,8},{10,9... | collective-permute-start | bytes 786440 | tf_op jit(solution)/shard_map/ppermute | solution.py:397
  159.3 15.4 %collective-permute-start.22 = (bf16[128,1024]{1,0:T(8,128)(2,1)S(1)}, bf16[128,1024]{1,0:T(8,128)(2,1)S(1)}, u32[]{:S(2)}, u32[]{:S(2)}) collective-permute-start(bf16[128,1024]{1,0:T(8,128)(2,1)S(1)} %collective-permute-done.21.a), channel_id=1, source_target_pairs={{0,1},{1,2},{2,3},{3,0},{4,5},{5,6},{6,7},{7,4},{8,9},{9,10},{10,1... | collective-permute-start | bytes 786440 | tf_op jit(solution)/shard_map/ppermute | solution.py:398
  159.3 15.4 %collective-permute-start.24 = (bf16[128,1024]{1,0:T(8,128)(2,1)S(1)}, bf16[128,1024]{1,0:T(8,128)(2,1)S(1)}, u32[]{:S(2)}, u32[]{:S(2)}) collective-permute-start(bf16[128,1024]{1,0:T(8,128)(2,1)S(1)} %collective-permute-done.23.d), channel_id=1, source_target_pairs={{0,3},{1,0},{2,1},{3,2},{4,7},{5,4},{6,5},{7,6},{8,11},{9,8},{10,9... | collective-permute-start | bytes 786440 | tf_op jit(solution)/shard_map/ppermute | solution.py:399
  180.0 8.4 %all-to-all-start.1 = ((f32[4,3,256]{2,1,0:T(4,128)}), f32[4,3,256]{2,1,0:T(4,128)S(1)}, u32[]{:S(2)}, u32[]{:S(2)}) async-start(f32[4,3,256]{2,1,0:T(4,128)} %broadcast_in_dim.22), calls=%async_computation.1 | async-start | bytes 32768 | tf_op jit(solution)/shard_map/all_to_all | solution.py:455
  190.9 14.1 %all-to-all-start.2 = ((f32[32,1,1]{2,1,0:T(1,128)}), f32[32,1,1]{2,1,0:T(1,128)S(1)}, u32[]{:S(2)}, u32[]{:S(2)}) async-start(f32[32,1,1]{2,1,0:T(1,128)} %broadcast_in_dim.24), calls=%async_computation.2 | async-start | bytes 32768 | tf_op jit(solution)/shard_map/all_to_all | solution.py:467
  (7 other events, 4.8 us)
Sparse Core Ops, SparseCore 0:
  26.3 57.7 all-gather.2
  86.9 77.9 all-gather.4

commit v3 on v2

--- a/solution.py
+++ b/solution.py
@@ -37,15 +37,6 @@
 
 def swap_cores(array):
     return lax.ppermute(array, "dp_2", ring(CS, 1))
-
-
-def around(array, axis, hops):
-    middle = array.shape[0] // 2
-    behind = lax.ppermute(array, axis, hops(1))
-    ahead = lax.ppermute(array, axis, hops(3))
-    first = lax.ppermute(behind[:middle], axis, hops(1))
-    second = lax.ppermute(ahead[middle:], axis, hops(3))
-    return behind, (first, second), ahead
 
 
 def blocks_in_order(y, x, core):
@@ -105,7 +96,7 @@
 
     zero = jnp.zeros(step3.shape[1:], F32)
     state, sums = lax.fori_loop(
-        0, length, advance, ((zero,) * (batches * nstate), (zero,) * batches), unroll=2
+        0, length, advance, ((zero,) * (batches * nstate), (zero,) * batches), unroll=4
     )
     for b in range(batches):
         total[b] = sums[b]
@@ -131,7 +122,7 @@
         return tuple(state)
 
     state = tuple(start[b, n] for b in range(batches) for n in range(nstate))
-    lax.fori_loop(0, length, advance, state, unroll=2)
+    lax.fori_loop(0, length, advance, state, unroll=4)
     for j in range(y3.shape[1]):
         gate = z[:, j * 128 : (j + 1) * 128].astype(F32)
         gate = gate / (1.0 + jnp.exp(-gate))
@@ -168,12 +159,8 @@
                 squares[...] = part
 
 
-def own_kernel(order, upper, lower, gain, head, acc, squares):
-    add_blocks((upper, lower), order, gain, head, None, acc, squares)
-
-
-def near_kernel(order, a, b, c, d, gain, head, acc_in, squares_in, acc, squares):
-    add_blocks((a, b, c, d), order, gain, head, (acc_in, squares_in), acc, squares)
+def near_kernel(order, a, b, c, d, e, f, gain, head, acc, squares):
+    add_blocks((a, b, c, d, e, f), order, gain, head, None, acc, squares)
 
 
 def last_kernel(order, upper, lower, gain, head, acc_in, squares_in, ids, stats, acc, squares):
@@ -193,6 +180,35 @@
             exps = jnp.sum(jnp.exp(logits - top), axis=-1, keepdims=True)
             picked = jnp.sum(jnp.where(entry == ids[cut], logits, 0.0), axis=-1, keepdims=True)
             stats[cut] = jnp.where(lane == 0, top, jnp.where(lane == 1, exps, picked))
+
+
+def pieces_kernel(lhs, *refs):
+    at, total = 0, None
+    for w in refs[:-1]:
+        deep = w.shape[0]
+        part = dot(lhs[:, at : at + deep], w[...])
+        total = part if total is None else total + part
+        at += deep
+    refs[-1][...] = total.astype(refs[-1].dtype)
+
+
+def finish_kernel(base, lengths, stats, token, sums):
+    tops = [stats[k, 0:1] for k in range(stats.shape[0])]
+    top = tops[0]
+    for t in tops[1:]:
+        top = jnp.maximum(top, t)
+    exps = sum(stats[k, 1:2] * jnp.exp(t - top) for k, t in enumerate(tops))
+    picked = sum(stats[k, 2:3] for k in range(stats.shape[0]))
+    logp = picked - (top + jnp.log(exps))
+    batches, length = token.shape
+    position = base[0] + lax.broadcasted_iota(jnp.int32, (1, length), 1)
+    total = jnp.zeros((1, 1), F32)
+    for b in range(batches):
+        part = logp[:, b * length : (b + 1) * length]
+        token[b : b + 1] = part
+        masked = jnp.where(position < lengths[b], part, 0.0)
+        total = total + jnp.sum(masked, axis=1, keepdims=True)
+    sums[...] = jnp.broadcast_to(total[None], sums.shape)
 
 
 def vmem():
@@ -235,7 +251,8 @@
     order = [(i, i + 1) for i in range(YS * XS * CS - 1)]
     tail = lax.ppermute(resid[:, local_len - (taps - 1) :, :], DP, order)
     near = {s: lax.ppermute(in_x, DP, turns(s, 0)) for s in (1, 3, 2)}
-    line = jnp.concatenate([in_x, near[1], near[2], near[3]], axis=0)
+    first = jnp.concatenate([in_x, near[1]], axis=0)
+    second = jnp.concatenate([near[2], near[3]], axis=0)
     halo = 16
     tail = jnp.pad(
         tail.reshape(batch_count * (taps - 1), width),
@@ -257,23 +274,39 @@
         tail,
         norm_gain.reshape(1, width),
     )
-    line, mine, theirs, in_z = lax.optimization_barrier((line, mine, theirs, in_z))
+    first, second, mine, theirs, in_z = lax.optimization_barrier(
+        (first, second, mine, theirs, in_z)
+    )
     all_z = lax.all_gather(in_z, DP, axis=0, tiled=True)
-    behind, opposite, ahead = around(line, DP, lambda by: turns(by, 1))
+    behind_first = lax.ppermute(first, DP, turns(1, 1))
+    ahead_second = lax.ppermute(second, DP, turns(3, 1))
+    behind_second = lax.ppermute(second, DP, turns(1, 1))
+    ahead_first = lax.ppermute(first, DP, turns(3, 1))
+    far_first = lax.ppermute(behind_first, DP, turns(1, 1))
+    far_second = lax.ppermute(ahead_second, DP, turns(3, 1))
     share = width // zs
     out_cut = [
         lax.dynamic_slice_in_dim(out_w, lax.rem(zi + by, zs) * share, share, 1)
         for by in range(zs)
     ]
-    opposite, out_cut = lax.optimization_barrier((opposite, out_cut))
-    pieces = [line, behind, jnp.concatenate(opposite, axis=0), ahead]
+    far_first, far_second, out_cut = lax.optimization_barrier((far_first, far_second, out_cut))
+    pieces = [
+        first, second, behind_first, behind_second, far_first, far_second, ahead_first, ahead_second
+    ]
+
+    def half_dot(lhs, kind, name):
+        return pl.pallas_call(
+            pieces_kernel,
+            out_shape=jax.ShapeDtypeStruct((lhs.shape[0], channels), kind),
+            in_specs=[vmem()] * (1 + len(pieces)),
+            out_specs=vmem(),
+            compiler_params=pltpu.CompilerParams(vmem_limit_bytes=48 << 20),
+            name=name,
+        )(lhs, *pieces)
+
     theirs = swap_cores(theirs)
-    depth = width // CS // 4
-    cut = [slice(s * depth, (s + 1) * depth) for s in range(4)]
-    turn = (0, 1, 3, 2)
-    for_them = sum(dot(theirs[:, cut[s]], pieces[s]) for s in turn)
-    from_them = swap_cores(for_them.astype(BF))
-    x_acc = sum(dot(mine[:, cut[s]], pieces[s]) for s in turn) + from_them.astype(F32)
+    from_them = swap_cores(half_dot(theirs, BF, "x_theirs"))
+    x_acc = half_dot(mine, F32, "x_mine") + from_them.astype(F32)
     x_all = x_acc.astype(BF)
     x_inner = x_all[:rows].reshape(batch_count, local_len, channels)
     before = x_all[rows : rows + batch_count * (taps - 1)].reshape(batch_count, taps - 1, channels)
@@ -398,25 +431,24 @@
     opposite_upper = lax.ppermute(behind_upper, "vocab", hops(1))
     opposite_lower = lax.ppermute(ahead_lower, "vocab", hops(3))
     vocab_rows = head_w.shape[0]
-    deep = 512
-    per = share // deep
     gain = final_gain.reshape(1, width)
 
-    def blocks(*hops_back):
+    def blocks(per, *hops_back):
         firsts = [lax.rem(zi - s + zs, zs) * per for s in hops_back]
         return jnp.stack([first + i for first in firsts for i in range(per)])
 
     def whole(*shape):
-        return pl.BlockSpec(shape, lambda j, order: (0,) * len(shape))
-
-    head_block = pl.BlockSpec((deep, vocab_rows), lambda j, order: (order[j], 0))
+        return vmem()
+
     sums = [whole(rows, vocab_rows), whole(rows, 128)]
     sums_shape = (
         jax.ShapeDtypeStruct((rows, vocab_rows), F32),
         jax.ShapeDtypeStruct((rows, 128), F32),
     )
 
-    def logits_call(kernel, name, from_where, pieces, extra, last=False):
+    def logits_call(kernel, name, deep, from_where, pieces, extra, last=False):
+        per = share // deep
+        head_block = pl.BlockSpec((deep, vocab_rows), lambda j, order: (order[j], 0))
         halves = [whole(middle, share)] * len(pieces)
         weights = [whole(1, width), head_block]
         extra_specs = [whole(*e.shape) for e in extra]
@@ -432,20 +464,21 @@
             out_shape=jax.ShapeDtypeStruct((rows, 128), F32) if last else sums_shape,
             compiler_params=pltpu.CompilerParams(vmem_limit_bytes=48 << 20),
             name=name,
-        )(blocks(*from_where), *pieces, gain, all_head, *extra)
-
-    acc = logits_call(own_kernel, "own_logits", (0,), (upper, lower), ())
+        )(blocks(per, *from_where), *pieces, gain, all_head, *extra)
+
     acc = logits_call(
         near_kernel,
         "near_logits",
-        (1, 3),
-        (behind_upper, behind_lower, ahead_upper, ahead_lower),
-        acc,
+        share,
+        (0, 1, 3),
+        (upper, lower, behind_upper, behind_lower, ahead_upper, ahead_lower),
+        (),
     )
     local_ids = targets.reshape(rows, 1) - zi * vocab_rows
     stats = logits_call(
         last_kernel,
         "last_logits",
+        share // 2,
         (2,),
         (opposite_upper, opposite_lower),
         (*acc, local_ids),
@@ -455,16 +488,18 @@
     stats = lax.all_to_all(
         jnp.broadcast_to(stats[None], (zs, *stats.shape)), "vocab", 0, 0, tiled=True
     )
-    all_top = jnp.max(stats[:, 0], axis=0)
-    all_exps = jnp.sum(stats[:, 1] * jnp.exp(stats[:, 0] - all_top), axis=0)
-    token_logp = (jnp.sum(stats[:, 2], axis=0) - (all_top + jnp.log(all_exps))).reshape(
-        batch_count, local_len
-    )
-    positions = lax.axis_index(DP) * local_len + jnp.arange(local_len, dtype=jnp.int32)
-    valid = positions[None, :] < lengths[:, None]
-    masked = jnp.sum(jnp.where(valid, token_logp, 0.0))
     peers = YS * XS * CS
-    sums = lax.all_to_all(jnp.broadcast_to(masked, (peers, 1)), DP, 0, 0, tiled=True)
+    token_logp, sums = pl.pallas_call(
+        finish_kernel,
+        out_shape=(
+            jax.ShapeDtypeStruct((batch_count, local_len), F32),
+            jax.ShapeDtypeStruct((peers, 1, 128), F32),
+        ),
+        in_specs=[smem(), smem(), vmem()],
+        out_specs=(vmem(),) * 2,
+        name="finish",
+    )((lax.axis_index(DP) * local_len).reshape(1), lengths, stats)
+    sums = lax.all_to_all(sums, DP, 0, 0, tiled=True)[:, 0, 0]
     mean_logp = jnp.sum(sums) / jnp.sum(lengths.astype(F32))
     return (hidden_share.reshape(batch_count, local_len, share), token_logp, mean_logp)
 

time: 216 us -> 215 us (level)
  matrix products: 21.5 us -> 10.9 us
  waiting for transfers between devices: 53.1 us -> 62.2 us
  Pallas kernels: 32.1 us -> 38 us
  local copies, waits for them, and re-layouts: 22.1 us -> 16.6 us
    dot_general x14 -> x6, matrix products: 21.5 us -> 10.9 us  [dot(): return jnp.dot(a, b, preferred_element_type=F32)]
    pallas_call x0 -> x3, Pallas kernels: none -> 7.96 us  [the longest x2 6.52 us: half_dot(): pl.pallas_call(pieces_kernel, out_shape=jax.ShapeDtypeStruct((lhs.shape[0...]
    ppermute x4 -> x6, waiting for transfers between devices: 7.71 us -> 13.8 us  [the longest x1 7 us: body(): behind_second = lax.ppermute(second, DP, turns(1, 1))]
    ppermute x1, waiting for transfers between devices: 4.98 us -> 0.38 us  [body(): up_low = lax.ppermute(after[middle:].astype(BF), 'vocab', hops(1))]
    ppermute x1, waiting for transfers between devices: 0.01 us -> 3.1 us  [body(): up = lax.ppermute(far[:middle], 'vocab', hops(1))]
    ppermute x1, waiting for transfers between devices: 0.01 us -> 2.52 us  [body(): behind_lower = lax.ppermute(lower, 'vocab', hops(1))]
    ppermute x1, waiting for transfers between devices: 3.11 us -> 5.62 us  [body(): lax.ppermute((after[:middle] + up.astype(F32)).astype(BF), 'vocab', hops(1))]
    ppermute x1, waiting for transfers between devices: 2.5 us -> 0.01 us  [body(): lax.ppermute((prior[middle:] + down.astype(F32)).astype(BF), 'vocab', hop...]
  transfers between devices with their start and end apart: 32 -> 34, of which waited for: 16 -> 18; matrix products, arithmetic and copies ran while one was open for 18% -> 12% of each run, Pallas kernels for 13% -> 15%
where the time goes in v3:
time: 215 us; the launch traced here: 214 us
  starting transfers between devices  63.4 us (29%)
  waiting for transfers between devices  62.2 us (29%)
  Pallas kernels  38 us (18%)
  between operations  17.4 us (8%)
  local copies, waits for them, and re-layouts  16.6 us (8%)
  matrix products  10.9 us (5%)
  other arithmetic  5.42 us (3%)
    pallas_call x2, Pallas kernels, logits_call(): pl.pallas_call(kernel, grid_spec=pltpu.PrefetchScalarGridSpec(num_scalar_...  12.1 us
    all_to_all x1, waiting for transfers between devices, body(): lax.all_to_all(jnp.broadcast_to(packed[None], (chips, *packed.shape)), CH...  11.3 us
    dot_general x6, matrix products, dot(): return jnp.dot(a, b, preferred_element_type=F32)  10.9 us
    all_to_all x1, starting transfers between devices, body(): sums = lax.all_to_all(sums, DP, 0, 0, tiled=True)[:, 0, 0]  8.83 us
    ppermute x3, waiting for transfers between devices, body(): low_sum = low_sum + lax.ppermute(low_sent, 'vocab', ring(zs, s)).astype(F32)  7.59 us
    pallas_call x1, Pallas kernels, body(): pl.pallas_call(lambda *refs: outputs_kernel(rows, local_len, nstate, *ref...  7.02 us
    dynamic_slice x1, local copies, waits for them, and re-layouts, body(): lax.dynamic_slice_in_dim(out_w, lax.rem(zi + by, zs) * share, share, 1)  7.01 us
    ppermute x1, waiting for transfers between devices, body(): behind_second = lax.ppermute(second, DP, turns(1, 1))  7 us
  transfers between devices with their start and end apart: 34, of which 18 were waited for; matrix products, arithmetic and copies ran while one was open for 12% of the time, Pallas kernels for 15%

profile of v3, /device:TPU:1, one launch (start us, length us, event | category | flops | bytes accessed | tf_op | source)
XLA Modules:
  0.0 213.8 jit_solution(872384118699048686)
XLA Ops:
  7.2 2.2 %collective-permute-start = (bf16[128,1024]{1,0:T(8,128)(2,1)}, bf16[128,1024]{1,0:T(8,128)(2,1)S(1)}, u32[]{:S(2)}, u32[]{:S(2)}) collective-permute-start(bf16[128,1024]{1,0:T(8,128)(2,1)} %param.19), channel_id=1, source_target_pairs={{0,8},{4,36},{8,16},{12,44},{16,24},{20,52},{24,0},{28,60},{32,40}... | collective-permute-start | bytes 786440 | tf_op jit(solution)/shard_map/ppermute | solution.py:253
  9.4 1.5 collective-permute-start.2
  10.9 1.6 collective-permute-start.1
  13.4 3.5 %collective-permute-start.3 = (bf16[2,3,4096]{2,1,0:T(4,128)(2,1)S(1)}, bf16[2,3,4096]{2,1,0:T(4,128)(2,1)S(1)}, u32[]{:S(2)}, u32[]{:S(2)}) collective-permute-start(bf16[2,3,4096]{2,1,0:T(4,128)(2,1)S(1)} %slice.260), channel_id=1, source_target_pairs={{0,4},{4,8},{8,12},{12,16},{16,20},{20,24},{24,28},{28,32},{32,36}... | collective-permute-start | bytes 147464 | tf_op jit(solution)/shard_map/ppermute | solution.py:252
  17.2 1.1 collective-permute-done.3
  19.0 4.3 %norm.1 = (bf16[256,4096]{1,0:T(8,128)(2,1)S(1)}, bf16[272,2048]{1,0:T(8,128)(2,1)S(1)}, bf16[272,2048]{1,0:T(8,128)(2,1)}) custom-call(s32[32]{0:T(128)S(1)} %stack.152.refs_0_, bf16[256,4096]{1,0:T(8,128)(2,1)} %bitcast.169, bf16[16,4096]{1,0:T(8,128)(2,1)S(1)} %pad.4.refs_2_, f32[1,4096]{1,0:T(1,128)S(1)} %bitcast.166), custom_call_target="tpu_custom_call" | custom-call | tf_op jit(solution)/shard_map/norm/pallas_call | solution.py:263
  23.4 1.0 copy-done
  24.4 1.3 copy-done.6
  26.0 2.6 %collective-permute-start.4 = (bf16[256,1024]{1,0:T(8,128)(2,1)S(1)}, bf16[256,1024]{1,0:T(8,128)(2,1)S(1)}, u32[]{:S(2)}, u32[]{:S(2)}) collective-permute-start(bf16[256,1024]{1,0:T(8,128)(2,1)S(1)} %pad_maximum_fusion.refs_0_), channel_id=1, source_target_pairs={{0,32},{4,12},{8,40},{12,20},{16,48},{20,28},{24,56},{28,4},{32,64... | collective-permute-start | bytes 1572872 | tf_op jit(solution)/shard_map/ppermute | solution.py:281
  29.5 6.8 %collective-permute-done.4.refs_2_ = bf16[256,1024]{1,0:T(8,128)(2,1)S(1)} collective-permute-done((bf16[256,1024]{1,0:T(8,128)(2,1)S(1)}, bf16[256,1024]{1,0:T(8,128)(2,1)S(1)}, u32[]{:S(2)}, u32[]{:S(2)}) %collective-permute-start.4) | collective-permute-done | bytes 524320 | tf_op jit(solution)/shard_map/ppermute | solution.py:281
  36.9 2.1 collective-permute-start.8
  39.0 2.7 %collective-permute-start.9 = (bf16[256,1024]{1,0:T(8,128)(2,1)S(1)}, bf16[256,1024]{1,0:T(8,128)(2,1)}, u32[]{:S(2)}, u32[]{:S(2)}) collective-permute-start(bf16[256,1024]{1,0:T(8,128)(2,1)S(1)} %pad_maximum_fusion.refs_0_), channel_id=1, source_target_pairs={{0,96},{4,28},{8,104},{12,4},{16,112},{20,12},{24,120},{28,20},{32... | collective-permute-start | bytes 1572872 | tf_op jit(solution)/shard_map/ppermute | solution.py:284
  41.7 7.0 %constant_dynamic-slice_fusion.3 = (bf16[1024,1024]{1,0:T(8,128)(2,1)}, bf16[1024,1024]{1,0:T(8,128)(2,1)}, bf16[1024,1024]{1,0:T(8,128)(2,1)}, bf16[1024,1024]{1,0:T(8,128)(2,1)}) fusion(bf16[1024,4096]{1,0:T(8,128)(2,1)} %param.29, s32[]{:T(128)S(6)} %select_n.260, s32[]{:T(128)S(6)} %select_n.258, s32[]{:T(128)S(6)} %select_n.257, s32[]{:T(128)S(6)} %select_n.259), kind=kLoop, calls=%fused_computation.131 | loop fusion | bytes 16777232 | tf_op jit(solution)/shard_map/dynamic_slice | solution.py:289
  48.8 7.0 %collective-permute-done.5.refs_3_ = bf16[256,1024]{1,0:T(8,128)(2,1)} collective-permute-done((bf16[256,1024]{1,0:T(8,128)(2,1)S(1)}, bf16[256,1024]{1,0:T(8,128)(2,1)}, u32[]{:S(2)}, u32[]{:S(2)}) %collective-permute-start.5) | collective-permute-done | bytes 524320 | tf_op jit(solution)/shard_map/ppermute | solution.py:283
  55.8 3.7 %x_theirs.1 = bf16[272,1024]{1,0:T(8,128)(2,1)} custom-call(bf16[272,2048]{1,0:T(8,128)(2,1)} %collective-permute-done.10.lhs, bf16[256,1024]{1,0:T(8,128)(2,1)S(1)} %pad_maximum_fusion.refs_0_, bf16[256,1024]{1,0:T(8,128)(2,1)S(1)} %pad_maximum_fusion.1.refs_1_, bf16[256,1024]{1,0:T(8,128)(2,1)S(1)} %collective-permute-done.4.refs_2_, ...), custom_call_target="tpu_custom_call" | custom-call | tf_op jit(solution)/shard_map/x_theirs/pallas_call | solution.py:298
  59.4 4.0 %collective-permute-start.11 = (bf16[272,1024]{1,0:T(8,128)(2,1)}, bf16[272,1024]{1,0:T(8,128)(2,1)}, u32[]{:S(2)}, u32[]{:S(2)}) collective-permute-start(bf16[272,1024]{1,0:T(8,128)(2,1)} %x_theirs.1), channel_id=1, source_target_pairs={{0,4},{4,0},{1,5},{5,1},{2,6},{6,2},{3,7},{7,3},{8,12},{12,8},{9,1... | collective-permute-start | bytes 1671176 | tf_op jit(solution)/shard_map/ppermute | solution.py:39
  63.6 2.8 %x_mine.1 = f32[272,1024]{1,0:T(8,128)S(1)} custom-call(bf16[272,2048]{1,0:T(8,128)(2,1)} %copy-done, bf16[256,1024]{1,0:T(8,128)(2,1)S(1)} %pad_maximum_fusion.refs_0_, bf16[256,1024]{1,0:T(8,128)(2,1)S(1)} %pad_maximum_fusion.1.refs_1_, bf16[256,1024]{1,0:T(8,128)(2,1)S(1)} %collective-permute-done.4.refs_2_, ...), custom_call_target="tpu_custom_call" | custom-call | tf_op jit(solution)/shard_map/x_mine/pallas_call | solution.py:298
  66.5 1.2 add_convert_fusion
  69.5 3.4 %collective-permute-start.14 = (bf16[256,288]{1,0:T(8,128)(2,1)S(1)}, bf16[256,288]{1,0:T(8,128)(2,1)S(1)}, u32[]{:S(2)}, u32[]{:S(2)}) collective-permute-start(bf16[256,288]{1,0:T(8,128)(2,1)S(1)} %convolution_convert_fusion.2), channel_id=1, source_target_pairs={{0,2},{1,3},{2,0},{3,1},{4,6},{5,7},{6,4},{7,5},{8,10},{9,11},{10,... | collective-permute-start | bytes 442376 | tf_op jit(solution)/shard_map/ppermute | solution.py:322
  74.4 1.0 copy.48
  75.4 2.8 %collective-permute-done.14 = bf16[256,288]{1,0:T(8,128)(2,1)S(1)} collective-permute-done((bf16[256,288]{1,0:T(8,128)(2,1)S(1)}, bf16[256,288]{1,0:T(8,128)(2,1)S(1)}, u32[]{:S(2)}, u32[]{:S(2)}) %collective-permute-start.14) | collective-permute-done | bytes 147488 | tf_op jit(solution)/shard_map/ppermute | solution.py:322
  78.2 4.7 %collective-permute-done.13 = bf16[256,288]{1,0:T(8,128)(2,1)S(1)} collective-permute-done((bf16[256,288]{1,0:T(8,128)(2,1)S(1)}, bf16[256,288]{1,0:T(8,128)(2,1)S(1)}, u32[]{:S(2)}, u32[]{:S(2)}) %collective-permute-start.13) | collective-permute-done | bytes 147488 | tf_op jit(solution)/shard_map/ppermute | solution.py:322
  84.3 1.0 copy-done.1
  85.3 6.6 %steps.1 = (f32[256,8,128]{2,1,0:T(8,128)S(1)}, f32[256,8,128]{2,1,0:T(8,128)S(1)}, f32[2,16,8,128]{3,2,1,0:T(8,128)S(1)}, f32[2,8,128]{2,1,0:T(8,128)S(1)}) custom-call(f32[8192]{0:T(1024)S(1)} %reshape.106.refs_0_, f32[256,256]{1,0:T(8,128)S(1)} %slice.351.refs_1_, f32[1,256]{1,0:T(1,128)S(1)} %bitcast.168, bf16[256,1024]{1,0:T(8,128)(2,1)S(1)} %copy-done.1, ...), custom_call_target="tpu_custom_call" | custom-call | tf_op jit(solution)/shard_map/steps/pallas_call | solution.py:331
  92.3 1.0 collective-permute-done.15
  94.4 4.9 %all-to-all-start = ((bf16[16,2,10,8,128]{4,3,2,1,0:T(8,128)(2,1)}), bf16[16,2,10,8,128]{4,3,2,1,0:T(8,128)(2,1)S(1)}, u32[]{:S(2)}, u32[]{:S(2)}) async-start(bf16[16,2,10,8,128]{4,3,2,1,0:T(8,128)(2,1)} %broadcast_in_dim.15), calls=%async_computation | async-start | bytes 1310720 | tf_op jit(solution)/shard_map/all_to_all | solution.py:375
  99.3 6.4 %convolution_convert_fusion.refs_5_ = bf16[256,1024]{1,0:T(8,128)(2,1)S(1)} fusion(bf16[256,4096]{1,0:T(8,128)(2,1)} %copy-done.6, bf16[4096,1024]{1,0:T(8,128)(2,1)} %all-gather.3.cloned.1.call-done), kind=kOutput, calls=%fused_computation.1 | convolution fusion | flops 2147745792 | bytes 11010048 | tf_op jit(solution)/shard_map/dot_general | solution.py:57
  105.7 11.3 %all-to-all-done = bf16[16,2,10,8,128]{4,3,2,1,0:T(8,128)(2,1)S(1)} async-done(((bf16[16,2,10,8,128]{4,3,2,1,0:T(8,128)(2,1)}), bf16[16,2,10,8,128]{4,3,2,1,0:T(8,128)(2,1)S(1)}, u32[]{:S(2)}, u32[]{:S(2)}) %all-to-all-start) | async-done | bytes 655392 | tf_op jit(solution)/shard_map/all_to_all | solution.py:375
  119.5 7.0 %outputs.1 = bf16[256,1024]{1,0:T(8,128)(2,1)S(1)} custom-call(f32[8192]{0:T(1024)S(1)} %reshape.106.refs_0_, f32[256,8,128]{2,1,0:T(8,128)S(1)} %get-tuple-element.38.refs_1_, f32[256,8,128]{2,1,0:T(8,128)S(1)} %get-tuple-element.39.refs_2_, f32[16,8,128]{2,1,0:T(8,128)S(1)} %bitcast.162, f32[2,16,8,128]{3,2,1,0:T(8,128)S(1)} %pad_maximum_fusion.3.refs_4_, ...), custom_call_target="tpu_custom_call" | custom-call | tf_op jit(solution)/shard_map/outputs/pallas_call | solution.py:393
  127.3 2.7 %collective-permute-start.19 = (bf16[128,1024]{1,0:T(8,128)(2,1)S(1)}, bf16[128,1024]{1,0:T(8,128)(2,1)S(1)}, u32[]{:S(2)}, u32[]{:S(2)}) collective-permute-start(bf16[128,1024]{1,0:T(8,128)(2,1)S(1)} %slice.600), channel_id=1, source_target_pairs={{0,3},{1,0},{2,1},{3,2},{4,7},{5,4},{6,5},{7,6},{8,11},{9,8},{10,9... | collective-permute-start | bytes 786440 | tf_op jit(solution)/shard_map/ppermute | solution.py:416
  130.9 2.7 %collective-permute-start.21 = (bf16[128,1024]{1,0:T(8,128)(2,1)S(1)}, bf16[128,1024]{1,0:T(8,128)(2,1)S(1)}, u32[]{:S(2)}, u32[]{:S(2)}) collective-permute-start(bf16[128,1024]{1,0:T(8,128)(2,1)S(1)} %get-tuple-element.88), channel_id=1, source_target_pairs={{0,3},{1,0},{2,1},{3,2},{4,7},{5,4},{6,5},{7,6},{8,11},{9,8},{10,9... | collective-permute-start | bytes 786440 | tf_op jit(solution)/shard_map/ppermute | solution.py:409
  134.4 1.9 convolution_add_fusion
  136.3 3.1 %collective-permute-done.17 = bf16[128,1024]{1,0:T(8,128)(2,1)S(1)} collective-permute-done((bf16[128,1024]{1,0:T(8,128)(2,1)S(1)}, bf16[128,1024]{1,0:T(8,128)(2,1)S(1)}, u32[]{:S(2)}, u32[]{:S(2)}) %collective-permute-start.17) | collective-permute-done | bytes 262176 | tf_op jit(solution)/shard_map/ppermute | solution.py:408
  139.6 1.4 collective-permute-done.21
  141.0 3.6 %collective-permute-start.22 = (bf16[128,1024]{1,0:T(8,128)(2,1)S(1)}, bf16[128,1024]{1,0:T(8,128)(2,1)S(1)}, u32[]{:S(2)}, u32[]{:S(2)}) collective-permute-start(bf16[128,1024]{1,0:T(8,128)(2,1)S(1)} %fusion.7), channel_id=1, source_target_pairs={{0,3},{1,0},{2,1},{3,2},{4,7},{5,4},{6,5},{7,6},{8,11},{9,8},{10,9... | collective-permute-start | bytes 786440 | tf_op jit(solution)/shard_map/ppermute | solution.py:420
  145.0 5.6 %collective-permute-done.18 = bf16[128,1024]{1,0:T(8,128)(2,1)S(1)} collective-permute-done((bf16[128,1024]{1,0:T(8,128)(2,1)S(1)}, bf16[128,1024]{1,0:T(8,128)(2,1)S(1)}, u32[]{:S(2)}, u32[]{:S(2)}) %collective-permute-start.18) | collective-permute-done | bytes 262176 | tf_op jit(solution)/shard_map/ppermute | solution.py:417
  151.2 2.7 %collective-permute-start.25 = (bf16[128,1024]{1,0:T(8,128)(2,1)S(1)}, bf16[128,1024]{1,0:T(8,128)(2,1)S(1)}, u32[]{:S(2)}, u32[]{:S(2)}) collective-permute-start(bf16[128,1024]{1,0:T(8,128)(2,1)S(1)} %get-tuple-element.71.b), channel_id=1, source_target_pairs={{0,3},{1,0},{2,1},{3,2},{4,7},{5,4},{6,5},{7,6},{8,11},{9,8},{10,9... | collective-permute-start | bytes 786440 | tf_op jit(solution)/shard_map/ppermute | solution.py:428
  153.8 2.7 %collective-permute-start.28 = (bf16[128,1024]{1,0:T(8,128)(2,1)S(1)}, bf16[128,1024]{1,0:T(8,128)(2,1)S(1)}, u32[]{:S(2)}, u32[]{:S(2)}) collective-permute-start(bf16[128,1024]{1,0:T(8,128)(2,1)S(1)} %get-tuple-element.70.a), channel_id=1, source_target_pairs={{0,3},{1,0},{2,1},{3,2},{4,7},{5,4},{6,5},{7,6},{8,11},{9,8},{10,9... | collective-permute-start | bytes 786440 | tf_op jit(solution)/shard_map/ppermute | solution.py:430
  156.5 2.4 %collective-permute-done.23.c = bf16[128,1024]{1,0:T(8,128)(2,1)S(1)} collective-permute-done((bf16[128,1024]{1,0:T(8,128)(2,1)S(1)}, bf16[128,1024]{1,0:T(8,128)(2,1)S(1)}, u32[]{:S(2)}, u32[]{:S(2)}) %collective-permute-start.23) | collective-permute-done | bytes 262176 | tf_op jit(solution)/shard_map/ppermute | solution.py:427
  158.9 2.7 %collective-permute-start.26 = (bf16[128,1024]{1,0:T(8,128)(2,1)S(1)}, bf16[128,1024]{1,0:T(8,128)(2,1)S(1)}, u32[]{:S(2)}, u32[]{:S(2)}) collective-permute-start(bf16[128,1024]{1,0:T(8,128)(2,1)S(1)} %collective-permute-done.25.f), channel_id=1, source_target_pairs={{0,3},{1,0},{2,1},{3,2},{4,7},{5,4},{6,5},{7,6},{8,11},{9,8},{10,9... | collective-permute-start | bytes 786440 | tf_op jit(solution)/shard_map/ppermute | solution.py:432
  161.9 2.5 %collective-permute-done.27.d = bf16[128,1024]{1,0:T(8,128)(2,1)S(1)} collective-permute-done((bf16[128,1024]{1,0:T(8,128)(2,1)S(1)}, bf16[128,1024]{1,0:T(8,128)(2,1)S(1)}, u32[]{:S(2)}, u32[]{:S(2)}) %collective-permute-start.27) | collective-permute-done | bytes 262176 | tf_op jit(solution)/shard_map/ppermute | solution.py:429
  164.7 7.5 %near_logits.1 = (f32[256,2048]{1,0:T(8,128)S(1)}, f32[256,128]{1,0:T(8,128)S(1)}) custom-call(s32[3]{0:T(128)S(1)} %pad_add_fusion.1.order, bf16[128,1024]{1,0:T(8,128)(2,1)S(1)} %get-tuple-element.70.a, bf16[128,1024]{1,0:T(8,128)(2,1)S(1)} %get-tuple-element.71.b, bf16[128,1024]{1,0:T(8,128)(2,1)S(1)} %collective-permute-done.23.c, ...), custom_call_target="tpu_custom_call" | custom-call | tf_op jit(solution)/shard_map/near_logits/pallas_call | solution.py:455
  172.2 4.6 %last_logits.1 = f32[256,128]{1,0:T(8,128)S(1)} custom-call(s32[2]{0:T(128)S(1)} %pad_add_fusion.order, bf16[128,1024]{1,0:T(8,128)(2,1)S(1)} %collective-permute-done.24.upper, bf16[128,1024]{1,0:T(8,128)(2,1)S(1)} %collective-permute-done.26.lower, f32[1,4096]{1,0:T(1,128)S(1)} %bitcast.164, bf16[4096,2048]{1,0:T(8,128)(2,1)} %all-gather.5.cloned.1.call-done.head, ...), custom_call_target="tpu_custom_call" | custom-call | tf_op jit(solution)/shard_map/last_logits/pallas_call | solution.py:455
  177.5 4.2 %all-to-all-start.1 = ((f32[4,3,256]{2,1,0:T(4,128)}), f32[4,3,256]{2,1,0:T(4,128)S(1)}, u32[]{:S(2)}, u32[]{:S(2)}) async-start(f32[4,3,256]{2,1,0:T(4,128)} %broadcast_in_dim.17), calls=%async_computation.1 | async-start | bytes 32768 | tf_op jit(solution)/shard_map/all_to_all | solution.py:488
  182.4 3.5 %all-to-all-done.1.stats = f32[4,3,256]{2,1,0:T(4,128)S(1)} async-done(((f32[4,3,256]{2,1,0:T(4,128)}), f32[4,3,256]{2,1,0:T(4,128)S(1)}, u32[]{:S(2)}, u32[]{:S(2)}) %all-to-all-start.1) | async-done | bytes 12320 | tf_op jit(solution)/shard_map/all_to_all | solution.py:488
  186.5 1.4 finish.1
  188.0 8.8 %all-to-all-start.2 = ((f32[32,1,128]{2,1,0:T(1,128)}), f32[32,1,128]{2,1,0:T(1,128)S(1)}, u32[]{:S(2)}, u32[]{:S(2)}) async-start(f32[32,1,128]{2,1,0:T(1,128)} %get-tuple-element.56), calls=%async_computation.2 | async-start | bytes 32768 | tf_op jit(solution)/shard_map/all_to_all | solution.py:502
  197.6 6.2 %all-to-all-done.2 = f32[32,1,128]{2,1,0:T(1,128)S(1)} async-done(((f32[32,1,128]{2,1,0:T(1,128)}), f32[32,1,128]{2,1,0:T(1,128)S(1)}, u32[]{:S(2)}, u32[]{:S(2)}) %all-to-all-start.2) | async-done | bytes 16416 | tf_op jit(solution)/shard_map/all_to_all | solution.py:502
  (137 shorter events, 19.6 us)
Async XLA Ops:
  7.2 18.6 %copy-start.13 = (bf16[128,1024]{1,0:T(8,128)(2,1)S(1)}, bf16[128,1024]{1,0:T(8,128)(2,1)}, u32[]{:S(2)}) copy-start(bf16[128,1024]{1,0:T(8,128)(2,1)} %param.19) | copy-start | bytes 786436
  7.2 76.8 %all-gather.3.cloned.1.call-start = ((), (), s32[]{:S(2)}) async-start(), calls=%async_computation.3 | async-start | bytes 8650752 | tf_op jit(solution)/shard_map/all_gather | solution.py:280
  7.2 18.5 %collective-permute-start = (bf16[128,1024]{1,0:T(8,128)(2,1)}, bf16[128,1024]{1,0:T(8,128)(2,1)S(1)}, u32[]{:S(2)}, u32[]{:S(2)}) collective-permute-start(bf16[128,1024]{1,0:T(8,128)(2,1)} %param.19), channel_id=1, source_target_pairs={{0,8},{4,36},{8,16},{12,44},{16,24},{20,52},{24,0},{28,60},{32,40}... | collective-permute-start | bytes 786440 | tf_op jit(solution)/shard_map/ppermute | solution.py:253
  9.4 16.4 %collective-permute-start.2 = (bf16[128,1024]{1,0:T(8,128)(2,1)}, bf16[128,1024]{1,0:T(8,128)(2,1)S(1)}, u32[]{:S(2)}, u32[]{:S(2)}) collective-permute-start(bf16[128,1024]{1,0:T(8,128)(2,1)} %param.19), channel_id=1, source_target_pairs={{0,24},{4,100},{8,0},{12,108},{16,8},{20,116},{24,16},{28,124},{32... | collective-permute-start | bytes 786440 | tf_op jit(solution)/shard_map/ppermute | solution.py:253
  10.9 14.8 %collective-permute-start.1 = (bf16[128,1024]{1,0:T(8,128)(2,1)}, bf16[128,1024]{1,0:T(8,128)(2,1)S(1)}, u32[]{:S(2)}, u32[]{:S(2)}) collective-permute-start(bf16[128,1024]{1,0:T(8,128)(2,1)} %param.19), channel_id=1, source_target_pairs={{0,16},{4,68},{8,24},{12,76},{16,0},{20,84},{24,8},{28,92},{32,48}... | collective-permute-start | bytes 786440 | tf_op jit(solution)/shard_map/ppermute | solution.py:253
  13.4 4.8 %collective-permute-start.3 = (bf16[2,3,4096]{2,1,0:T(4,128)(2,1)S(1)}, bf16[2,3,4096]{2,1,0:T(4,128)(2,1)S(1)}, u32[]{:S(2)}, u32[]{:S(2)}) collective-permute-start(bf16[2,3,4096]{2,1,0:T(4,128)(2,1)S(1)} %slice.260), channel_id=1, source_target_pairs={{0,4},{4,8},{8,12},{12,16},{16,20},{20,24},{24,28},{28,32},{32,36}... | collective-permute-start | bytes 147464 | tf_op jit(solution)/shard_map/ppermute | solution.py:252
  25.9 138.9 %all-gather.5.cloned.1.call-start = ((), (), s32[]{:S(2)}) async-start(), calls=%async_computation.4 | async-start | bytes 17301504 | tf_op jit(solution)/shard_map/all_gather | solution.py:324
  25.9 29.9 %collective-permute-start.10 = (bf16[272,2048]{1,0:T(8,128)(2,1)}, bf16[272,2048]{1,0:T(8,128)(2,1)}, u32[]{:S(2)}, u32[]{:S(2)}) collective-permute-start(bf16[272,2048]{1,0:T(8,128)(2,1)} %get-tuple-element.37), channel_id=1, source_target_pairs={{0,4},{4,0},{1,5},{5,1},{2,6},{6,2},{3,7},{7,3},{8,12},{12,8},{9,1... | collective-permute-start | bytes 3342344 | tf_op jit(solution)/shard_map/ppermute | solution.py:39
  26.0 10.3 %collective-permute-start.4 = (bf16[256,1024]{1,0:T(8,128)(2,1)S(1)}, bf16[256,1024]{1,0:T(8,128)(2,1)S(1)}, u32[]{:S(2)}, u32[]{:S(2)}) collective-permute-start(bf16[256,1024]{1,0:T(8,128)(2,1)S(1)} %pad_maximum_fusion.refs_0_), channel_id=1, source_target_pairs={{0,32},{4,12},{8,40},{12,20},{16,48},{20,28},{24,56},{28,4},{32,64... | collective-permute-start | bytes 1572872 | tf_op jit(solution)/shard_map/ppermute | solution.py:281
  28.6 8.3 %collective-permute-start.7 = (bf16[256,1024]{1,0:T(8,128)(2,1)S(1)}, bf16[256,1024]{1,0:T(8,128)(2,1)S(1)}, u32[]{:S(2)}, u32[]{:S(2)}) collective-permute-start(bf16[256,1024]{1,0:T(8,128)(2,1)S(1)} %pad_maximum_fusion.1.refs_1_), channel_id=1, source_target_pairs={{0,96},{4,28},{8,104},{12,4},{16,112},{20,12},{24,120},{28,20},{32... | collective-permute-start | bytes 1572872 | tf_op jit(solution)/shard_map/ppermute | solution.py:282
  36.3 12.4 %collective-permute-start.6 = (bf16[256,1024]{1,0:T(8,128)(2,1)S(1)}, bf16[256,1024]{1,0:T(8,128)(2,1)S(1)}, u32[]{:S(2)}, u32[]{:S(2)}) collective-permute-start(bf16[256,1024]{1,0:T(8,128)(2,1)S(1)} %collective-permute-done.4.refs_2_), channel_id=1, source_target_pairs={{0,32},{4,12},{8,40},{12,20},{16,48},{20,28},{24,56},{28,4},{32,64... | collective-permute-start | bytes 1572872 | tf_op jit(solution)/shard_map/ppermute | solution.py:285
  36.9 11.8 %collective-permute-start.8 = (bf16[256,1024]{1,0:T(8,128)(2,1)S(1)}, bf16[256,1024]{1,0:T(8,128)(2,1)S(1)}, u32[]{:S(2)}, u32[]{:S(2)}) collective-permute-start(bf16[256,1024]{1,0:T(8,128)(2,1)S(1)} %collective-permute-done.7.refs_7_), channel_id=1, source_target_pairs={{0,96},{4,28},{8,104},{12,4},{16,112},{20,12},{24,120},{28,20},{32... | collective-permute-start | bytes 1572872 | tf_op jit(solution)/shard_map/ppermute | solution.py:286
  39.0 16.7 %collective-permute-start.5 = (bf16[256,1024]{1,0:T(8,128)(2,1)S(1)}, bf16[256,1024]{1,0:T(8,128)(2,1)}, u32[]{:S(2)}, u32[]{:S(2)}) collective-permute-start(bf16[256,1024]{1,0:T(8,128)(2,1)S(1)} %pad_maximum_fusion.1.refs_1_), channel_id=1, source_target_pairs={{0,32},{4,12},{8,40},{12,20},{16,48},{20,28},{24,56},{28,4},{32,64... | collective-permute-start | bytes 1572872 | tf_op jit(solution)/shard_map/ppermute | solution.py:283
  39.0 16.7 %collective-permute-start.9 = (bf16[256,1024]{1,0:T(8,128)(2,1)S(1)}, bf16[256,1024]{1,0:T(8,128)(2,1)}, u32[]{:S(2)}, u32[]{:S(2)}) collective-permute-start(bf16[256,1024]{1,0:T(8,128)(2,1)S(1)} %pad_maximum_fusion.refs_0_), channel_id=1, source_target_pairs={{0,96},{4,28},{8,104},{12,4},{16,112},{20,12},{24,120},{28,20},{32... | collective-permute-start | bytes 1572872 | tf_op jit(solution)/shard_map/ppermute | solution.py:284
  48.7 14.7 %copy-start.14 = (bf16[1024,32]{0,1:T(8,128)(2,1)S(1)}, bf16[1024,32]{0,1:T(8,128)(2,1)}, u32[]{:S(2)}) copy-start(bf16[1024,32]{0,1:T(8,128)(2,1)} %param.24) | copy-start | bytes 196612
  48.7 14.8 %copy-start.17 = (f32[4,1024]{1,0:T(4,128)S(1)}, f32[4,1024]{1,0:T(4,128)}, u32[]{:S(2)}) copy-start(f32[4,1024]{1,0:T(4,128)} %param.21) | copy-start | bytes 49156
  59.4 7.0 %collective-permute-start.11 = (bf16[272,1024]{1,0:T(8,128)(2,1)}, bf16[272,1024]{1,0:T(8,128)(2,1)}, u32[]{:S(2)}, u32[]{:S(2)}) collective-permute-start(bf16[272,1024]{1,0:T(8,128)(2,1)} %x_theirs.1), channel_id=1, source_target_pairs={{0,4},{4,0},{1,5},{5,1},{2,6},{6,2},{3,7},{7,3},{8,12},{12,8},{9,1... | collective-permute-start | bytes 1671176 | tf_op jit(solution)/shard_map/ppermute | solution.py:39
  68.6 5.7 %copy-start.11 = (bf16[2048,128]{1,0:T(8,128)(2,1)S(1)}, bf16[2048,128]{1,0:T(8,128)(2,1)}, u32[]{:S(2)}) copy-start(bf16[2048,128]{1,0:T(8,128)(2,1)} %param.31) | copy-start | bytes 1572868
  69.0 15.1 %copy-start.15 = (f32[1024,16]{0,1:T(8,128)S(1)}, f32[1024,16]{0,1:T(8,128)}, u32[]{:S(2)}) copy-start(f32[1024,16]{0,1:T(8,128)} %param.28) | copy-start | bytes 196612
  69.4 14.8 %copy-start.4 = (f32[1024]{0:T(1024)S(1)}, f32[1024]{0:T(1024)}, u32[]{:S(2)}) copy-start(f32[1024]{0:T(1024)} %param.27) | copy-start | bytes 12292
  69.4 14.8 %copy-start.5 = (f32[256]{0:T(256)S(1)}, f32[256]{0:T(256)}, u32[]{:S(2)}) copy-start(f32[256]{0:T(256)} %param.25) | copy-start | bytes 3076
  69.5 8.8 %collective-permute-start.14 = (bf16[256,288]{1,0:T(8,128)(2,1)S(1)}, bf16[256,288]{1,0:T(8,128)(2,1)S(1)}, u32[]{:S(2)}, u32[]{:S(2)}) collective-permute-start(bf16[256,288]{1,0:T(8,128)(2,1)S(1)} %convolution_convert_fusion.2), channel_id=1, source_target_pairs={{0,2},{1,3},{2,0},{3,1},{4,6},{5,7},{6,4},{7,5},{8,10},{9,11},{10,... | collective-permute-start | bytes 442376 | tf_op jit(solution)/shard_map/ppermute | solution.py:322
  72.9 10.1 %collective-permute-start.13 = (bf16[256,288]{1,0:T(8,128)(2,1)S(1)}, bf16[256,288]{1,0:T(8,128)(2,1)S(1)}, u32[]{:S(2)}, u32[]{:S(2)}) collective-permute-start(bf16[256,288]{1,0:T(8,128)(2,1)S(1)} %convolution_convert_fusion.2), channel_id=1, source_target_pairs={{0,3},{1,0},{2,1},{3,2},{4,7},{5,4},{6,5},{7,6},{8,11},{9,8},{10,9... | collective-permute-start | bytes 442376 | tf_op jit(solution)/shard_map/ppermute | solution.py:322
  73.4 9.5 %collective-permute-start.12 = (bf16[256,288]{1,0:T(8,128)(2,1)S(1)}, bf16[256,288]{1,0:T(8,128)(2,1)S(1)}, u32[]{:S(2)}, u32[]{:S(2)}) collective-permute-start(bf16[256,288]{1,0:T(8,128)(2,1)S(1)} %convolution_convert_fusion.2), channel_id=1, source_target_pairs={{0,1},{1,2},{2,3},{3,0},{4,5},{5,6},{6,7},{7,4},{8,9},{9,10},{10,1... | collective-permute-start | bytes 442376 | tf_op jit(solution)/shard_map/ppermute | solution.py:322
  92.0 1.3 collective-permute-start.15
  94.4 22.6 %all-to-all-start = ((bf16[16,2,10,8,128]{4,3,2,1,0:T(8,128)(2,1)}), bf16[16,2,10,8,128]{4,3,2,1,0:T(8,128)(2,1)S(1)}, u32[]{:S(2)}, u32[]{:S(2)}) async-start(bf16[16,2,10,8,128]{4,3,2,1,0:T(8,128)(2,1)} %broadcast_in_dim.15), calls=%async_computation | async-start | bytes 1310720 | tf_op jit(solution)/shard_map/all_to_all | solution.py:375
  117.5 1.9 collective-permute-start.16
  118.5 8.0 %copy-start.8 = (bf16[1024,1024]{1,0:T(8,128)(2,1)S(1)}, bf16[1024,1024]{1,0:T(8,128)(2,1)}, u32[]{:S(2)}) copy-start(bf16[1024,1024]{1,0:T(8,128)(2,1)} %get-tuple-element.51) | copy-start | bytes 6291460
  126.5 3.5 %copy-start.10 = (bf16[1024,1024]{1,0:T(8,128)(2,1)S(1)}, bf16[1024,1024]{1,0:T(8,128)(2,1)}, u32[]{:S(2)}) copy-start(bf16[1024,1024]{1,0:T(8,128)(2,1)} %get-tuple-element.46) | copy-start | bytes 6291460
  127.3 6.3 %copy-start.7 = (bf16[1024,1024]{1,0:T(8,128)(2,1)S(1)}, bf16[1024,1024]{1,0:T(8,128)(2,1)}, u32[]{:S(2)}) copy-start(bf16[1024,1024]{1,0:T(8,128)(2,1)} %get-tuple-element.49) | copy-start | bytes 6291460
  127.3 17.3 %collective-permute-start.19 = (bf16[128,1024]{1,0:T(8,128)(2,1)S(1)}, bf16[128,1024]{1,0:T(8,128)(2,1)S(1)}, u32[]{:S(2)}, u32[]{:S(2)}) collective-permute-start(bf16[128,1024]{1,0:T(8,128)(2,1)S(1)} %slice.600), channel_id=1, source_target_pairs={{0,3},{1,0},{2,1},{3,2},{4,7},{5,4},{6,5},{7,6},{8,11},{9,8},{10,9... | collective-permute-start | bytes 786440 | tf_op jit(solution)/shard_map/ppermute | solution.py:416
  130.8 8.6 %collective-permute-start.17 = (bf16[128,1024]{1,0:T(8,128)(2,1)S(1)}, bf16[128,1024]{1,0:T(8,128)(2,1)S(1)}, u32[]{:S(2)}, u32[]{:S(2)}) collective-permute-start(bf16[128,1024]{1,0:T(8,128)(2,1)S(1)} %get-tuple-element.87), channel_id=1, source_target_pairs={{0,1},{1,2},{2,3},{3,0},{4,5},{5,6},{6,7},{7,4},{8,9},{9,10},{10,1... | collective-permute-start | bytes 786440 | tf_op jit(solution)/shard_map/ppermute | solution.py:408
  130.9 3.5 %copy-start.9 = (bf16[1024,1024]{1,0:T(8,128)(2,1)S(1)}, bf16[1024,1024]{1,0:T(8,128)(2,1)}, u32[]{:S(2)}) copy-start(bf16[1024,1024]{1,0:T(8,128)(2,1)} %get-tuple-element.47) | copy-start | bytes 6291460
  130.9 10.1 %collective-permute-start.21 = (bf16[128,1024]{1,0:T(8,128)(2,1)S(1)}, bf16[128,1024]{1,0:T(8,128)(2,1)S(1)}, u32[]{:S(2)}, u32[]{:S(2)}) collective-permute-start(bf16[128,1024]{1,0:T(8,128)(2,1)S(1)} %get-tuple-element.88), channel_id=1, source_target_pairs={{0,3},{1,0},{2,1},{3,2},{4,7},{5,4},{6,5},{7,6},{8,11},{9,8},{10,9... | collective-permute-start | bytes 786440 | tf_op jit(solution)/shard_map/ppermute | solution.py:409
  134.3 10.7 %collective-permute-start.20 = (bf16[128,1024]{1,0:T(8,128)(2,1)S(1)}, bf16[128,1024]{1,0:T(8,128)(2,1)S(1)}, u32[]{:S(2)}, u32[]{:S(2)}) collective-permute-start(bf16[128,1024]{1,0:T(8,128)(2,1)S(1)} %slice.599), channel_id=1, source_target_pairs={{0,1},{1,2},{2,3},{3,0},{4,5},{5,6},{6,7},{7,4},{8,9},{9,10},{10,1... | collective-permute-start | bytes 786440 | tf_op jit(solution)/shard_map/ppermute | solution.py:415
  139.4 22.1 %copy-start.19 = (s32[2,128]{1,0:T(2,128)S(1)}, s32[2,128]{1,0:T(2,128)}, u32[]{:S(2)}) copy-start(s32[2,128]{1,0:T(2,128)} %param.32) | copy-start | bytes 3076
  139.5 25.3 %copy-start.2 = (f32[4096]{0:T(1024)S(1)}, f32[4096]{0:T(1024)}, u32[]{:S(2)}) copy-start(f32[4096]{0:T(1024)} %param.30) | copy-start | bytes 49156
  139.5 11.1 %collective-permute-start.18 = (bf16[128,1024]{1,0:T(8,128)(2,1)S(1)}, bf16[128,1024]{1,0:T(8,128)(2,1)S(1)}, u32[]{:S(2)}, u32[]{:S(2)}) collective-permute-start(bf16[128,1024]{1,0:T(8,128)(2,1)S(1)} %fusion.8), channel_id=1, source_target_pairs={{0,1},{1,2},{2,3},{3,0},{4,5},{5,6},{6,7},{7,4},{8,9},{9,10},{10,1... | collective-permute-start | bytes 786440 | tf_op jit(solution)/shard_map/ppermute | solution.py:417
  141.0 9.6 %collective-permute-start.22 = (bf16[128,1024]{1,0:T(8,128)(2,1)S(1)}, bf16[128,1024]{1,0:T(8,128)(2,1)S(1)}, u32[]{:S(2)}, u32[]{:S(2)}) collective-permute-start(bf16[128,1024]{1,0:T(8,128)(2,1)S(1)} %fusion.7), channel_id=1, source_target_pairs={{0,3},{1,0},{2,1},{3,2},{4,7},{5,4},{6,5},{7,6},{8,11},{9,8},{10,9... | collective-permute-start | bytes 786440 | tf_op jit(solution)/shard_map/ppermute | solution.py:420
  150.9 8.0 %collective-permute-start.23 = (bf16[128,1024]{1,0:T(8,128)(2,1)S(1)}, bf16[128,1024]{1,0:T(8,128)(2,1)S(1)}, u32[]{:S(2)}, u32[]{:S(2)}) collective-permute-start(bf16[128,1024]{1,0:T(8,128)(2,1)S(1)} %get-tuple-element.70.a), channel_id=1, source_target_pairs={{0,1},{1,2},{2,3},{3,0},{4,5},{5,6},{6,7},{7,4},{8,9},{9,10},{10,1... | collective-permute-start | bytes 786440 | tf_op jit(solution)/shard_map/ppermute | solution.py:427
  151.2 7.7 %collective-permute-start.25 = (bf16[128,1024]{1,0:T(8,128)(2,1)S(1)}, bf16[128,1024]{1,0:T(8,128)(2,1)S(1)}, u32[]{:S(2)}, u32[]{:S(2)}) collective-permute-start(bf16[128,1024]{1,0:T(8,128)(2,1)S(1)} %get-tuple-element.71.b), channel_id=1, source_target_pairs={{0,3},{1,0},{2,1},{3,2},{4,7},{5,4},{6,5},{7,6},{8,11},{9,8},{10,9... | collective-permute-start | bytes 786440 | tf_op jit(solution)/shard_map/ppermute | solution.py:428
  153.8 10.6 %collective-permute-start.27 = (bf16[128,1024]{1,0:T(8,128)(2,1)S(1)}, bf16[128,1024]{1,0:T(8,128)(2,1)S(1)}, u32[]{:S(2)}, u32[]{:S(2)}) collective-permute-start(bf16[128,1024]{1,0:T(8,128)(2,1)S(1)} %get-tuple-element.71.b), channel_id=1, source_target_pairs={{0,1},{1,2},{2,3},{3,0},{4,5},{5,6},{6,7},{7,4},{8,9},{9,10},{10,1... | collective-permute-start | bytes 786440 | tf_op jit(solution)/shard_map/ppermute | solution.py:429
  153.8 10.6 %collective-permute-start.28 = (bf16[128,1024]{1,0:T(8,128)(2,1)S(1)}, bf16[128,1024]{1,0:T(8,128)(2,1)S(1)}, u32[]{:S(2)}, u32[]{:S(2)}) collective-permute-start(bf16[128,1024]{1,0:T(8,128)(2,1)S(1)} %get-tuple-element.70.a), channel_id=1, source_target_pairs={{0,3},{1,0},{2,1},{3,2},{4,7},{5,4},{6,5},{7,6},{8,11},{9,8},{10,9... | collective-permute-start | bytes 786440 | tf_op jit(solution)/shard_map/ppermute | solution.py:430
  158.9 13.3 %collective-permute-start.24 = (bf16[128,1024]{1,0:T(8,128)(2,1)S(1)}, bf16[128,1024]{1,0:T(8,128)(2,1)S(1)}, u32[]{:S(2)}, u32[]{:S(2)}) collective-permute-start(bf16[128,1024]{1,0:T(8,128)(2,1)S(1)} %collective-permute-done.23.c), channel_id=1, source_target_pairs={{0,1},{1,2},{2,3},{3,0},{4,5},{5,6},{6,7},{7,4},{8,9},{9,10},{10,1... | collective-permute-start | bytes 786440 | tf_op jit(solution)/shard_map/ppermute | solution.py:431
  158.9 13.3 %collective-permute-start.26 = (bf16[128,1024]{1,0:T(8,128)(2,1)S(1)}, bf16[128,1024]{1,0:T(8,128)(2,1)S(1)}, u32[]{:S(2)}, u32[]{:S(2)}) collective-permute-start(bf16[128,1024]{1,0:T(8,128)(2,1)S(1)} %collective-permute-done.25.f), channel_id=1, source_target_pairs={{0,3},{1,0},{2,1},{3,2},{4,7},{5,4},{6,5},{7,6},{8,11},{9,8},{10,9... | collective-permute-start | bytes 786440 | tf_op jit(solution)/shard_map/ppermute | solution.py:432
  172.2 9.5 %copy-start.20 = (s32[2]{0:T(128)S(1)}, s32[2]{0:T(128)}, u32[]{:S(2)}) copy-start(s32[2]{0:T(128)} %lengths.1) | copy-start | bytes 28
  177.5 8.4 %all-to-all-start.1 = ((f32[4,3,256]{2,1,0:T(4,128)}), f32[4,3,256]{2,1,0:T(4,128)S(1)}, u32[]{:S(2)}, u32[]{:S(2)}) async-start(f32[4,3,256]{2,1,0:T(4,128)} %broadcast_in_dim.17), calls=%async_computation.1 | async-start | bytes 32768 | tf_op jit(solution)/shard_map/all_to_all | solution.py:488
  188.0 15.9 %all-to-all-start.2 = ((f32[32,1,128]{2,1,0:T(1,128)}), f32[32,1,128]{2,1,0:T(1,128)S(1)}, u32[]{:S(2)}, u32[]{:S(2)}) async-start(f32[32,1,128]{2,1,0:T(1,128)} %get-tuple-element.56), calls=%async_computation.2 | async-start | bytes 32768 | tf_op jit(solution)/shard_map/all_to_all | solution.py:502
  (7 other events, 7.2 us)
Sparse Core Ops, SparseCore 0:
  26.0 57.9 all-gather.2
  86.8 77.8 all-gather.4

commit v4 on v3

--- a/solution.py
+++ b/solution.py
@@ -159,8 +159,12 @@
                 squares[...] = part
 
 
-def near_kernel(order, a, b, c, d, e, f, gain, head, acc, squares):
-    add_blocks((a, b, c, d, e, f), order, gain, head, None, acc, squares)
+def own_kernel(order, upper, lower, gain, head, acc, squares):
+    add_blocks((upper, lower), order, gain, head, None, acc, squares)
+
+
+def near_kernel(order, a, b, c, d, gain, head, acc_in, squares_in, acc, squares):
+    add_blocks((a, b, c, d), order, gain, head, (acc_in, squares_in), acc, squares)
 
 
 def last_kernel(order, upper, lower, gain, head, acc_in, squares_in, ids, stats, acc, squares):
@@ -466,13 +470,14 @@
             name=name,
         )(blocks(per, *from_where), *pieces, gain, all_head, *extra)
 
+    acc = logits_call(own_kernel, "own_logits", share // 2, (0,), (upper, lower), ())
     acc = logits_call(
         near_kernel,
         "near_logits",
         share,
-        (0, 1, 3),
-        (upper, lower, behind_upper, behind_lower, ahead_upper, ahead_lower),
-        (),
+        (1, 3),
+        (behind_upper, behind_lower, ahead_upper, ahead_lower),
+        acc,
     )
     local_ids = targets.reshape(rows, 1) - zi * vocab_rows
     stats = logits_call(

time: 215 us -> 214 us (level)
  starting transfers between devices: 63.4 us -> 60 us
    ppermute x1, waiting for transfers between devices: 0.38 us -> 5 us  [body(): up_low = lax.ppermute(after[middle:].astype(BF), 'vocab', hops(1))]
    all_gather x1, waiting for transfers between devices: 0.32 us -> 3.65 us  [body(): all_head = lax.all_gather(head_t, DP, axis=0, tiled=True)]
    ppermute x1, waiting for transfers between devices: 3.1 us -> 0.01 us  [body(): up = lax.ppermute(far[:middle], 'vocab', hops(1))]
    ppermute x1, waiting for transfers between devices: 5.62 us -> 3.07 us  [body(): lax.ppermute((after[:middle] + up.astype(F32)).astype(BF), 'vocab', hops(1))]
    ppermute x1, waiting for transfers between devices: 0.01 us -> 2.54 us  [body(): lax.ppermute((prior[middle:] + down.astype(F32)).astype(BF), 'vocab', hop...]
    ppermute x1, waiting for transfers between devices: 2.52 us -> 0.01 us  [body(): behind_lower = lax.ppermute(lower, 'vocab', hops(1))]
    pallas_call x2 -> x3, Pallas kernels: 12.1 us -> 13.5 us  [logits_call(): pl.pallas_call(kernel, grid_spec=pltpu.PrefetchScalarGridSpec(num_scalar_...]
  transfers between devices with their start and end apart: 34 -> 34, of which waited for: 18 -> 16; matrix products, arithmetic and copies ran while one was open for 12% -> 12% of each run, Pallas kernels for 15% -> 16%
where the time goes in v4:
time: 214 us
  waiting for transfers between devices  63.2 us (30%)
  starting transfers between devices  60 us (28%)
  Pallas kernels  39.4 us (18%)
  between operations  17.4 us (8%)
  local copies, waits for them, and re-layouts  17.3 us (8%)
  matrix products  10.8 us (5%)
  other arithmetic  5.49 us (3%)
    pallas_call x3, Pallas kernels, logits_call(): pl.pallas_call(kernel, grid_spec=pltpu.PrefetchScalarGridSpec(num_scalar_...  13.5 us
    all_to_all x1, waiting for transfers between devices, body(): lax.all_to_all(jnp.broadcast_to(packed[None], (chips, *packed.shape)), CH...  11.7 us
    dot_general x6, matrix products, dot(): return jnp.dot(a, b, preferred_element_type=F32)  10.8 us
    ppermute x3, waiting for transfers between devices, body(): low_sum = low_sum + lax.ppermute(low_sent, 'vocab', ring(zs, s)).astype(F32)  8.12 us
    unnamed x45, local copies, waits for them, and re-layouts  7.08 us
    pallas_call x1, Pallas kernels, body(): pl.pallas_call(lambda *refs: outputs_kernel(rows, local_len, nstate, *ref...  7.02 us
    dynamic_slice x1, local copies, waits for them, and re-layouts, body(): lax.dynamic_slice_in_dim(out_w, lax.rem(zi + by, zs) * share, share, 1)  7 us
    ppermute x1, waiting for transfers between devices, body(): behind_second = lax.ppermute(second, DP, turns(1, 1))  7 us
  transfers between devices with their start and end apart: 34, of which 16 were waited for; matrix products, arithmetic and copies ran while one was open for 12% of the time, Pallas kernels for 16%

profile of v4, /device:TPU:1, one launch (start us, length us, event | category | flops | bytes accessed | tf_op | source)
XLA Modules:
  0.0 213.6 jit_solution(13882289558851558017)
XLA Ops:
  7.2 2.2 %collective-permute-start = (bf16[128,1024]{1,0:T(8,128)(2,1)}, bf16[128,1024]{1,0:T(8,128)(2,1)S(1)}, u32[]{:S(2)}, u32[]{:S(2)}) collective-permute-start(bf16[128,1024]{1,0:T(8,128)(2,1)} %param.19), channel_id=1, source_target_pairs={{0,8},{4,36},{8,16},{12,44},{16,24},{20,52},{24,0},{28,60},{32,40}... | collective-permute-start | bytes 786440 | tf_op jit(solution)/shard_map/ppermute | solution.py:257
  9.4 2.6 %collective-permute-start.1 = (bf16[128,1024]{1,0:T(8,128)(2,1)}, bf16[128,1024]{1,0:T(8,128)(2,1)S(1)}, u32[]{:S(2)}, u32[]{:S(2)}) collective-permute-start(bf16[128,1024]{1,0:T(8,128)(2,1)} %param.19), channel_id=1, source_target_pairs={{0,16},{4,68},{8,24},{12,76},{16,0},{20,84},{24,8},{28,92},{32,48}... | collective-permute-start | bytes 786440 | tf_op jit(solution)/shard_map/ppermute | solution.py:257
  12.0 1.1 collective-permute-start.2
  14.0 3.5 %collective-permute-start.3 = (bf16[2,3,4096]{2,1,0:T(4,128)(2,1)S(1)}, bf16[2,3,4096]{2,1,0:T(4,128)(2,1)S(1)}, u32[]{:S(2)}, u32[]{:S(2)}) collective-permute-start(bf16[2,3,4096]{2,1,0:T(4,128)(2,1)S(1)} %slice.260), channel_id=1, source_target_pairs={{0,4},{4,8},{8,12},{12,16},{16,20},{20,24},{24,28},{28,32},{32,36}... | collective-permute-start | bytes 147464 | tf_op jit(solution)/shard_map/ppermute | solution.py:256
  17.8 1.0 collective-permute-done.3
  19.6 4.3 %norm.1 = (bf16[256,4096]{1,0:T(8,128)(2,1)S(1)}, bf16[272,2048]{1,0:T(8,128)(2,1)S(1)}, bf16[272,2048]{1,0:T(8,128)(2,1)}) custom-call(s32[32]{0:T(128)S(1)} %stack.158.refs_0_, bf16[256,4096]{1,0:T(8,128)(2,1)} %bitcast.171, bf16[16,4096]{1,0:T(8,128)(2,1)S(1)} %pad.4.refs_2_, f32[1,4096]{1,0:T(1,128)S(1)} %bitcast.168), custom_call_target="tpu_custom_call" | custom-call | tf_op jit(solution)/shard_map/norm/pallas_call | solution.py:267
  25.0 1.3 copy-done.6
  26.6 2.5 %collective-permute-start.4 = (bf16[256,1024]{1,0:T(8,128)(2,1)S(1)}, bf16[256,1024]{1,0:T(8,128)(2,1)S(1)}, u32[]{:S(2)}, u32[]{:S(2)}) collective-permute-start(bf16[256,1024]{1,0:T(8,128)(2,1)S(1)} %pad_maximum_fusion.refs_0_), channel_id=1, source_target_pairs={{0,32},{4,12},{8,40},{12,20},{16,48},{20,28},{24,56},{28,4},{32,64... | collective-permute-start | bytes 1572872 | tf_op jit(solution)/shard_map/ppermute | solution.py:285
  29.0 1.1 collective-permute-start.7
  30.1 6.8 %collective-permute-done.4.refs_2_ = bf16[256,1024]{1,0:T(8,128)(2,1)S(1)} collective-permute-done((bf16[256,1024]{1,0:T(8,128)(2,1)S(1)}, bf16[256,1024]{1,0:T(8,128)(2,1)S(1)}, u32[]{:S(2)}, u32[]{:S(2)}) %collective-permute-start.4) | collective-permute-done | bytes 524320 | tf_op jit(solution)/shard_map/ppermute | solution.py:285
  37.4 2.3 %collective-permute-start.8 = (bf16[256,1024]{1,0:T(8,128)(2,1)S(1)}, bf16[256,1024]{1,0:T(8,128)(2,1)S(1)}, u32[]{:S(2)}, u32[]{:S(2)}) collective-permute-start(bf16[256,1024]{1,0:T(8,128)(2,1)S(1)} %collective-permute-done.7.refs_7_), channel_id=1, source_target_pairs={{0,96},{4,28},{8,104},{12,4},{16,112},{20,12},{24,120},{28,20},{32... | collective-permute-start | bytes 1572872 | tf_op jit(solution)/shard_map/ppermute | solution.py:290
  39.6 2.7 %collective-permute-start.9 = (bf16[256,1024]{1,0:T(8,128)(2,1)S(1)}, bf16[256,1024]{1,0:T(8,128)(2,1)}, u32[]{:S(2)}, u32[]{:S(2)}) collective-permute-start(bf16[256,1024]{1,0:T(8,128)(2,1)S(1)} %pad_maximum_fusion.refs_0_), channel_id=1, source_target_pairs={{0,96},{4,28},{8,104},{12,4},{16,112},{20,12},{24,120},{28,20},{32... | collective-permute-start | bytes 1572872 | tf_op jit(solution)/shard_map/ppermute | solution.py:288
  42.3 7.0 %constant_dynamic-slice_fusion.3 = (bf16[1024,1024]{1,0:T(8,128)(2,1)}, bf16[1024,1024]{1,0:T(8,128)(2,1)}, bf16[1024,1024]{1,0:T(8,128)(2,1)}, bf16[1024,1024]{1,0:T(8,128)(2,1)}) fusion(bf16[1024,4096]{1,0:T(8,128)(2,1)} %param.29, s32[]{:T(128)S(6)} %select_n.260, s32[]{:T(128)S(6)} %select_n.258, s32[]{:T(128)S(6)} %select_n.257, s32[]{:T(128)S(6)} %select_n.259), kind=kLoop, calls=%fused_computation.131 | loop fusion | bytes 16777232 | tf_op jit(solution)/shard_map/dynamic_slice | solution.py:293
  49.4 7.0 %collective-permute-done.5.refs_3_ = bf16[256,1024]{1,0:T(8,128)(2,1)} collective-permute-done((bf16[256,1024]{1,0:T(8,128)(2,1)S(1)}, bf16[256,1024]{1,0:T(8,128)(2,1)}, u32[]{:S(2)}, u32[]{:S(2)}) %collective-permute-start.5) | collective-permute-done | bytes 524320 | tf_op jit(solution)/shard_map/ppermute | solution.py:287
  56.4 3.7 %x_theirs.1 = bf16[272,1024]{1,0:T(8,128)(2,1)} custom-call(bf16[272,2048]{1,0:T(8,128)(2,1)} %collective-permute-done.10.lhs, bf16[256,1024]{1,0:T(8,128)(2,1)S(1)} %pad_maximum_fusion.refs_0_, bf16[256,1024]{1,0:T(8,128)(2,1)S(1)} %pad_maximum_fusion.1.refs_1_, bf16[256,1024]{1,0:T(8,128)(2,1)S(1)} %collective-permute-done.4.refs_2_, ...), custom_call_target="tpu_custom_call" | custom-call | tf_op jit(solution)/shard_map/x_theirs/pallas_call | solution.py:302
  60.0 4.0 %collective-permute-start.11 = (bf16[272,1024]{1,0:T(8,128)(2,1)}, bf16[272,1024]{1,0:T(8,128)(2,1)}, u32[]{:S(2)}, u32[]{:S(2)}) collective-permute-start(bf16[272,1024]{1,0:T(8,128)(2,1)} %x_theirs.1), channel_id=1, source_target_pairs={{0,4},{4,0},{1,5},{5,1},{2,6},{6,2},{3,7},{7,3},{8,12},{12,8},{9,1... | collective-permute-start | bytes 1671176 | tf_op jit(solution)/shard_map/ppermute | solution.py:39
  64.2 2.8 %x_mine.1 = f32[272,1024]{1,0:T(8,128)S(1)} custom-call(bf16[272,2048]{1,0:T(8,128)(2,1)} %copy-done, bf16[256,1024]{1,0:T(8,128)(2,1)S(1)} %pad_maximum_fusion.refs_0_, bf16[256,1024]{1,0:T(8,128)(2,1)S(1)} %pad_maximum_fusion.1.refs_1_, bf16[256,1024]{1,0:T(8,128)(2,1)S(1)} %collective-permute-done.4.refs_2_, ...), custom_call_target="tpu_custom_call" | custom-call | tf_op jit(solution)/shard_map/x_mine/pallas_call | solution.py:302
  67.1 1.2 add_convert_fusion
  70.1 1.5 collective-permute-start.12
  71.7 2.0 collective-permute-start.13
  73.7 1.3 collective-permute-start.14
  75.9 3.0 %collective-permute-done.12 = bf16[256,288]{1,0:T(8,128)(2,1)S(1)} collective-permute-done((bf16[256,288]{1,0:T(8,128)(2,1)S(1)}, bf16[256,288]{1,0:T(8,128)(2,1)S(1)}, u32[]{:S(2)}, u32[]{:S(2)}) %collective-permute-start.12) | collective-permute-done | bytes 147488 | tf_op jit(solution)/shard_map/ppermute | solution.py:326
  79.0 5.1 %collective-permute-done.14 = bf16[256,288]{1,0:T(8,128)(2,1)S(1)} collective-permute-done((bf16[256,288]{1,0:T(8,128)(2,1)S(1)}, bf16[256,288]{1,0:T(8,128)(2,1)S(1)}, u32[]{:S(2)}, u32[]{:S(2)}) %collective-permute-start.14) | collective-permute-done | bytes 147488 | tf_op jit(solution)/shard_map/ppermute | solution.py:326
  85.9 6.6 %steps.1 = (f32[256,8,128]{2,1,0:T(8,128)S(1)}, f32[256,8,128]{2,1,0:T(8,128)S(1)}, f32[2,16,8,128]{3,2,1,0:T(8,128)S(1)}, f32[2,8,128]{2,1,0:T(8,128)S(1)}) custom-call(f32[8192]{0:T(1024)S(1)} %reshape.106.refs_0_, f32[256,256]{1,0:T(8,128)S(1)} %slice.351.refs_1_, f32[1,256]{1,0:T(1,128)S(1)} %bitcast.170, bf16[256,1024]{1,0:T(8,128)(2,1)S(1)} %copy-done.1, ...), custom_call_target="tpu_custom_call" | custom-call | tf_op jit(solution)/shard_map/steps/pallas_call | solution.py:335
  95.0 4.9 %all-to-all-start = ((bf16[16,2,10,8,128]{4,3,2,1,0:T(8,128)(2,1)}), bf16[16,2,10,8,128]{4,3,2,1,0:T(8,128)(2,1)S(1)}, u32[]{:S(2)}, u32[]{:S(2)}) async-start(bf16[16,2,10,8,128]{4,3,2,1,0:T(8,128)(2,1)} %broadcast_in_dim.15), calls=%async_computation | async-start | bytes 1310720 | tf_op jit(solution)/shard_map/all_to_all | solution.py:379
  99.8 6.4 %convolution_convert_fusion.refs_5_ = bf16[256,1024]{1,0:T(8,128)(2,1)S(1)} fusion(bf16[256,4096]{1,0:T(8,128)(2,1)} %copy-done.6, bf16[4096,1024]{1,0:T(8,128)(2,1)} %all-gather.3.cloned.1.call-done), kind=kOutput, calls=%fused_computation.1 | convolution fusion | flops 2147745792 | bytes 11010048 | tf_op jit(solution)/shard_map/dot_general | solution.py:57
  106.3 11.7 %all-to-all-done = bf16[16,2,10,8,128]{4,3,2,1,0:T(8,128)(2,1)S(1)} async-done(((bf16[16,2,10,8,128]{4,3,2,1,0:T(8,128)(2,1)}), bf16[16,2,10,8,128]{4,3,2,1,0:T(8,128)(2,1)S(1)}, u32[]{:S(2)}, u32[]{:S(2)}) %all-to-all-start) | async-done | bytes 655392 | tf_op jit(solution)/shard_map/all_to_all | solution.py:379
  120.5 7.0 %outputs.1 = bf16[256,1024]{1,0:T(8,128)(2,1)S(1)} custom-call(f32[8192]{0:T(1024)S(1)} %reshape.106.refs_0_, f32[256,8,128]{2,1,0:T(8,128)S(1)} %get-tuple-element.40.refs_1_, f32[256,8,128]{2,1,0:T(8,128)S(1)} %get-tuple-element.41.refs_2_, f32[16,8,128]{2,1,0:T(8,128)S(1)} %bitcast.163, f32[2,16,8,128]{3,2,1,0:T(8,128)S(1)} %pad_maximum_fusion.3.refs_4_, ...), custom_call_target="tpu_custom_call" | custom-call | tf_op jit(solution)/shard_map/outputs/pallas_call | solution.py:397
  128.3 2.2 %collective-permute-start.21 = (bf16[128,1024]{1,0:T(8,128)(2,1)S(1)}, bf16[128,1024]{1,0:T(8,128)(2,1)S(1)}, u32[]{:S(2)}, u32[]{:S(2)}) collective-permute-start(bf16[128,1024]{1,0:T(8,128)(2,1)S(1)} %get-tuple-element.92), channel_id=1, source_target_pairs={{0,3},{1,0},{2,1},{3,2},{4,7},{5,4},{6,5},{7,6},{8,11},{9,8},{10,9... | collective-permute-start | bytes 786440 | tf_op jit(solution)/shard_map/ppermute | solution.py:413
  132.9 2.0 collective-permute-start.19
  134.9 1.8 convolution_add_fusion
  136.9 2.7 %collective-permute-start.22 = (bf16[128,1024]{1,0:T(8,128)(2,1)S(1)}, bf16[128,1024]{1,0:T(8,128)(2,1)S(1)}, u32[]{:S(2)}, u32[]{:S(2)}) collective-permute-start(bf16[128,1024]{1,0:T(8,128)(2,1)S(1)} %fusion.7), channel_id=1, source_target_pairs={{0,3},{1,0},{2,1},{3,2},{4,7},{5,4},{6,5},{7,6},{8,11},{9,8},{10,9... | collective-permute-start | bytes 786440 | tf_op jit(solution)/shard_map/ppermute | solution.py:424
  139.7 5.0 %collective-permute-done.20 = bf16[128,1024]{1,0:T(8,128)(2,1)S(1)} collective-permute-done((bf16[128,1024]{1,0:T(8,128)(2,1)S(1)}, bf16[128,1024]{1,0:T(8,128)(2,1)S(1)}, u32[]{:S(2)}, u32[]{:S(2)}) %collective-permute-start.20) | collective-permute-done | bytes 262176 | tf_op jit(solution)/shard_map/ppermute | solution.py:419
  144.7 2.5 %collective-permute-done.22 = bf16[128,1024]{1,0:T(8,128)(2,1)S(1)} collective-permute-done((bf16[128,1024]{1,0:T(8,128)(2,1)S(1)}, bf16[128,1024]{1,0:T(8,128)(2,1)S(1)}, u32[]{:S(2)}, u32[]{:S(2)}) %collective-permute-start.22) | collective-permute-done | bytes 262176 | tf_op jit(solution)/shard_map/ppermute | solution.py:424
  147.2 3.1 %collective-permute-done.18 = bf16[128,1024]{1,0:T(8,128)(2,1)S(1)} collective-permute-done((bf16[128,1024]{1,0:T(8,128)(2,1)S(1)}, bf16[128,1024]{1,0:T(8,128)(2,1)S(1)}, u32[]{:S(2)}, u32[]{:S(2)}) %collective-permute-start.18) | collective-permute-done | bytes 262176 | tf_op jit(solution)/shard_map/ppermute | solution.py:421
  150.9 2.7 %collective-permute-start.25 = (bf16[128,1024]{1,0:T(8,128)(2,1)S(1)}, bf16[128,1024]{1,0:T(8,128)(2,1)S(1)}, u32[]{:S(2)}, u32[]{:S(2)}) collective-permute-start(bf16[128,1024]{1,0:T(8,128)(2,1)S(1)} %get-tuple-element.75.lower), channel_id=1, source_target_pairs={{0,3},{1,0},{2,1},{3,2},{4,7},{5,4},{6,5},{7,6},{8,11},{9,8},{10,9... | collective-permute-start | bytes 786440 | tf_op jit(solution)/shard_map/ppermute | solution.py:432
  153.5 2.7 %collective-permute-start.28 = (bf16[128,1024]{1,0:T(8,128)(2,1)S(1)}, bf16[128,1024]{1,0:T(8,128)(2,1)S(1)}, u32[]{:S(2)}, u32[]{:S(2)}) collective-permute-start(bf16[128,1024]{1,0:T(8,128)(2,1)S(1)} %get-tuple-element.74.upper), channel_id=1, source_target_pairs={{0,3},{1,0},{2,1},{3,2},{4,7},{5,4},{6,5},{7,6},{8,11},{9,8},{10,9... | collective-permute-start | bytes 786440 | tf_op jit(solution)/shard_map/ppermute | solution.py:434
  156.2 2.4 %collective-permute-done.23.a = bf16[128,1024]{1,0:T(8,128)(2,1)S(1)} collective-permute-done((bf16[128,1024]{1,0:T(8,128)(2,1)S(1)}, bf16[128,1024]{1,0:T(8,128)(2,1)S(1)}, u32[]{:S(2)}, u32[]{:S(2)}) %collective-permute-start.23) | collective-permute-done | bytes 262176 | tf_op jit(solution)/shard_map/ppermute | solution.py:431
  158.6 2.7 %collective-permute-start.26 = (bf16[128,1024]{1,0:T(8,128)(2,1)S(1)}, bf16[128,1024]{1,0:T(8,128)(2,1)S(1)}, u32[]{:S(2)}, u32[]{:S(2)}) collective-permute-start(bf16[128,1024]{1,0:T(8,128)(2,1)S(1)} %collective-permute-done.25.d), channel_id=1, source_target_pairs={{0,3},{1,0},{2,1},{3,2},{4,7},{5,4},{6,5},{7,6},{8,11},{9,8},{10,9... | collective-permute-start | bytes 786440 | tf_op jit(solution)/shard_map/ppermute | solution.py:436
  161.6 3.7 %all-gather.5.cloned.1.call-done.head = bf16[4096,2048]{1,0:T(8,128)(2,1)} async-done(((bf16[128,2048]{1,0:T(8,128)(2,1)}), bf16[4096,2048]{1,0:T(8,128)(2,1)}) %all-gather.5.cloned.1.call-update) | async-done | bytes 16777232 | tf_op jit(solution)/shard_map/all_gather | solution.py:328
  165.3 3.6 %own_logits.1 = (f32[256,2048]{1,0:T(8,128)S(1)}, f32[256,128]{1,0:T(8,128)S(1)}) custom-call(s32[2]{0:T(128)S(1)} %pad_add_fusion.2.order, bf16[128,1024]{1,0:T(8,128)(2,1)S(1)} %get-tuple-element.74.upper, bf16[128,1024]{1,0:T(8,128)(2,1)S(1)} %get-tuple-element.75.lower, f32[1,4096]{1,0:T(1,128)S(1)} %bitcast.164, ...), custom_call_target="tpu_custom_call" | custom-call | tf_op jit(solution)/shard_map/own_logits/pallas_call | solution.py:459
  168.9 5.3 %near_logits.1 = (f32[256,2048]{1,0:T(8,128)S(1)}, f32[256,128]{1,0:T(8,128)S(1)}) custom-call(s32[2]{0:T(128)S(1)} %pad_add_fusion.1.order, bf16[128,1024]{1,0:T(8,128)(2,1)S(1)} %collective-permute-done.23.a, bf16[128,1024]{1,0:T(8,128)(2,1)S(1)} %collective-permute-done.27.b, bf16[128,1024]{1,0:T(8,128)(2,1)S(1)} %collective-permute-done.28.c, ...), custom_call_target="tpu_custom_call" | custom-call | tf_op jit(solution)/shard_map/near_logits/pallas_call | solution.py:459
  174.2 4.6 %last_logits.1 = f32[256,128]{1,0:T(8,128)S(1)} custom-call(s32[2]{0:T(128)S(1)} %pad_add_fusion.order, bf16[128,1024]{1,0:T(8,128)(2,1)S(1)} %collective-permute-done.24.upper, bf16[128,1024]{1,0:T(8,128)(2,1)S(1)} %collective-permute-done.26.lower, f32[1,4096]{1,0:T(1,128)S(1)} %bitcast.166, bf16[4096,2048]{1,0:T(8,128)(2,1)} %all-gather.5.cloned.1.call-done.head, ...), custom_call_target="tpu_custom_call" | custom-call | tf_op jit(solution)/shard_map/last_logits/pallas_call | solution.py:459
  179.6 4.1 %all-to-all-start.1 = ((f32[4,3,256]{2,1,0:T(4,128)}), f32[4,3,256]{2,1,0:T(4,128)S(1)}, u32[]{:S(2)}, u32[]{:S(2)}) async-start(f32[4,3,256]{2,1,0:T(4,128)} %broadcast_in_dim.17), calls=%async_computation.1 | async-start | bytes 32768 | tf_op jit(solution)/shard_map/all_to_all | solution.py:493
  184.3 3.6 %all-to-all-done.1.stats = f32[4,3,256]{2,1,0:T(4,128)S(1)} async-done(((f32[4,3,256]{2,1,0:T(4,128)}), f32[4,3,256]{2,1,0:T(4,128)S(1)}, u32[]{:S(2)}, u32[]{:S(2)}) %all-to-all-start.1) | async-done | bytes 12320 | tf_op jit(solution)/shard_map/all_to_all | solution.py:493
  188.5 1.4 finish.1
  189.9 6.8 %all-to-all-start.2 = ((f32[32,1,128]{2,1,0:T(1,128)}), f32[32,1,128]{2,1,0:T(1,128)S(1)}, u32[]{:S(2)}, u32[]{:S(2)}) async-start(f32[32,1,128]{2,1,0:T(1,128)} %get-tuple-element.60), calls=%async_computation.2 | async-start | bytes 32768 | tf_op jit(solution)/shard_map/all_to_all | solution.py:507
  197.6 6.1 %all-to-all-done.2 = f32[32,1,128]{2,1,0:T(1,128)S(1)} async-done(((f32[32,1,128]{2,1,0:T(1,128)}), f32[32,1,128]{2,1,0:T(1,128)S(1)}, u32[]{:S(2)}, u32[]{:S(2)}) %all-to-all-start.2) | async-done | bytes 16416 | tf_op jit(solution)/shard_map/all_to_all | solution.py:507
  (139 shorter events, 20.7 us)
Async XLA Ops:
  7.2 19.1 %copy-start.13 = (bf16[128,1024]{1,0:T(8,128)(2,1)S(1)}, bf16[128,1024]{1,0:T(8,128)(2,1)}, u32[]{:S(2)}) copy-start(bf16[128,1024]{1,0:T(8,128)(2,1)} %param.19) | copy-start | bytes 786436
  7.2 77.4 %all-gather.3.cloned.1.call-start = ((), (), s32[]{:S(2)}) async-start(), calls=%async_computation.3 | async-start | bytes 8650752 | tf_op jit(solution)/shard_map/all_gather | solution.py:284
  7.2 19.1 %collective-permute-start = (bf16[128,1024]{1,0:T(8,128)(2,1)}, bf16[128,1024]{1,0:T(8,128)(2,1)S(1)}, u32[]{:S(2)}, u32[]{:S(2)}) collective-permute-start(bf16[128,1024]{1,0:T(8,128)(2,1)} %param.19), channel_id=1, source_target_pairs={{0,8},{4,36},{8,16},{12,44},{16,24},{20,52},{24,0},{28,60},{32,40}... | collective-permute-start | bytes 786440 | tf_op jit(solution)/shard_map/ppermute | solution.py:257
  9.4 16.9 %collective-permute-start.1 = (bf16[128,1024]{1,0:T(8,128)(2,1)}, bf16[128,1024]{1,0:T(8,128)(2,1)S(1)}, u32[]{:S(2)}, u32[]{:S(2)}) collective-permute-start(bf16[128,1024]{1,0:T(8,128)(2,1)} %param.19), channel_id=1, source_target_pairs={{0,16},{4,68},{8,24},{12,76},{16,0},{20,84},{24,8},{28,92},{32,48}... | collective-permute-start | bytes 786440 | tf_op jit(solution)/shard_map/ppermute | solution.py:257
  12.0 14.3 %collective-permute-start.2 = (bf16[128,1024]{1,0:T(8,128)(2,1)}, bf16[128,1024]{1,0:T(8,128)(2,1)S(1)}, u32[]{:S(2)}, u32[]{:S(2)}) collective-permute-start(bf16[128,1024]{1,0:T(8,128)(2,1)} %param.19), channel_id=1, source_target_pairs={{0,24},{4,100},{8,0},{12,108},{16,8},{20,116},{24,16},{28,124},{32... | collective-permute-start | bytes 786440 | tf_op jit(solution)/shard_map/ppermute | solution.py:257
  14.0 4.8 %collective-permute-start.3 = (bf16[2,3,4096]{2,1,0:T(4,128)(2,1)S(1)}, bf16[2,3,4096]{2,1,0:T(4,128)(2,1)S(1)}, u32[]{:S(2)}, u32[]{:S(2)}) collective-permute-start(bf16[2,3,4096]{2,1,0:T(4,128)(2,1)S(1)} %slice.260), channel_id=1, source_target_pairs={{0,4},{4,8},{8,12},{12,16},{16,20},{20,24},{24,28},{28,32},{32,36}... | collective-permute-start | bytes 147464 | tf_op jit(solution)/shard_map/ppermute | solution.py:256
  26.4 138.8 %all-gather.5.cloned.1.call-start = ((), (), s32[]{:S(2)}) async-start(), calls=%async_computation.4 | async-start | bytes 17301504 | tf_op jit(solution)/shard_map/all_gather | solution.py:328
  26.5 29.9 %collective-permute-start.10 = (bf16[272,2048]{1,0:T(8,128)(2,1)}, bf16[272,2048]{1,0:T(8,128)(2,1)}, u32[]{:S(2)}, u32[]{:S(2)}) collective-permute-start(bf16[272,2048]{1,0:T(8,128)(2,1)} %get-tuple-element.39), channel_id=1, source_target_pairs={{0,4},{4,0},{1,5},{5,1},{2,6},{6,2},{3,7},{7,3},{8,12},{12,8},{9,1... | collective-permute-start | bytes 3342344 | tf_op jit(solution)/shard_map/ppermute | solution.py:39
  26.6 10.3 %collective-permute-start.4 = (bf16[256,1024]{1,0:T(8,128)(2,1)S(1)}, bf16[256,1024]{1,0:T(8,128)(2,1)S(1)}, u32[]{:S(2)}, u32[]{:S(2)}) collective-permute-start(bf16[256,1024]{1,0:T(8,128)(2,1)S(1)} %pad_maximum_fusion.refs_0_), channel_id=1, source_target_pairs={{0,32},{4,12},{8,40},{12,20},{16,48},{20,28},{24,56},{28,4},{32,64... | collective-permute-start | bytes 1572872 | tf_op jit(solution)/shard_map/ppermute | solution.py:285
  29.0 8.3 %collective-permute-start.7 = (bf16[256,1024]{1,0:T(8,128)(2,1)S(1)}, bf16[256,1024]{1,0:T(8,128)(2,1)S(1)}, u32[]{:S(2)}, u32[]{:S(2)}) collective-permute-start(bf16[256,1024]{1,0:T(8,128)(2,1)S(1)} %pad_maximum_fusion.1.refs_1_), channel_id=1, source_target_pairs={{0,96},{4,28},{8,104},{12,4},{16,112},{20,12},{24,120},{28,20},{32... | collective-permute-start | bytes 1572872 | tf_op jit(solution)/shard_map/ppermute | solution.py:286
  36.9 12.4 %collective-permute-start.6 = (bf16[256,1024]{1,0:T(8,128)(2,1)S(1)}, bf16[256,1024]{1,0:T(8,128)(2,1)S(1)}, u32[]{:S(2)}, u32[]{:S(2)}) collective-permute-start(bf16[256,1024]{1,0:T(8,128)(2,1)S(1)} %collective-permute-done.4.refs_2_), channel_id=1, source_target_pairs={{0,32},{4,12},{8,40},{12,20},{16,48},{20,28},{24,56},{28,4},{32,64... | collective-permute-start | bytes 1572872 | tf_op jit(solution)/shard_map/ppermute | solution.py:289
  37.4 12.0 %collective-permute-start.8 = (bf16[256,1024]{1,0:T(8,128)(2,1)S(1)}, bf16[256,1024]{1,0:T(8,128)(2,1)S(1)}, u32[]{:S(2)}, u32[]{:S(2)}) collective-permute-start(bf16[256,1024]{1,0:T(8,128)(2,1)S(1)} %collective-permute-done.7.refs_7_), channel_id=1, source_target_pairs={{0,96},{4,28},{8,104},{12,4},{16,112},{20,12},{24,120},{28,20},{32... | collective-permute-start | bytes 1572872 | tf_op jit(solution)/shard_map/ppermute | solution.py:290
  39.6 16.7 %collective-permute-start.5 = (bf16[256,1024]{1,0:T(8,128)(2,1)S(1)}, bf16[256,1024]{1,0:T(8,128)(2,1)}, u32[]{:S(2)}, u32[]{:S(2)}) collective-permute-start(bf16[256,1024]{1,0:T(8,128)(2,1)S(1)} %pad_maximum_fusion.1.refs_1_), channel_id=1, source_target_pairs={{0,32},{4,12},{8,40},{12,20},{16,48},{20,28},{24,56},{28,4},{32,64... | collective-permute-start | bytes 1572872 | tf_op jit(solution)/shard_map/ppermute | solution.py:287
  39.6 16.7 %collective-permute-start.9 = (bf16[256,1024]{1,0:T(8,128)(2,1)S(1)}, bf16[256,1024]{1,0:T(8,128)(2,1)}, u32[]{:S(2)}, u32[]{:S(2)}) collective-permute-start(bf16[256,1024]{1,0:T(8,128)(2,1)S(1)} %pad_maximum_fusion.refs_0_), channel_id=1, source_target_pairs={{0,96},{4,28},{8,104},{12,4},{16,112},{20,12},{24,120},{28,20},{32... | collective-permute-start | bytes 1572872 | tf_op jit(solution)/shard_map/ppermute | solution.py:288
  49.3 14.6 %copy-start.14 = (bf16[1024,32]{0,1:T(8,128)(2,1)S(1)}, bf16[1024,32]{0,1:T(8,128)(2,1)}, u32[]{:S(2)}) copy-start(bf16[1024,32]{0,1:T(8,128)(2,1)} %param.24) | copy-start | bytes 196612
  49.3 14.8 %copy-start.17 = (f32[4,1024]{1,0:T(4,128)S(1)}, f32[4,1024]{1,0:T(4,128)}, u32[]{:S(2)}) copy-start(f32[4,1024]{1,0:T(4,128)} %param.21) | copy-start | bytes 49156
  60.0 7.0 %collective-permute-start.11 = (bf16[272,1024]{1,0:T(8,128)(2,1)}, bf16[272,1024]{1,0:T(8,128)(2,1)}, u32[]{:S(2)}, u32[]{:S(2)}) collective-permute-start(bf16[272,1024]{1,0:T(8,128)(2,1)} %x_theirs.1), channel_id=1, source_target_pairs={{0,4},{4,0},{1,5},{5,1},{2,6},{6,2},{3,7},{7,3},{8,12},{12,8},{9,1... | collective-permute-start | bytes 1671176 | tf_op jit(solution)/shard_map/ppermute | solution.py:39
  69.2 5.7 %copy-start.11 = (bf16[2048,128]{1,0:T(8,128)(2,1)S(1)}, bf16[2048,128]{1,0:T(8,128)(2,1)}, u32[]{:S(2)}) copy-start(bf16[2048,128]{1,0:T(8,128)(2,1)} %param.31) | copy-start | bytes 1572868
  69.7 14.9 %copy-start.15 = (f32[1024,16]{0,1:T(8,128)S(1)}, f32[1024,16]{0,1:T(8,128)}, u32[]{:S(2)}) copy-start(f32[1024,16]{0,1:T(8,128)} %param.28) | copy-start | bytes 196612
  70.1 14.7 %copy-start.4 = (f32[1024]{0:T(1024)S(1)}, f32[1024]{0:T(1024)}, u32[]{:S(2)}) copy-start(f32[1024]{0:T(1024)} %param.27) | copy-start | bytes 12292
  70.1 14.7 %copy-start.5 = (f32[256]{0:T(256)S(1)}, f32[256]{0:T(256)}, u32[]{:S(2)}) copy-start(f32[256]{0:T(256)} %param.25) | copy-start | bytes 3076
  70.1 8.9 %collective-permute-start.12 = (bf16[256,288]{1,0:T(8,128)(2,1)S(1)}, bf16[256,288]{1,0:T(8,128)(2,1)S(1)}, u32[]{:S(2)}, u32[]{:S(2)}) collective-permute-start(bf16[256,288]{1,0:T(8,128)(2,1)S(1)} %convolution_convert_fusion.2), channel_id=1, source_target_pairs={{0,1},{1,2},{2,3},{3,0},{4,5},{5,6},{6,7},{7,4},{8,9},{9,10},{10,1... | collective-permute-start | bytes 442376 | tf_op jit(solution)/shard_map/ppermute | solution.py:326
  71.7 7.3 %collective-permute-start.13 = (bf16[256,288]{1,0:T(8,128)(2,1)S(1)}, bf16[256,288]{1,0:T(8,128)(2,1)S(1)}, u32[]{:S(2)}, u32[]{:S(2)}) collective-permute-start(bf16[256,288]{1,0:T(8,128)(2,1)S(1)} %convolution_convert_fusion.2), channel_id=1, source_target_pairs={{0,3},{1,0},{2,1},{3,2},{4,7},{5,4},{6,5},{7,6},{8,11},{9,8},{10,9... | collective-permute-start | bytes 442376 | tf_op jit(solution)/shard_map/ppermute | solution.py:326
  73.7 10.4 %collective-permute-start.14 = (bf16[256,288]{1,0:T(8,128)(2,1)S(1)}, bf16[256,288]{1,0:T(8,128)(2,1)S(1)}, u32[]{:S(2)}, u32[]{:S(2)}) collective-permute-start(bf16[256,288]{1,0:T(8,128)(2,1)S(1)} %convolution_convert_fusion.2), channel_id=1, source_target_pairs={{0,2},{1,3},{2,0},{3,1},{4,6},{5,7},{6,4},{7,5},{8,10},{9,11},{10,... | collective-permute-start | bytes 442376 | tf_op jit(solution)/shard_map/ppermute | solution.py:326
  92.5 1.4 collective-permute-start.15
  95.0 23.0 %all-to-all-start = ((bf16[16,2,10,8,128]{4,3,2,1,0:T(8,128)(2,1)}), bf16[16,2,10,8,128]{4,3,2,1,0:T(8,128)(2,1)S(1)}, u32[]{:S(2)}, u32[]{:S(2)}) async-start(bf16[16,2,10,8,128]{4,3,2,1,0:T(8,128)(2,1)} %broadcast_in_dim.15), calls=%async_computation | async-start | bytes 1310720 | tf_op jit(solution)/shard_map/all_to_all | solution.py:379
  118.5 1.9 collective-permute-start.16
  119.5 8.0 %copy-start.10 = (bf16[1024,1024]{1,0:T(8,128)(2,1)S(1)}, bf16[1024,1024]{1,0:T(8,128)(2,1)}, u32[]{:S(2)}) copy-start(bf16[1024,1024]{1,0:T(8,128)(2,1)} %get-tuple-element.48) | copy-start | bytes 6291460
  127.5 3.0 %copy-start.8 = (bf16[1024,1024]{1,0:T(8,128)(2,1)S(1)}, bf16[1024,1024]{1,0:T(8,128)(2,1)}, u32[]{:S(2)}) copy-start(bf16[1024,1024]{1,0:T(8,128)(2,1)} %get-tuple-element.51) | copy-start | bytes 6291460
  128.3 8.5 %collective-permute-start.21 = (bf16[128,1024]{1,0:T(8,128)(2,1)S(1)}, bf16[128,1024]{1,0:T(8,128)(2,1)S(1)}, u32[]{:S(2)}, u32[]{:S(2)}) collective-permute-start(bf16[128,1024]{1,0:T(8,128)(2,1)S(1)} %get-tuple-element.92), channel_id=1, source_target_pairs={{0,3},{1,0},{2,1},{3,2},{4,7},{5,4},{6,5},{7,6},{8,11},{9,8},{10,9... | collective-permute-start | bytes 786440 | tf_op jit(solution)/shard_map/ppermute | solution.py:413
  130.5 1.6 copy-start.7
  130.5 9.0 %collective-permute-start.17 = (bf16[128,1024]{1,0:T(8,128)(2,1)S(1)}, bf16[128,1024]{1,0:T(8,128)(2,1)S(1)}, u32[]{:S(2)}, u32[]{:S(2)}) collective-permute-start(bf16[128,1024]{1,0:T(8,128)(2,1)S(1)} %get-tuple-element.91), channel_id=1, source_target_pairs={{0,1},{1,2},{2,3},{3,0},{4,5},{5,6},{6,7},{7,4},{8,9},{9,10},{10,1... | collective-permute-start | bytes 786440 | tf_op jit(solution)/shard_map/ppermute | solution.py:412
  131.3 3.6 %copy-start.9 = (bf16[1024,1024]{1,0:T(8,128)(2,1)S(1)}, bf16[1024,1024]{1,0:T(8,128)(2,1)}, u32[]{:S(2)}) copy-start(bf16[1024,1024]{1,0:T(8,128)(2,1)} %get-tuple-element.49) | copy-start | bytes 6291460
  131.3 13.4 %collective-permute-start.20 = (bf16[128,1024]{1,0:T(8,128)(2,1)S(1)}, bf16[128,1024]{1,0:T(8,128)(2,1)S(1)}, u32[]{:S(2)}, u32[]{:S(2)}) collective-permute-start(bf16[128,1024]{1,0:T(8,128)(2,1)S(1)} %slice.599), channel_id=1, source_target_pairs={{0,1},{1,2},{2,3},{3,0},{4,5},{5,6},{6,7},{7,4},{8,9},{9,10},{10,1... | collective-permute-start | bytes 786440 | tf_op jit(solution)/shard_map/ppermute | solution.py:419
  132.9 11.8 %collective-permute-start.19 = (bf16[128,1024]{1,0:T(8,128)(2,1)S(1)}, bf16[128,1024]{1,0:T(8,128)(2,1)S(1)}, u32[]{:S(2)}, u32[]{:S(2)}) collective-permute-start(bf16[128,1024]{1,0:T(8,128)(2,1)S(1)} %slice.600), channel_id=1, source_target_pairs={{0,3},{1,0},{2,1},{3,2},{4,7},{5,4},{6,5},{7,6},{8,11},{9,8},{10,9... | collective-permute-start | bytes 786440 | tf_op jit(solution)/shard_map/ppermute | solution.py:420
  136.8 16.7 %copy-start.19 = (s32[2,128]{1,0:T(2,128)S(1)}, s32[2,128]{1,0:T(2,128)}, u32[]{:S(2)}) copy-start(s32[2,128]{1,0:T(2,128)} %param.32) | copy-start | bytes 3076
  136.8 28.4 %copy-start.2 = (f32[4096]{0:T(1024)S(1)}, f32[4096]{0:T(1024)}, u32[]{:S(2)}) copy-start(f32[4096]{0:T(1024)} %param.30) | copy-start | bytes 49156
  136.9 10.4 %collective-permute-start.22 = (bf16[128,1024]{1,0:T(8,128)(2,1)S(1)}, bf16[128,1024]{1,0:T(8,128)(2,1)S(1)}, u32[]{:S(2)}, u32[]{:S(2)}) collective-permute-start(bf16[128,1024]{1,0:T(8,128)(2,1)S(1)} %fusion.7), channel_id=1, source_target_pairs={{0,3},{1,0},{2,1},{3,2},{4,7},{5,4},{6,5},{7,6},{8,11},{9,8},{10,9... | collective-permute-start | bytes 786440 | tf_op jit(solution)/shard_map/ppermute | solution.py:424
  139.6 10.7 %collective-permute-start.18 = (bf16[128,1024]{1,0:T(8,128)(2,1)S(1)}, bf16[128,1024]{1,0:T(8,128)(2,1)S(1)}, u32[]{:S(2)}, u32[]{:S(2)}) collective-permute-start(bf16[128,1024]{1,0:T(8,128)(2,1)S(1)} %fusion.8), channel_id=1, source_target_pairs={{0,1},{1,2},{2,3},{3,0},{4,5},{5,6},{6,7},{7,4},{8,9},{9,10},{10,1... | collective-permute-start | bytes 786440 | tf_op jit(solution)/shard_map/ppermute | solution.py:421
  150.6 8.0 %collective-permute-start.23 = (bf16[128,1024]{1,0:T(8,128)(2,1)S(1)}, bf16[128,1024]{1,0:T(8,128)(2,1)S(1)}, u32[]{:S(2)}, u32[]{:S(2)}) collective-permute-start(bf16[128,1024]{1,0:T(8,128)(2,1)S(1)} %get-tuple-element.74.upper), channel_id=1, source_target_pairs={{0,1},{1,2},{2,3},{3,0},{4,5},{5,6},{6,7},{7,4},{8,9},{9,10},{10,1... | collective-permute-start | bytes 786440 | tf_op jit(solution)/shard_map/ppermute | solution.py:431
  150.9 7.7 %collective-permute-start.25 = (bf16[128,1024]{1,0:T(8,128)(2,1)S(1)}, bf16[128,1024]{1,0:T(8,128)(2,1)S(1)}, u32[]{:S(2)}, u32[]{:S(2)}) collective-permute-start(bf16[128,1024]{1,0:T(8,128)(2,1)S(1)} %get-tuple-element.75.lower), channel_id=1, source_target_pairs={{0,3},{1,0},{2,1},{3,2},{4,7},{5,4},{6,5},{7,6},{8,11},{9,8},{10,9... | collective-permute-start | bytes 786440 | tf_op jit(solution)/shard_map/ppermute | solution.py:432
  153.5 15.4 %collective-permute-start.27 = (bf16[128,1024]{1,0:T(8,128)(2,1)S(1)}, bf16[128,1024]{1,0:T(8,128)(2,1)S(1)}, u32[]{:S(2)}, u32[]{:S(2)}) collective-permute-start(bf16[128,1024]{1,0:T(8,128)(2,1)S(1)} %get-tuple-element.75.lower), channel_id=1, source_target_pairs={{0,1},{1,2},{2,3},{3,0},{4,5},{5,6},{6,7},{7,4},{8,9},{9,10},{10,1... | collective-permute-start | bytes 786440 | tf_op jit(solution)/shard_map/ppermute | solution.py:433
  153.5 15.4 %collective-permute-start.28 = (bf16[128,1024]{1,0:T(8,128)(2,1)S(1)}, bf16[128,1024]{1,0:T(8,128)(2,1)S(1)}, u32[]{:S(2)}, u32[]{:S(2)}) collective-permute-start(bf16[128,1024]{1,0:T(8,128)(2,1)S(1)} %get-tuple-element.74.upper), channel_id=1, source_target_pairs={{0,3},{1,0},{2,1},{3,2},{4,7},{5,4},{6,5},{7,6},{8,11},{9,8},{10,9... | collective-permute-start | bytes 786440 | tf_op jit(solution)/shard_map/ppermute | solution.py:434
  158.6 15.7 %collective-permute-start.24 = (bf16[128,1024]{1,0:T(8,128)(2,1)S(1)}, bf16[128,1024]{1,0:T(8,128)(2,1)S(1)}, u32[]{:S(2)}, u32[]{:S(2)}) collective-permute-start(bf16[128,1024]{1,0:T(8,128)(2,1)S(1)} %collective-permute-done.23.a), channel_id=1, source_target_pairs={{0,1},{1,2},{2,3},{3,0},{4,5},{5,6},{6,7},{7,4},{8,9},{9,10},{10,1... | collective-permute-start | bytes 786440 | tf_op jit(solution)/shard_map/ppermute | solution.py:435
  158.6 15.7 %collective-permute-start.26 = (bf16[128,1024]{1,0:T(8,128)(2,1)S(1)}, bf16[128,1024]{1,0:T(8,128)(2,1)S(1)}, u32[]{:S(2)}, u32[]{:S(2)}) collective-permute-start(bf16[128,1024]{1,0:T(8,128)(2,1)S(1)} %collective-permute-done.25.d), channel_id=1, source_target_pairs={{0,3},{1,0},{2,1},{3,2},{4,7},{5,4},{6,5},{7,6},{8,11},{9,8},{10,9... | collective-permute-start | bytes 786440 | tf_op jit(solution)/shard_map/ppermute | solution.py:436
  174.2 9.4 %copy-start.20 = (s32[2]{0:T(128)S(1)}, s32[2]{0:T(128)}, u32[]{:S(2)}) copy-start(s32[2]{0:T(128)} %lengths.1) | copy-start | bytes 28
  179.6 8.3 %all-to-all-start.1 = ((f32[4,3,256]{2,1,0:T(4,128)}), f32[4,3,256]{2,1,0:T(4,128)S(1)}, u32[]{:S(2)}, u32[]{:S(2)}) async-start(f32[4,3,256]{2,1,0:T(4,128)} %broadcast_in_dim.17), calls=%async_computation.1 | async-start | bytes 32768 | tf_op jit(solution)/shard_map/all_to_all | solution.py:493
  189.9 13.8 %all-to-all-start.2 = ((f32[32,1,128]{2,1,0:T(1,128)}), f32[32,1,128]{2,1,0:T(1,128)S(1)}, u32[]{:S(2)}, u32[]{:S(2)}) async-start(f32[32,1,128]{2,1,0:T(1,128)} %get-tuple-element.60), calls=%async_computation.2 | async-start | bytes 32768 | tf_op jit(solution)/shard_map/all_to_all | solution.py:507
  (7 other events, 7.3 us)
Sparse Core Ops, SparseCore 0:
  26.5 57.9 all-gather.2
  87.4 77.8 all-gather.4
